TPU v7x, 32 devices: a whole 2x2x4 slice. The times are simulated.
32 devices in a mesh: seq: 8 (over z, y), head: 4 (over x, core).
Axes of the slice: x: 2, y: 2, z: 4, core: 2. Of those that a mesh axis runs over, the one named last changes fastest.
Arguments:
- query_rows: bfloat16 [16384, 2048], P('seq', 'head'), may hold values from -6 to 6
- key_rows: bfloat16 [16384, 2048], P('seq', 'head'), may hold values from -6 to 6
- value_rows: bfloat16 [16384, 2048], P('seq', 'head'), may hold values from -6 to 6
- out_cotangent: bfloat16 [16384, 2048], P('seq', 'head'), may hold values from -6 to 6
- norm_gain: float32 [2048], P('head'), may hold values from 0.5 to 1.5
- decay_rate: float32 [16], P('head'), may hold values from 1.2207031e-05 to 0.0333333333
- document_lengths: int32 [32], replicated, may hold values from 1 to 8192, 16384 in all
- group_home: int32 [64], P('seq'), may hold values from 0 to 63, as said below
Outputs:
- query_grad: bfloat16 [16384, 2048], P('seq', 'head')
- key_grad: bfloat16 [16384, 2048], P('seq', 'head')
- value_grad: bfloat16 [16384, 2048], P('seq', 'head')
Inputs may be any that keep to these rules, and one draw needn't show every extreme that they name: document_lengths sum to 16384; the longest holds exactly half of them. group_home is a permutation of the 64 sequence groups; the groups stored on one device along seq hold exactly one group of each device's aligned block of sequence groups.
All inputs are finite; a program needn't handle non-finite values.
Results may differ from a plain program's by a relative error of at most 0.0095.
Values may be sent and summed in bfloat16 or wider, within the bound.
No kernel may reach another device: no remote copies, remote signals or barrier semaphores. Data moves between devices by JAX's collectives and lax.ppermute only.
A program may use at most 128 MiB of HBM per device.

v0:
```python
import jax
import jax.numpy as jnp
from jax import lax
from jax.sharding import PartitionSpec as P

HEAD_SIZE = 128
SPAN = 256


EPSILON = 1e-06


def from_behind(block, axis, distance):
    devices = range(lax.axis_size(axis))
    route = [(i - distance, i) for i in devices if i - distance in devices]
    return lax.ppermute(block, axis, route)


def segment_of(positions, doc_ends):
    return jnp.sum((doc_ends <= positions[..., None]).astype(jnp.int32), axis=-1)


def span_weights(seq_spans, doc_ends, decay_rates, span_width):
    offsets = jnp.arange(span_width, dtype=jnp.int32)
    positions = seq_spans[:, None] * span_width + offsets[None, :]
    segment = segment_of(positions, doc_ends)
    before = jnp.where(seq_spans == 0, -1, segment_of(seq_spans * span_width - 1, doc_ends))
    last_segment = segment[:, -1]
    step_float = offsets.astype(jnp.float32)
    query_side = (
        jnp.exp(-decay_rates[None, None, :] * (step_float[None, :, None] + 1.0))
        * (segment == before[:, None]).astype(jnp.float32)[:, :, None]
    )
    key_side = (
        jnp.exp(-decay_rates[None, None, :] * (span_width - 1.0 - step_float)[None, :, None])
        * (segment == last_segment[:, None]).astype(jnp.float32)[:, :, None]
    )
    carry_rate = (
        jnp.exp(-decay_rates * span_width)[None, :]
        * (before == last_segment).astype(jnp.float32)[:, None]
    )
    return (query_side, key_side, carry_rate, segment)


def span_masks(segment, decay_rates, span_width):
    step_float = jnp.arange(span_width, dtype=jnp.float32)
    spread = step_float[:, None] - step_float[None, :]
    same_doc = (segment[:, :, None] == segment[:, None, :]) & (spread >= 0.0)[None]
    return jnp.where(
        same_doc[:, None],
        jnp.exp(-decay_rates[None, :, None, None] * jnp.maximum(spread, 0.0)[None, None]),
        0.0,
    )


def relay_forward(factor, state):

    def relay_turn(turn_index, incoming):
        return from_behind(
            (factor[:, None, None] * incoming + state).astype(jnp.bfloat16), "seq", 1
        ).astype(jnp.float32)

    return lax.fori_loop(0, lax.axis_size("seq") - 1, relay_turn, jnp.zeros_like(state))


def relay_backward(factor, state):

    def relay_turn(turn_index, incoming):
        return from_behind(
            (factor[:, None, None] * incoming + state).astype(jnp.bfloat16), "seq", -1
        ).astype(jnp.float32)

    return lax.fori_loop(0, lax.axis_size("seq") - 1, relay_turn, jnp.zeros_like(state))


def forward_chain(carry_rate, summary):
    span_count = carry_rate.shape[0]
    running = jnp.zeros_like(summary[0])
    factor = jnp.ones_like(carry_rate[0])
    local_prev = []
    factors = []
    for span_index in range(span_count):
        local_prev.append(running)
        factors.append(factor)
        running = carry_rate[span_index][:, None, None] * running + summary[span_index]
        factor = factor * carry_rate[span_index]
    incoming = relay_forward(factor, running)
    return jnp.stack(local_prev) + jnp.stack(factors)[:, :, None, None] * incoming[None]


def reverse_chain(carry_rate, rev_summary):
    span_count = carry_rate.shape[0]
    running = jnp.zeros_like(rev_summary[0])
    factor = jnp.ones_like(carry_rate[0])
    after_local = [running] * span_count
    after_factor = [factor] * span_count
    for span_index in range(span_count - 1, -1, -1):
        after_local[span_index] = running
        after_factor[span_index] = factor
        running = rev_summary[span_index] + carry_rate[span_index][:, None, None] * running
        factor = factor * carry_rate[span_index]
    incoming = relay_backward(factor, running)
    return jnp.stack(after_local) + jnp.stack(after_factor)[:, :, None, None] * incoming[None]


def forward_local(query_c, key_c, value_c, decay_mask, key_side):
    scores = jnp.einsum("cjhd,clhd->chjl", query_c, key_c, preferred_element_type=jnp.float32)
    mixing = (scores * decay_mask).astype(jnp.bfloat16)
    weighted = (key_side[..., None] * value_c).astype(jnp.bfloat16)
    summary = jnp.einsum("cjhd,cjhe->chde", key_c, weighted, preferred_element_type=jnp.float32)
    return (mixing, summary)


def output_local(mixing, query_c, value_c, prev_states, query_side):
    inner = jnp.einsum("chjl,clhe->cjhe", mixing, value_c, preferred_element_type=jnp.float32)
    outer = jnp.einsum("cjhd,chde->cjhe", query_c, prev_states, preferred_element_type=jnp.float32)
    return inner + query_side[..., None] * outer


def cotangent_of(attn_out, upstream, norm_gain):
    flat_out = attn_out.reshape(-1, norm_gain.shape[0])
    upstream_f = upstream.reshape(-1, norm_gain.shape[0]).astype(jnp.float32)
    squares = jnp.sum(flat_out * flat_out, axis=1)
    crossed = jnp.sum(norm_gain * upstream_f * flat_out, axis=1)
    squares, crossed = lax.psum((squares, crossed), "head")
    hidden_total = norm_gain.shape[0] * lax.axis_size("head")
    scaling = 1.0 / jnp.sqrt(squares / hidden_total + EPSILON)
    pulled = crossed / hidden_total
    grad_in = (
        scaling[:, None] * norm_gain * upstream_f
        - (scaling**3)[:, None] * flat_out * pulled[:, None]
    )
    return grad_in.astype(jnp.bfloat16).reshape(attn_out.shape)


def query_summary(query_c, grad_in, query_side):
    weighted = (query_side[..., None] * grad_in).astype(jnp.bfloat16)
    return jnp.einsum("cjhd,cjhe->chde", query_c, weighted, preferred_element_type=jnp.float32)


def backward_local(
    query_c,
    key_c,
    value_c,
    grad_in,
    mixing,
    decay_mask,
    query_side,
    key_side,
    prev_states,
    after_states,
):
    pulled = jnp.einsum("cjhe,clhe->chjl", grad_in, value_c, preferred_element_type=jnp.float32)
    score_grad = (pulled * decay_mask).astype(jnp.bfloat16)
    query_grad = jnp.einsum(
        "chjl,clhd->cjhd", score_grad, key_c, preferred_element_type=jnp.float32
    )
    query_grad = query_grad + query_side[..., None] * jnp.einsum(
        "cjhe,chde->cjhd", grad_in, prev_states, preferred_element_type=jnp.float32
    )
    key_grad = jnp.einsum(
        "chjl,cjhd->clhd", score_grad, query_c, preferred_element_type=jnp.float32
    )
    key_grad = key_grad + key_side[..., None] * jnp.einsum(
        "clhe,chde->clhd", value_c, after_states, preferred_element_type=jnp.float32
    )
    value_grad = jnp.einsum("chjl,cjhe->clhe", mixing, grad_in, preferred_element_type=jnp.float32)
    value_grad = value_grad + key_side[..., None] * jnp.einsum(
        "clhd,chde->clhe", key_c, after_states, preferred_element_type=jnp.float32
    )
    return (
        query_grad.astype(jnp.bfloat16),
        key_grad.astype(jnp.bfloat16),
        value_grad.astype(jnp.bfloat16),
    )


def shards(
    query_rows,
    key_rows,
    value_rows,
    out_cotangent,
    norm_gain,
    decay_rate,
    document_lengths,
    group_home,
):
    devices = lax.axis_size("seq")
    position = lax.axis_index("seq")
    head_count = query_rows.shape[1] // HEAD_SIZE
    group_rows = query_rows.shape[0] // devices
    span_count = query_rows.shape[0] // SPAN
    doc_ends = jnp.cumsum(document_lengths)
    target = group_home // devices
    home_slot = group_home % devices
    device_ids = jnp.arange(devices, dtype=jnp.int32)
    chosen = target[None, :] == device_ids[:, None]
    picked = jnp.sum(jnp.where(chosen, device_ids[None, :], 0), axis=1)
    sending_slot = jnp.take(home_slot, picked)
    own_spans = position * span_count + jnp.arange(span_count, dtype=jnp.int32)
    group_shape = (devices, group_rows, head_count, HEAD_SIZE)
    span_shape = (span_count, SPAN, head_count, HEAD_SIZE)

    def outgoing(rows):
        return jnp.take(rows.reshape(group_shape), picked, axis=0)

    arrived = (
        lax.all_to_all(outgoing(query_rows), "seq", split_axis=0, concat_axis=0, tiled=True),
        lax.all_to_all(outgoing(key_rows), "seq", split_axis=0, concat_axis=0, tiled=True),
        lax.all_to_all(outgoing(value_rows), "seq", split_axis=0, concat_axis=0, tiled=True),
        lax.all_to_all(outgoing(out_cotangent), "seq", split_axis=0, concat_axis=0, tiled=True),
        lax.all_to_all(sending_slot, "seq", split_axis=0, concat_axis=0, tiled=True),
    )
    arrived_slot = arrived[4]
    matches = arrived_slot[None, :] == device_ids[:, None]
    source_pick = jnp.sum(jnp.where(matches, device_ids[None, :], 0), axis=1)

    def ordered(groups):
        return jnp.take(groups, source_pick, axis=0).reshape(span_shape)

    query_s = ordered(arrived[0])
    key_s = ordered(arrived[1])
    value_s = ordered(arrived[2])
    query_side, key_side, carry_rate, segment = span_weights(own_spans, doc_ends, decay_rate, SPAN)
    decay_mask = span_masks(segment, decay_rate, SPAN)
    mixing, summary = forward_local(query_s, key_s, value_s, decay_mask, key_side)
    upstream_s = ordered(arrived[3])
    prev_states = forward_chain(carry_rate, summary).astype(jnp.bfloat16)
    attn_out = output_local(mixing, query_s, value_s, prev_states, query_side)
    grad_in = cotangent_of(attn_out, upstream_s, norm_gain)
    rev_summary = query_summary(query_s, grad_in, query_side)
    after_states = reverse_chain(carry_rate, rev_summary).astype(jnp.bfloat16)
    query_grad, key_grad, value_grad = backward_local(
        query_s,
        key_s,
        value_s,
        grad_in,
        mixing,
        decay_mask,
        query_side,
        key_side,
        prev_states,
        after_states,
    )

    def homeward(values):
        return jnp.take(values.reshape(group_shape), arrived_slot, axis=0)

    returned = (
        lax.all_to_all(homeward(query_grad), "seq", split_axis=0, concat_axis=0, tiled=True),
        lax.all_to_all(homeward(key_grad), "seq", split_axis=0, concat_axis=0, tiled=True),
        lax.all_to_all(homeward(value_grad), "seq", split_axis=0, concat_axis=0, tiled=True),
    )
    flat_shape = query_rows.shape
    return tuple((jnp.take(piece, target, axis=0).reshape(flat_shape) for piece in returned))


def solution(mesh):
    in_specs = (
        P("seq", "head"),
        P("seq", "head"),
        P("seq", "head"),
        P("seq", "head"),
        P("head"),
        P("head"),
        P(),
        P("seq"),
    )
    out_specs = (P("seq", "head"), P("seq", "head"), P("seq", "head"))
    return jax.shard_map(shards, mesh=mesh, in_specs=in_specs, out_specs=out_specs, check_vma=False)
```

profile of v0, /device:TPU:0, one launch (start us, length us, event | category | flops | bytes accessed | tf_op | source)
XLA Modules:
  0.0 629.5 jit_solution(4399307830956344644)
XLA Ops:
  3.6 7.3 %all-to-all-start.1 = ((s32[8,1,1]{2,1,0:T(1,128)}), s32[8,1,1]{2,1,0:T(1,128)S(1)}, u32[]{:S(2)}, u32[]{:S(2)}) async-start(s32[8,1,1]{2,1,0:T(1,128)} %copy.216), calls=%async_computation.1 | async-start | bytes 8192 | tf_op jit(solution)/shard_map/all_to_all | solution.py:212
  22.3 3.7 gather_fusion.3
  26.0 4.0 reshape.534
  33.4 3.7 gather_fusion.5
  37.2 4.0 reshape.532
  44.6 3.7 gather_fusion.1
  48.3 6.5 %broadcast_select_fusion.10 = (bf16[8,256,4,128]{3,1,2,0:T(8,128)(2,1)}, bf16[8,256,4,128]{3,1,2,0:T(8,128)(2,1)}, bf16[8,256,4,128]{3,1,2,0:T(8,128)(2,1)}, bf16[8,256,4,128]{3,1,2,0:T(8,128)(2,1)}) fusion(bf16[8,256,4,128]{3,1,2,0:T(8,128)(2,1)S(1)} %gather_fusion.7, pred[8]{0:T(512)(128)(4,1)S(1)} %compare_and_fusion.4, ...), kind=kLoop, calls=%fused_computation.64 | loop fusion | flops 4194304 | bytes 16777224 | tf_op jit(solution)/shard_map/jit(_take)/select_n | solution.py:205
  54.8 53.9 %all_to_all.41 = bf16[8,256,4,128]{3,1,2,0:T(8,128)(2,1)S(1)} all-to-all(bf16[8,256,4,128]{3,1,2,0:T(8,128)(2,1)} %get-tuple-element.175), channel_id=1, replica_groups=mesh['seq'=8,'head'=4] {'seq'}, dimensions={0} | all-to-all | bytes 4194304 | tf_op jit(solution)/shard_map/all_to_all | solution.py:211
  108.7 51.3 %all_to_all.42 = bf16[8,256,4,128]{3,1,2,0:T(8,128)(2,1)} all-to-all(bf16[8,256,4,128]{3,1,2,0:T(8,128)(2,1)S(1)} %copy-done.15), channel_id=1, replica_groups=mesh['seq'=8,'head'=4] {'seq'}, dimensions={0} | all-to-all | bytes 4194304 | tf_op jit(solution)/shard_map/all_to_all | solution.py:209
  160.0 4.5 all-to-all-start.2
  165.7 46.1 %all-to-all-done.2 = bf16[8,256,4,128]{3,1,2,0:T(8,128)(2,1)} async-done(((bf16[8,256,4,128]{3,1,2,0:T(8,128)(2,1)}), bf16[8,256,4,128]{3,1,2,0:T(8,128)(2,1)}, u32[]{:S(2)}, u32[]{:S(2)}) %all-to-all-start.2) | async-done | bytes 2097184 | tf_op jit(solution)/shard_map/all_to_all | solution.py:210
  211.8 4.5 all-to-all-start.3
  221.8 3.9 copy.231
  225.7 3.7 gather_fusion.4
  232.3 4.5 gather_fusion.2
  236.8 4.1 fusion.17
  240.9 23.1 %all-to-all-done.3 = bf16[8,256,4,128]{3,1,2,0:T(8,128)(2,1)} async-done(((bf16[8,256,4,128]{3,1,2,0:T(8,128)(2,1)}), bf16[8,256,4,128]{3,1,2,0:T(8,128)(2,1)}, u32[]{:S(2)}, u32[]{:S(2)}) %all-to-all-start.3) | async-done | bytes 2097184 | tf_op jit(solution)/shard_map/all_to_all | solution.py:208
  264.0 3.7 gather_fusion.6
  267.8 4.0 fusion.4
  279.3 51.6 %while.22 = (s32[]{:T(128)}, f32[4,128,128]{2,1,0:T(8,128)S(1)}, f32[4]{0:T(128)S(1)}, f32[4,128,128]{2,1,0:T(8,128)S(1)}, s32[]{:T(128)}, /*index=5*/s32[]{:T(128)}) while((s32[]{:T(128)}, f32[4,128,128]{2,1,0:T(8,128)S(1)}, f32[4]{0:T(128)S(1)}, f32[4,128,128]{2,1,0:T(8,128)S(1)}, s32[]{:T(128)}, /*index=5*/s32[]{:T(128)}) %tuple.101), condition=%wide.region_6.8_spmd.clone, body=%wide.region_5.7_spmd.clone.sunk | while | flops 327683 | bytes 1572999 | solution.py:63
  285.3 4.4 collective-permute-start
  292.3 4.4 collective-permute-start
  299.3 4.4 collective-permute-start
  306.3 4.6 collective-permute-start
  314.1 5.6 collective-permute-start
  323.4 5.0 collective-permute-start
  330.9 7.3 %multiply_reduce_fusion = (f32[8,256]{1,0:T(8,128)S(1)}, f32[8,256]{1,0:T(8,128)S(1)}, f32[8,256,4,128]{1,3,2,0:T(8,128)}) fusion(bf16[8,256,4,128]{1,3,2,0:T(8,128)(2,1)S(1)} %copy-done.6, pred[8]{0:T(512)(128)(4,1)S(1)} %compare_and_fusion.3, f32[4,128]{1,0:T(4,128)S(1)} %bitcast.212, bf16[8,256,4,128]{3,1,2,0:T(8,128)(2,1)} %gather_fusion.6, ...), kind=kOutput, calls=%fused_computation.43 | convolution fusion | flops 280489984 | bytes 14993544 | tf_op jit(solution)/shard_map/cjhd,chde->cjhe/dot_general | solution.py:116
  338.3 10.4 %all-reduce = (f32[2048]{0:T(1024)S(1)}, f32[2048]{0:T(1024)S(1)}) all-reduce(f32[2048]{0:T(1024)S(1)} %bitcast.210, f32[2048]{0:T(1024)S(1)} %bitcast.211), channel_id=1, replica_groups=mesh['seq'=8,'head'=4] {'head'}, use_global_device_ids=true, to_apply=%region_10.12 | all-reduce | flops 4096 | bytes 32768 | tf_op jit(solution)/shard_map/psum | solution.py:125
  348.7 4.2 fusion.7
  362.3 3.8 fusion.49
  368.0 57.9 %while.23 = (s32[]{:T(128)}, f32[4,128,128]{2,1,0:T(8,128)S(1)}, f32[4]{0:T(128)S(1)}, f32[4,128,128]{2,1,0:T(8,128)S(1)}, s32[]{:T(128)}, /*index=5*/s32[]{:T(128)}) while((s32[]{:T(128)}, f32[4,128,128]{2,1,0:T(8,128)S(1)}, f32[4]{0:T(128)S(1)}, f32[4,128,128]{2,1,0:T(8,128)S(1)}, s32[]{:T(128)}, /*index=5*/s32[]{:T(128)}) %tuple.104), condition=%wide.region_12.14_spmd.clone, body=%wide.region_11.13_spmd.clone.sunk | while | flops 327683 | bytes 1572999 | solution.py:73
  369.4 7.0 %collective-permute-done.1 = bf16[4,128,128]{2,1,0:T(8,128)(2,1)S(1)} collective-permute-done((bf16[4,128,128]{2,1,0:T(8,128)(2,1)S(1)}, bf16[4,128,128]{2,1,0:T(8,128)(2,1)S(1)}, u32[]{:S(2)}, u32[]{:S(2)}) %collective-permute-start.1) | collective-permute-done | bytes 131104 | tf_op jit(solution)/shard_map/while/body/eval_jaxpr/ppermute | solution.py:16
  377.8 6.9 %collective-permute-done.1 = bf16[4,128,128]{2,1,0:T(8,128)(2,1)S(1)} collective-permute-done((bf16[4,128,128]{2,1,0:T(8,128)(2,1)S(1)}, bf16[4,128,128]{2,1,0:T(8,128)(2,1)S(1)}, u32[]{:S(2)}, u32[]{:S(2)}) %collective-permute-start.1) | collective-permute-done | bytes 131104 | tf_op jit(solution)/shard_map/while/body/eval_jaxpr/ppermute | solution.py:16
  386.1 6.5 %collective-permute-done.1 = bf16[4,128,128]{2,1,0:T(8,128)(2,1)S(1)} collective-permute-done((bf16[4,128,128]{2,1,0:T(8,128)(2,1)S(1)}, bf16[4,128,128]{2,1,0:T(8,128)(2,1)S(1)}, u32[]{:S(2)}, u32[]{:S(2)}) %collective-permute-start.1) | collective-permute-done | bytes 131104 | tf_op jit(solution)/shard_map/while/body/eval_jaxpr/ppermute | solution.py:16
  394.0 6.5 %collective-permute-done.1 = bf16[4,128,128]{2,1,0:T(8,128)(2,1)S(1)} collective-permute-done((bf16[4,128,128]{2,1,0:T(8,128)(2,1)S(1)}, bf16[4,128,128]{2,1,0:T(8,128)(2,1)S(1)}, u32[]{:S(2)}, u32[]{:S(2)}) %collective-permute-start.1) | collective-permute-done | bytes 131104 | tf_op jit(solution)/shard_map/while/body/eval_jaxpr/ppermute | solution.py:16
  401.9 6.5 %collective-permute-done.1 = bf16[4,128,128]{2,1,0:T(8,128)(2,1)S(1)} collective-permute-done((bf16[4,128,128]{2,1,0:T(8,128)(2,1)S(1)}, bf16[4,128,128]{2,1,0:T(8,128)(2,1)S(1)}, u32[]{:S(2)}, u32[]{:S(2)}) %collective-permute-start.1) | collective-permute-done | bytes 131104 | tf_op jit(solution)/shard_map/while/body/eval_jaxpr/ppermute | solution.py:16
  409.9 7.9 %collective-permute-done.1 = bf16[4,128,128]{2,1,0:T(8,128)(2,1)S(1)} collective-permute-done((bf16[4,128,128]{2,1,0:T(8,128)(2,1)S(1)}, bf16[4,128,128]{2,1,0:T(8,128)(2,1)S(1)}, u32[]{:S(2)}, u32[]{:S(2)}) %collective-permute-start.1) | collective-permute-done | bytes 131104 | tf_op jit(solution)/shard_map/while/body/eval_jaxpr/ppermute | solution.py:16
  419.2 6.6 %collective-permute-done.1 = bf16[4,128,128]{2,1,0:T(8,128)(2,1)S(1)} collective-permute-done((bf16[4,128,128]{2,1,0:T(8,128)(2,1)S(1)}, bf16[4,128,128]{2,1,0:T(8,128)(2,1)S(1)}, u32[]{:S(2)}, u32[]{:S(2)}) %collective-permute-start.1) | collective-permute-done | bytes 131104 | tf_op jit(solution)/shard_map/while/body/eval_jaxpr/ppermute | solution.py:16
  425.9 5.9 fusion.11
  441.9 4.9 fusion.15
  446.8 3.7 gather_fusion.9
  450.5 4.1 broadcast_select_fusion.3
  454.7 46.5 %all_to_all.43 = bf16[8,256,4,128]{1,3,2,0:T(8,128)(2,1)} all-to-all(bf16[8,256,4,128]{1,3,2,0:T(8,128)(2,1)S(1)} %get-tuple-element.172), channel_id=1, replica_groups=mesh['seq'=8,'head'=4] {'seq'}, dimensions={0} | all-to-all | bytes 4194304 | tf_op jit(solution)/shard_map/all_to_all | solution.py:252
  501.2 49.2 %all_to_all.44 = bf16[8,256,4,128]{1,3,2,0:T(8,128)(2,1)} all-to-all(bf16[8,256,4,128]{1,3,2,0:T(8,128)(2,1)S(1)} %get-tuple-element.173), channel_id=1, replica_groups=mesh['seq'=8,'head'=4] {'seq'}, dimensions={0} | all-to-all | bytes 4194304 | tf_op jit(solution)/shard_map/all_to_all | solution.py:251
  550.4 4.6 all-to-all-start.5
  560.9 40.5 %all-to-all-done.5 = bf16[8,256,4,128]{1,3,2,0:T(8,128)(2,1)} async-done(((bf16[8,256,4,128]{1,3,2,0:T(8,128)(2,1)}), bf16[8,256,4,128]{1,3,2,0:T(8,128)(2,1)}, u32[]{:S(2)}, u32[]{:S(2)}) %all-to-all-start.5) | async-done | bytes 2097184 | tf_op jit(solution)/shard_map/all_to_all | solution.py:250
  605.0 5.2 broadcast_select_fusion
  610.2 4.2 copy.267
  (194 shorter events, 116.9 us)
Async XLA Ops:
  3.6 51.1 %all-to-all-start.1 = ((s32[8,1,1]{2,1,0:T(1,128)}), s32[8,1,1]{2,1,0:T(1,128)S(1)}, u32[]{:S(2)}, u32[]{:S(2)}) async-start(s32[8,1,1]{2,1,0:T(1,128)} %copy.216), calls=%async_computation.1 | async-start | bytes 8192 | tf_op jit(solution)/shard_map/all_to_all | solution.py:212
  54.8 53.9 %copy-start.15 = (bf16[8,256,4,128]{3,1,2,0:T(8,128)(2,1)S(1)}, bf16[8,256,4,128]{3,1,2,0:T(8,128)(2,1)}, u32[]{:S(2)}) copy-start(bf16[8,256,4,128]{3,1,2,0:T(8,128)(2,1)} %get-tuple-element.178) | copy-start | bytes 6291460
  160.0 4.5 copy-start.22
  160.0 5.6 copy-start.23
  160.0 51.8 %all-to-all-start.2 = ((bf16[8,256,4,128]{3,1,2,0:T(8,128)(2,1)}), bf16[8,256,4,128]{3,1,2,0:T(8,128)(2,1)}, u32[]{:S(2)}, u32[]{:S(2)}) async-start(bf16[8,256,4,128]{3,1,2,0:T(8,128)(2,1)} %get-tuple-element.176), calls=%async_computation.2 | async-start | bytes 4194304 | tf_op jit(solution)/shard_map/all_to_all | solution.py:210
  211.8 52.2 %all-to-all-start.3 = ((bf16[8,256,4,128]{3,1,2,0:T(8,128)(2,1)}), bf16[8,256,4,128]{3,1,2,0:T(8,128)(2,1)}, u32[]{:S(2)}, u32[]{:S(2)}) async-start(bf16[8,256,4,128]{3,1,2,0:T(8,128)(2,1)} %get-tuple-element.177), calls=%async_computation.3 | async-start | bytes 4194304 | tf_op jit(solution)/shard_map/all_to_all | solution.py:208
  218.0 49.7 %copy-start.19 = (pred[8,256,256]{2,1,0:T(8,128)(4,1)}, pred[8,256,256]{2,1,0:T(8,128)(4,1)S(1)}, u32[]{:S(2)}) copy-start(pred[8,256,256]{2,1,0:T(8,128)(4,1)S(1)} %compare_and_fusion) | copy-start | bytes 1572868
  232.3 39.5 %copy-start.2 = (bf16[8,256,4,128]{1,3,2,0:T(8,128)(2,1)}, bf16[8,256,4,128]{1,3,2,0:T(8,128)(2,1)S(1)}, u32[]{:S(2)}) copy-start(bf16[8,256,4,128]{1,3,2,0:T(8,128)(2,1)S(1)} %copy.221) | copy-start | bytes 6291460
  271.8 4.1 copy-start
  271.8 4.1 copy-start.9
  271.8 5.1 copy-start.12
  277.6 53.3 %copy-start.6 = (bf16[8,256,4,128]{1,3,2,0:T(8,128)(2,1)S(1)}, bf16[8,256,4,128]{1,3,2,0:T(8,128)(2,1)}, u32[]{:S(2)}) copy-start(bf16[8,256,4,128]{1,3,2,0:T(8,128)(2,1)} %copy.231) | copy-start | bytes 6291460
  277.9 1.3 copy-start.13
  279.3 51.6 %copy-start.21 = (f32[512]{0:T(512)S(1)}, f32[512]{0:T(512)}, u32[]{:S(2)}) copy-start(f32[512]{0:T(512)} %param.18) | copy-start | bytes 6148
  279.4 5.8 collective-permute-start
  285.3 6.9 %collective-permute-start = (bf16[4,128,128]{2,1,0:T(8,128)(2,1)S(1)}, bf16[4,128,128]{2,1,0:T(8,128)(2,1)S(1)}, u32[]{:S(2)}, u32[]{:S(2)}) collective-permute-start(bf16[4,128,128]{2,1,0:T(8,128)(2,1)S(1)} %fusion.63), channel_id=1, source_target_pairs={{0,4},{4,8},{8,12},{12,16},{16,20},{20,24},{24,28},{1,5},{5,9},{9,... | collective-permute-start | bytes 393224 | tf_op jit(solution)/shard_map/while/body/eval_jaxpr/ppermute | solution.py:16
  292.3 6.9 %collective-permute-start = (bf16[4,128,128]{2,1,0:T(8,128)(2,1)S(1)}, bf16[4,128,128]{2,1,0:T(8,128)(2,1)S(1)}, u32[]{:S(2)}, u32[]{:S(2)}) collective-permute-start(bf16[4,128,128]{2,1,0:T(8,128)(2,1)S(1)} %fusion.63), channel_id=1, source_target_pairs={{0,4},{4,8},{8,12},{12,16},{16,20},{20,24},{24,28},{1,5},{5,9},{9,... | collective-permute-start | bytes 393224 | tf_op jit(solution)/shard_map/while/body/eval_jaxpr/ppermute | solution.py:16
  299.3 6.9 %collective-permute-start = (bf16[4,128,128]{2,1,0:T(8,128)(2,1)S(1)}, bf16[4,128,128]{2,1,0:T(8,128)(2,1)S(1)}, u32[]{:S(2)}, u32[]{:S(2)}) collective-permute-start(bf16[4,128,128]{2,1,0:T(8,128)(2,1)S(1)} %fusion.63), channel_id=1, source_target_pairs={{0,4},{4,8},{8,12},{12,16},{16,20},{20,24},{24,28},{1,5},{5,9},{9,... | collective-permute-start | bytes 393224 | tf_op jit(solution)/shard_map/while/body/eval_jaxpr/ppermute | solution.py:16
  306.3 7.6 %collective-permute-start = (bf16[4,128,128]{2,1,0:T(8,128)(2,1)S(1)}, bf16[4,128,128]{2,1,0:T(8,128)(2,1)S(1)}, u32[]{:S(2)}, u32[]{:S(2)}) collective-permute-start(bf16[4,128,128]{2,1,0:T(8,128)(2,1)S(1)} %fusion.63), channel_id=1, source_target_pairs={{0,4},{4,8},{8,12},{12,16},{16,20},{20,24},{24,28},{1,5},{5,9},{9,... | collective-permute-start | bytes 393224 | tf_op jit(solution)/shard_map/while/body/eval_jaxpr/ppermute | solution.py:16
  314.1 9.2 %collective-permute-start = (bf16[4,128,128]{2,1,0:T(8,128)(2,1)S(1)}, bf16[4,128,128]{2,1,0:T(8,128)(2,1)S(1)}, u32[]{:S(2)}, u32[]{:S(2)}) collective-permute-start(bf16[4,128,128]{2,1,0:T(8,128)(2,1)S(1)} %fusion.63), channel_id=1, source_target_pairs={{0,4},{4,8},{8,12},{12,16},{16,20},{20,24},{24,28},{1,5},{5,9},{9,... | collective-permute-start | bytes 393224 | tf_op jit(solution)/shard_map/while/body/eval_jaxpr/ppermute | solution.py:16
  323.4 7.5 %collective-permute-start = (bf16[4,128,128]{2,1,0:T(8,128)(2,1)S(1)}, bf16[4,128,128]{2,1,0:T(8,128)(2,1)S(1)}, u32[]{:S(2)}, u32[]{:S(2)}) collective-permute-start(bf16[4,128,128]{2,1,0:T(8,128)(2,1)S(1)} %fusion.63), channel_id=1, source_target_pairs={{0,4},{4,8},{8,12},{12,16},{16,20},{20,24},{24,28},{1,5},{5,9},{9,... | collective-permute-start | bytes 393224 | tf_op jit(solution)/shard_map/while/body/eval_jaxpr/ppermute | solution.py:16
  348.7 4.2 copy-start.1
  352.9 2.7 copy-start.7
  355.6 1.6 copy-start.3
  355.6 1.9 copy-start.18
  355.6 2.0 copy-start.20
  359.3 2.9 copy-start.5
  366.6 1.3 copy-start.10
  368.1 8.3 %collective-permute-start.1 = (bf16[4,128,128]{2,1,0:T(8,128)(2,1)S(1)}, bf16[4,128,128]{2,1,0:T(8,128)(2,1)S(1)}, u32[]{:S(2)}, u32[]{:S(2)}) collective-permute-start(bf16[4,128,128]{2,1,0:T(8,128)(2,1)S(1)} %fusion.64), channel_id=1, source_target_pairs={{4,0},{8,4},{12,8},{16,12},{20,16},{24,20},{28,24},{5,1},{9,5},{13... | collective-permute-start | bytes 393224 | tf_op jit(solution)/shard_map/while/body/eval_jaxpr/ppermute | solution.py:16
  376.5 8.2 %collective-permute-start.1 = (bf16[4,128,128]{2,1,0:T(8,128)(2,1)S(1)}, bf16[4,128,128]{2,1,0:T(8,128)(2,1)S(1)}, u32[]{:S(2)}, u32[]{:S(2)}) collective-permute-start(bf16[4,128,128]{2,1,0:T(8,128)(2,1)S(1)} %fusion.64), channel_id=1, source_target_pairs={{4,0},{8,4},{12,8},{16,12},{20,16},{24,20},{28,24},{5,1},{9,5},{13... | collective-permute-start | bytes 393224 | tf_op jit(solution)/shard_map/while/body/eval_jaxpr/ppermute | solution.py:16
  384.8 7.8 %collective-permute-start.1 = (bf16[4,128,128]{2,1,0:T(8,128)(2,1)S(1)}, bf16[4,128,128]{2,1,0:T(8,128)(2,1)S(1)}, u32[]{:S(2)}, u32[]{:S(2)}) collective-permute-start(bf16[4,128,128]{2,1,0:T(8,128)(2,1)S(1)} %fusion.64), channel_id=1, source_target_pairs={{4,0},{8,4},{12,8},{16,12},{20,16},{24,20},{28,24},{5,1},{9,5},{13... | collective-permute-start | bytes 393224 | tf_op jit(solution)/shard_map/while/body/eval_jaxpr/ppermute | solution.py:16
  392.7 7.8 %collective-permute-start.1 = (bf16[4,128,128]{2,1,0:T(8,128)(2,1)S(1)}, bf16[4,128,128]{2,1,0:T(8,128)(2,1)S(1)}, u32[]{:S(2)}, u32[]{:S(2)}) collective-permute-start(bf16[4,128,128]{2,1,0:T(8,128)(2,1)S(1)} %fusion.64), channel_id=1, source_target_pairs={{4,0},{8,4},{12,8},{16,12},{20,16},{24,20},{28,24},{5,1},{9,5},{13... | collective-permute-start | bytes 393224 | tf_op jit(solution)/shard_map/while/body/eval_jaxpr/ppermute | solution.py:16
  400.6 7.8 %collective-permute-start.1 = (bf16[4,128,128]{2,1,0:T(8,128)(2,1)S(1)}, bf16[4,128,128]{2,1,0:T(8,128)(2,1)S(1)}, u32[]{:S(2)}, u32[]{:S(2)}) collective-permute-start(bf16[4,128,128]{2,1,0:T(8,128)(2,1)S(1)} %fusion.64), channel_id=1, source_target_pairs={{4,0},{8,4},{12,8},{16,12},{20,16},{24,20},{28,24},{5,1},{9,5},{13... | collective-permute-start | bytes 393224 | tf_op jit(solution)/shard_map/while/body/eval_jaxpr/ppermute | solution.py:16
  408.6 9.2 %collective-permute-start.1 = (bf16[4,128,128]{2,1,0:T(8,128)(2,1)S(1)}, bf16[4,128,128]{2,1,0:T(8,128)(2,1)S(1)}, u32[]{:S(2)}, u32[]{:S(2)}) collective-permute-start(bf16[4,128,128]{2,1,0:T(8,128)(2,1)S(1)} %fusion.64), channel_id=1, source_target_pairs={{4,0},{8,4},{12,8},{16,12},{20,16},{24,20},{28,24},{5,1},{9,5},{13... | collective-permute-start | bytes 393224 | tf_op jit(solution)/shard_map/while/body/eval_jaxpr/ppermute | solution.py:16
  417.9 7.9 %collective-permute-start.1 = (bf16[4,128,128]{2,1,0:T(8,128)(2,1)S(1)}, bf16[4,128,128]{2,1,0:T(8,128)(2,1)S(1)}, u32[]{:S(2)}, u32[]{:S(2)}) collective-permute-start(bf16[4,128,128]{2,1,0:T(8,128)(2,1)S(1)} %fusion.64), channel_id=1, source_target_pairs={{4,0},{8,4},{12,8},{16,12},{20,16},{24,20},{28,24},{5,1},{9,5},{13... | collective-permute-start | bytes 393224 | tf_op jit(solution)/shard_map/while/body/eval_jaxpr/ppermute | solution.py:16
  425.9 6.0 copy-start.4
  425.9 6.0 copy-start.8
  425.9 6.4 %copy-start.11 = (f32[8,4,128,128]{3,2,1,0:T(8,128)S(1)}, f32[8,4,128,128]{3,2,1,0:T(8,128)}, u32[]{:S(2)}) copy-start(f32[8,4,128,128]{3,2,1,0:T(8,128)} %copy-done.10) | copy-start | bytes 6291460
  446.8 3.7 copy-start.14
  550.4 51.0 %all-to-all-start.5 = ((bf16[8,256,4,128]{1,3,2,0:T(8,128)(2,1)}), bf16[8,256,4,128]{1,3,2,0:T(8,128)(2,1)}, u32[]{:S(2)}, u32[]{:S(2)}) async-start(bf16[8,256,4,128]{1,3,2,0:T(8,128)(2,1)} %get-tuple-element.174), calls=%async_computation.5 | async-start | bytes 4194304 | tf_op jit(solution)/shard_map/all_to_all | solution.py:250
  614.4 3.4 copy-start.17
  620.3 3.4 copy-start.16
where the time goes:
time: 631 us; the launch traced here: 630 us
  blocking collectives  211 us (33%)
  waiting for transfers between devices  177 us (28%)
  local copies, waits for them, and re-layouts  106 us (17%)
  starting transfers between devices  61.5 us (10%)
  matrix products  44.4 us (7%)
  other arithmetic  28.3 us (4%)
    ppermute x14, waiting for transfers between devices, from_behind(): return lax.ppermute(block, axis, route)  66.9 us
    all_to_all x1, blocking collectives, shards(): lax.all_to_all(outgoing(out_cotangent), 'seq', split_axis=0, concat_axis=...  53.9 us
    all_to_all x1, blocking collectives, shards(): lax.all_to_all(outgoing(key_rows), 'seq', split_axis=0, concat_axis=0, ti...  51.3 us
    all_to_all x1, blocking collectives, shards(): lax.all_to_all(homeward(key_grad), 'seq', split_axis=0, concat_axis=0, ti...  49.2 us
    all_to_all x1, blocking collectives, shards(): lax.all_to_all(homeward(value_grad), 'seq', split_axis=0, concat_axis=0,...  46.5 us
    all_to_all x1, waiting for transfers between devices, shards(): lax.all_to_all(outgoing(value_rows), 'seq', split_axis=0, concat_axis=0,...  46.1 us
    ppermute x14, starting transfers between devices, from_behind(): return lax.ppermute(block, axis, route)  40.5 us
    all_to_all x1, waiting for transfers between devices, shards(): lax.all_to_all(homeward(query_grad), 'seq', split_axis=0, concat_axis=0,...  40.5 us
  transfers between devices with their start and end apart: 18, of which 17 were waited for; matrix products, arithmetic and copies ran while one was open for 12% of the time, Pallas kernels for 0%

commit v1 on v0

v1 whole, which is shorter than its diff:
```python
import functools

import jax
import jax.numpy as jnp
from jax import lax
from jax.experimental import pallas as pl
from jax.experimental.pallas import tpu as pltpu
from jax.sharding import PartitionSpec as P

HEAD_SIZE = 128
LANES = 128
EPSILON = 1e-06
TAIL = 16
F32 = jnp.float32
BF16 = jnp.bfloat16


def dot(a, b, ca, cb):
    return lax.dot_general(a, b, (((ca,), (cb,)), ((), ())), preferred_element_type=F32)


def head_cols(h):
    return slice(h * HEAD_SIZE, (h + 1) * HEAD_SIZE)


def token_index(span):
    return lax.broadcasted_iota(jnp.int32, (span, LANES), 0)


def key_table(rate, span):
    return jnp.exp(-rate * (span - 1.0 - token_index(span).astype(F32)))


def query_table(rate, span):
    return jnp.exp(-rate * (token_index(span).astype(F32) + 1.0))


def row_to_cols(row, width):
    cols = jnp.transpose(jnp.broadcast_to(row, (LANES, row.shape[1])))
    return jnp.concatenate([cols] * (width // LANES), axis=1) if width > LANES else cols


def cols_to_row(cols):
    return jnp.sum(jnp.transpose(cols), axis=0, keepdims=True)


def put_state(out_ref, step, h, rows, value):
    chunks = HEAD_SIZE // rows
    for part in range(chunks):
        out_ref[h * chunks + part, pl.ds(pl.multiple_of(step * rows, rows), rows), :] = value[
            part * rows : (part + 1) * rows
        ]


def get_state(ref, h, rows):
    chunks = HEAD_SIZE // rows
    return ref[h * chunks : (h + 1) * chunks, 0].reshape(HEAD_SIZE, HEAD_SIZE)


def summary_kernel(heads, rows, last_ref, home_ref, rate_ref, k_ref, v_ref, out_ref, table):
    step = pl.program_id(0)
    span = k_ref.shape[0]

    @pl.when(step == 0)
    def _():
        for h in range(heads):
            table[h] = key_table(rate_ref[h], span)
        tail = jnp.zeros((TAIL, LANES), F32)
        lane = lax.broadcasted_iota(jnp.int32, (TAIL, LANES), 1)
        for i in range(home_ref.shape[0]):
            tail = jnp.where(lane == i, home_ref[i].astype(F32), tail)
        for d in range(out_ref.shape[0]):
            out_ref[d, out_ref.shape[1] - TAIL :, :] = tail.astype(BF16)

    live = token_index(span) >= last_ref[step]
    for h in range(heads):
        side = jnp.where(live, table[h], 0.0)
        weighted = (side * v_ref[:, head_cols(h)].astype(F32)).astype(BF16)
        put_state(out_ref, step, h, rows, dot(k_ref[:, head_cols(h)], weighted, 0, 0).astype(BF16))


def scan_kernel(rows, spans, order_ref, cont_ref, rate_ref, in_ref, out_ref):
    slots = out_ref.shape[1] // rows
    factor = jnp.exp(jnp.full((8, LANES), rate_ref[0], F32))[0:1]

    def body(c, state):
        place = order_ref[c]
        device, slot = place // slots, place % slots
        at = pl.ds(pl.multiple_of(slot * rows, rows), rows)
        out_ref[device, at, :] = state.astype(BF16)
        carried = jnp.where(cont_ref[c] > 0, factor * state, 0.0)
        return carried + in_ref[device, at, :].astype(F32)

    lax.fori_loop(0, spans, body, jnp.zeros((rows, LANES), F32))


def fill_decay(decay, rate_ref, heads, span):
    j = lax.broadcasted_iota(jnp.int32, (span, span), 0)
    l = lax.broadcasted_iota(jnp.int32, (span, span), 1)
    spread = (j - l).astype(F32)
    for h in range(heads):
        decay[h] = jnp.where(
            spread >= 0.0, jnp.exp(-rate_ref[h] * jnp.maximum(spread, 0.0)), 0.0
        )


def local_kernel(heads, rate_ref, seg_ref, q_ref, k_ref, v_ref, out_ref, decay):
    span = q_ref.shape[0]

    @pl.when(pl.program_id(0) == 0)
    def _():
        fill_decay(decay, rate_ref, heads, span)

    seg = seg_ref[0]
    same = row_to_cols(seg, span) == seg
    for h in range(heads):
        cols = head_cols(h)
        scores = dot(q_ref[:, cols], k_ref[:, cols], 1, 1)
        mixing = (scores * jnp.where(same, decay[h], 0.0)).astype(BF16)
        out_ref[:, cols] = dot(mixing, v_ref[:, cols], 1, 0)


def output_kernel(
    heads, rows, first_ref, rate_ref, gain_ref, q_ref, u_ref, inner_ref, prev_ref, out_ref, sums_ref, table
):
    step = pl.program_id(0)
    span = q_ref.shape[0]

    @pl.when(step == 0)
    def _():
        for h in range(heads):
            table[h] = query_table(rate_ref[h], span)

    live = token_index(span) < first_ref[step]
    squares = jnp.zeros((span, LANES), F32)
    crossed = jnp.zeros((span, LANES), F32)
    for h in range(heads):
        cols = head_cols(h)
        outer = dot(q_ref[:, cols], get_state(prev_ref, h, rows), 1, 0)
        attn = inner_ref[:, cols] + jnp.where(live, table[h], 0.0) * outer
        out_ref[:, cols] = attn
        squares += attn * attn
        crossed += gain_ref[:, cols] * u_ref[:, cols].astype(F32) * attn
    sums_ref[0, 0:1, :] = cols_to_row(squares)
    sums_ref[0, 1:2, :] = cols_to_row(crossed)


def cotangent_kernel(
    heads, rows, channels, first_ref, rate_ref, gain_ref, sums_ref, q_ref, u_ref, attn_ref, g_ref, out_ref, table
):
    step = pl.program_id(0)
    span = q_ref.shape[0]

    @pl.when(step == 0)
    def _():
        for h in range(heads):
            table[h] = query_table(rate_ref[h], span)

    total = jnp.sum(sums_ref[:, 0], axis=0)
    scaling = 1.0 / jnp.sqrt(total[0:1] / channels + EPSILON)
    pulled = total[1:2] / channels
    first = row_to_cols(scaling, LANES)
    second = row_to_cols(scaling * scaling * scaling * pulled, LANES)
    live = token_index(span) < first_ref[step]
    for h in range(heads):
        cols = head_cols(h)
        grad = first * gain_ref[:, cols] * u_ref[:, cols].astype(F32) - second * attn_ref[:, cols]
        grad = grad.astype(BF16)
        g_ref[:, cols] = grad
        weighted = (jnp.where(live, table[h], 0.0) * grad.astype(F32)).astype(BF16)
        put_state(out_ref, step, h, rows, dot(q_ref[:, cols], weighted, 0, 0).astype(BF16))


def inner_grads_kernel(
    heads, rows, first_ref, rate_ref, seg_ref, q_ref, k_ref, v_ref, g_ref, prev_ref,
    dq_ref, dk_ref, dv_ref, decay, table,
):
    step = pl.program_id(0)
    span = q_ref.shape[0]

    @pl.when(step == 0)
    def _():
        fill_decay(decay, rate_ref, heads, span)
        for h in range(heads):
            table[h] = query_table(rate_ref[h], span)

    seg = seg_ref[0]
    same = row_to_cols(seg, span) == seg
    live = token_index(span) < first_ref[step]
    for h in range(heads):
        cols = head_cols(h)
        q, k, v, g = q_ref[:, cols], k_ref[:, cols], v_ref[:, cols], g_ref[:, cols]
        mask = jnp.where(same, decay[h], 0.0)
        mixing = (dot(q, k, 1, 1) * mask).astype(BF16)
        score_grad = (dot(g, v, 1, 1) * mask).astype(BF16)
        outer = dot(g, get_state(prev_ref, h, rows), 1, 1)
        dq = dot(score_grad, k, 1, 0) + jnp.where(live, table[h], 0.0) * outer
        dq_ref[:, cols] = dq.astype(BF16)
        dk_ref[:, cols] = dot(score_grad, q, 0, 0)
        dv_ref[:, cols] = dot(mixing, g, 0, 0)


def outer_grads_kernel(
    heads, rows, last_ref, rate_ref, k_ref, v_ref, after_ref, dk_in, dv_in, dk_ref, dv_ref, table
):
    step = pl.program_id(0)
    span = k_ref.shape[0]

    @pl.when(step == 0)
    def _():
        for h in range(heads):
            table[h] = key_table(rate_ref[h], span)

    live = token_index(span) >= last_ref[step]
    for h in range(heads):
        cols = head_cols(h)
        side = jnp.where(live, table[h], 0.0)
        after = get_state(after_ref, h, rows)
        dk = dk_in[:, cols] + side * dot(v_ref[:, cols], after, 1, 1)
        dv = dv_in[:, cols] + side * dot(k_ref[:, cols], after, 1, 0)
        dk_ref[:, cols] = dk.astype(BF16)
        dv_ref[:, cols] = dv.astype(BF16)


def exchange(blocks):
    return lax.all_to_all(blocks, "seq", split_axis=0, concat_axis=0, tiled=True)


def shards(query, key, value, upstream, norm_gain, decay_rate, document_lengths, group_home):
    devices = lax.axis_size("seq")
    position = lax.axis_index("seq")
    tokens, width = query.shape
    heads = width // HEAD_SIZE
    slots = group_home.shape[0]
    span = tokens // slots
    spans = slots * devices
    rows = width // devices
    channels = width * lax.axis_size("head")
    params = pltpu.CompilerParams(dimension_semantics=("arbitrary",), vmem_limit_bytes=32 << 20)

    doc_ends = jnp.cumsum(document_lengths)
    starts = group_home * span
    later = doc_ends[None, :] >= jnp.maximum(starts, 1)[:, None]
    first_end = jnp.min(jnp.where(later, doc_ends[None, :], tokens * devices), axis=1) - starts
    first_end = jnp.where(starts == 0, 0, first_end)
    earlier = doc_ends[None, :] < (starts + span)[:, None]
    last_start = jnp.max(jnp.where(earlier, doc_ends[None, :], 0), axis=1) - starts
    positions = starts[:, None, None] + jnp.arange(span, dtype=jnp.int32)[None, None, :]
    seg = jnp.sum((doc_ends <= positions[..., None]).astype(F32), axis=-1)
    all_starts = jnp.arange(spans, dtype=jnp.int32) * span
    crosses = (doc_ends[None, :] >= all_starts[:, None]) & (doc_ends[None, :] < (all_starts + span)[:, None])
    cont = jnp.logical_not(jnp.any(crosses, axis=1)).astype(jnp.int32)
    scan_rate = -span * jnp.sum(
        jnp.where(jnp.arange(heads) == (position * rows) // HEAD_SIZE, decay_rate, 0.0), keepdims=True
    )

    smem = pl.BlockSpec(memory_space=pltpu.SMEM)
    tok = pl.BlockSpec((span, width), lambda i: (i, 0))
    seg_spec = pl.BlockSpec((1, 1, span), lambda i: (i, 0, 0))
    gain_spec = pl.BlockSpec((1, width), lambda i: (0, 0))
    state_spec = pl.BlockSpec((devices, 1, rows, LANES), lambda i: (0, i, 0, 0))
    gain = norm_gain.reshape(1, width)

    def whole(shape):
        return pl.BlockSpec(shape, lambda i: (0,) * len(shape))

    def shaped(shape, dtype):
        return jax.ShapeDtypeStruct(shape, dtype)

    side_table = pltpu.VMEM((heads, span, LANES), F32)
    decay_table = pltpu.VMEM((heads, span, span), F32)
    packed = (devices, slots * rows + TAIL, LANES)
    plain = (devices, slots * rows, LANES)

    sent = pl.pallas_call(
        functools.partial(summary_kernel, heads, rows),
        grid=(slots,),
        in_specs=[smem, smem, smem, tok, tok],
        out_specs=whole(packed),
        out_shape=shaped(packed, BF16),
        scratch_shapes=[side_table],
        compiler_params=params,
        name="summaries",
    )(last_start, group_home, decay_rate, key, value)

    arrived = exchange(sent)

    inner = pl.pallas_call(
        functools.partial(local_kernel, heads),
        grid=(slots,),
        in_specs=[smem, seg_spec, tok, tok, tok],
        out_specs=tok,
        out_shape=shaped((tokens, width), F32),
        scratch_shapes=[decay_table],
        compiler_params=params,
        name="inner",
    )(decay_rate, seg, query, key, value)

    homes = arrived[:, slots * rows, :slots].astype(jnp.int32).reshape(-1)
    hits = homes[None, :] == jnp.arange(spans, dtype=jnp.int32)[:, None]
    order = jnp.sum(jnp.where(hits, jnp.arange(spans, dtype=jnp.int32)[None, :], 0), axis=1)

    def scan(blocks, order, cont):
        return pl.pallas_call(
            functools.partial(scan_kernel, rows, spans),
            grid=(1,),
            in_specs=[smem, smem, smem, whole(blocks.shape)],
            out_specs=whole(plain),
            out_shape=shaped(plain, BF16),
            compiler_params=params,
            name="scan",
        )(order, cont, scan_rate, blocks)

    prev = exchange(scan(arrived, order, cont)).reshape(devices, slots, rows, LANES)

    attn, sums = pl.pallas_call(
        functools.partial(output_kernel, heads, rows),
        grid=(slots,),
        in_specs=[smem, smem, gain_spec, tok, tok, tok, state_spec],
        out_specs=[tok, pl.BlockSpec((1, 2, span), lambda i: (i, 0, 0))],
        out_shape=[shaped((tokens, width), F32), shaped((slots, 2, span), F32)],
        scratch_shapes=[side_table],
        compiler_params=params,
        name="output",
    )(first_end, decay_rate, gain, query, upstream, inner, prev)

    sums = lax.all_gather(sums, "head")

    grad_in, rev_sent = pl.pallas_call(
        functools.partial(cotangent_kernel, heads, rows, channels),
        grid=(slots,),
        in_specs=[
            smem, smem, gain_spec,
            pl.BlockSpec((sums.shape[0], 1, 2, span), lambda i: (0, i, 0, 0)),
            tok, tok, tok,
        ],
        out_specs=[tok, whole(plain)],
        out_shape=[shaped((tokens, width), BF16), shaped(plain, BF16)],
        scratch_shapes=[side_table],
        compiler_params=params,
        name="cotangent",
    )(first_end, decay_rate, gain, sums, query, upstream, attn)

    rev_arrived = exchange(rev_sent)

    query_grad, key_inner, value_inner = pl.pallas_call(
        functools.partial(inner_grads_kernel, heads, rows),
        grid=(slots,),
        in_specs=[smem, smem, seg_spec, tok, tok, tok, tok, state_spec],
        out_specs=[tok, tok, tok],
        out_shape=[shaped((tokens, width), BF16), shaped((tokens, width), F32), shaped((tokens, width), F32)],
        scratch_shapes=[decay_table, side_table],
        compiler_params=params,
        name="inner_grads",
    )(first_end, decay_rate, seg, query, key, value, grad_in, prev)

    after = exchange(scan(rev_arrived, order[::-1], cont[::-1])).reshape(devices, slots, rows, LANES)

    key_grad, value_grad = pl.pallas_call(
        functools.partial(outer_grads_kernel, heads, rows),
        grid=(slots,),
        in_specs=[smem, smem, tok, tok, state_spec, tok, tok],
        out_specs=[tok, tok],
        out_shape=[shaped((tokens, width), BF16)] * 2,
        scratch_shapes=[side_table],
        compiler_params=params,
        name="outer_grads",
    )(last_start, decay_rate, key, value, after, key_inner, value_inner)
    return query_grad, key_grad, value_grad


def solution(mesh):
    in_specs = (
        P("seq", "head"),
        P("seq", "head"),
        P("seq", "head"),
        P("seq", "head"),
        P("head"),
        P("head"),
        P(),
        P("seq"),
    )
    out_specs = (P("seq", "head"), P("seq", "head"), P("seq", "head"))
    return jax.shard_map(shards, mesh=mesh, in_specs=in_specs, out_specs=out_specs, check_vma=False)
```

time: 631 us -> 177 us (0.28)
  blocking collectives: 211 us -> 5.24 us
  waiting for transfers between devices: 177 us -> 69.1 us
  local copies, waits for them, and re-layouts: 106 us -> 34.9 us
  matrix products: 44.4 us -> 0 us
  Pallas kernels: 0 us -> 43 us
  starting transfers between devices: 61.5 us -> 19.6 us
  other arithmetic: 28.3 us -> 2.73 us
    all_to_all x4 -> x0, blocking collectives: 201 us -> none  [the longest x1 53.9 us: shards(): lax.all_to_all(outgoing(out_cotangent), 'seq', split_axis=0, concat_axis=...]
    ppermute x14 -> x0, waiting for transfers between devices: 66.9 us -> none  [from_behind(): return lax.ppermute(block, axis, route)]
    gather x17 -> x0, local copies, waits for them, and re-layouts: 55.5 us -> none  [the longest x6 20.8 us: ordered(): return jnp.take(groups, source_pick, axis=0).reshape(span_shape)]
    dot_general x12 -> x0, matrix products: 44.4 us -> none  [the longest x1 7.34 us: output_local(): jnp.einsum('cjhd,chde->cjhe', query_c, prev_states, preferred_element_typ...]
    pallas_call x0 -> x8, Pallas kernels: none -> 43 us  [the longest x1 13.8 us: shards(): pl.pallas_call(functools.partial(inner_grads_kernel, heads, rows), grid=(...]
    all_to_all x4, waiting for transfers between devices: 110 us -> 69.1 us  [exchange(): lax.all_to_all(blocks, 'seq', split_axis=0, concat_axis=0, tiled=True)]
    ppermute x14 -> x0, starting transfers between devices: 40.5 us -> none  [from_behind(): return lax.ppermute(block, axis, route)]
    reshape x8 -> x0, local copies, waits for them, and re-layouts: 23.6 us -> none  [outgoing(): return jnp.take(rows.reshape(group_shape), picked, axis=0)]
  transfers between devices with their start and end apart: 18 -> 4, of which waited for: 17 -> 4; matrix products, arithmetic and copies ran while one was open for 12% -> 1% of each run, Pallas kernels for 0% -> 11%
where the time goes in v1:
time: 177 us; the launch traced here: 176 us
  waiting for transfers between devices  69.1 us (39%)
  Pallas kernels  43 us (24%)
  local copies, waits for them, and re-layouts  34.9 us (20%)
  starting transfers between devices  19.6 us (11%)
  blocking collectives  5.24 us (3%)
  other arithmetic  2.73 us (2%)
    all_to_all x4, waiting for transfers between devices, exchange(): lax.all_to_all(blocks, 'seq', split_axis=0, concat_axis=0, tiled=True)  69.1 us
    unnamed x52, local copies, waits for them, and re-layouts  33.9 us
    all_to_all x4, starting transfers between devices, exchange(): lax.all_to_all(blocks, 'seq', split_axis=0, concat_axis=0, tiled=True)  19.6 us
    pallas_call x1, Pallas kernels, shards(): pl.pallas_call(functools.partial(inner_grads_kernel, heads, rows), grid=(...  13.8 us
    pallas_call x1, Pallas kernels, shards(): pl.pallas_call(functools.partial(outer_grads_kernel, heads, rows), grid=(...  6.9 us
    pallas_call x1, Pallas kernels, shards(): pl.pallas_call(functools.partial(local_kernel, heads), grid=(slots,), in_...  6.18 us
    all_gather x1, blocking collectives, shards(): sums = lax.all_gather(sums, 'head')  5.24 us
    pallas_call x1, Pallas kernels, shards(): pl.pallas_call(functools.partial(cotangent_kernel, heads, rows, channels)...  4.46 us
  transfers between devices with their start and end apart: 4, of which 4 were waited for; matrix products, arithmetic and copies ran while one was open for 1% of the time, Pallas kernels for 11%

profile of v1, /device:TPU:0, one launch (start us, length us, event | category | flops | bytes accessed | tf_op | source)
XLA Modules:
  0.0 176.0 jit_solution(3180995202150205562)
XLA Ops:
  0.6 0.7 broadcast_maximum_fusion
  1.3 0.7 copy.14
  2.1 0.1 reduce.1
  2.2 0.2 select_reduce_fusion.1
  2.4 0.7 fusion.2
  3.1 1.6 copy-done.1
  4.7 1.6 copy-done.5
  6.3 0.7 copy-done.22
  6.9 0.7 copy-done.25
  7.6 3.9 %summaries.1 = bf16[8,528,128]{2,1,0:T(8,128)(2,1)} custom-call(s32[8]{0:T(128)S(1)} %get-tuple-element.23.last_ref, s32[8]{0:T(128)S(1)} %copy-done.25, f32[4]{0:T(128)S(1)} %copy-done.22, bf16[2048,512]{1,0:T(8,128)(2,1)S(1)} %copy-done.1, bf16[2048,512]{1,0:T(8,128)(2,1)S(1)} %copy-done.5), custom_call_target="tpu_custom_call" | custom-call | tf_op jit(solution)/shard_map/summaries/pallas_call | solution.py:275
  11.5 7.4 %all-to-all-start = ((bf16[8,528,128]{2,1,0:T(8,128)(2,1)}), bf16[8,528,128]{2,1,0:T(8,128)(2,1)S(1)}, u32[]{:S(2)}, u32[]{:S(2)}) async-start(bf16[8,528,128]{2,1,0:T(8,128)(2,1)} %summaries.1), calls=%async_computation | async-start | bytes 2162688 | tf_op jit(solution)/shard_map/all_to_all | solution.py:226
  19.0 0.6 fusion.1
  20.3 25.1 %all-to-all-done.in_ref = bf16[8,528,128]{2,1,0:T(8,128)(2,1)S(1)} async-done(((bf16[8,528,128]{2,1,0:T(8,128)(2,1)}), bf16[8,528,128]{2,1,0:T(8,128)(2,1)S(1)}, u32[]{:S(2)}, u32[]{:S(2)}) %all-to-all-start) | async-done | bytes 1081376 | tf_op jit(solution)/shard_map/all_to_all | solution.py:226
  45.5 0.1 select_reduce_fusion.order_ref
  45.7 1.7 scan.2
  47.4 1.0 copy-done.18
  48.3 3.6 %all-to-all-start.1 = ((bf16[8,512,128]{2,1,0:T(8,128)(2,1)}), bf16[8,512,128]{2,1,0:T(8,128)(2,1)S(1)}, u32[]{:S(2)}, u32[]{:S(2)}) async-start(bf16[8,512,128]{2,1,0:T(8,128)(2,1)} %copy-done.18), calls=%async_computation.1 | async-start | bytes 2097152 | tf_op jit(solution)/shard_map/all_to_all | solution.py:226
  52.0 0.1 convert_reduce_fusion
  52.2 1.6 copy-done.2
  53.8 1.6 copy-done.6
  55.4 6.2 %inner.1.inner_ref = f32[2048,512]{1,0:T(8,128)S(1)} custom-call(f32[4]{0:T(128)S(1)} %copy-done.23, f32[8,1,256]{2,1,0:T(1,128)S(1)} %reduce_sum.30.seg_ref, bf16[2048,512]{1,0:T(8,128)(2,1)S(1)} %copy-done, bf16[2048,512]{1,0:T(8,128)(2,1)S(1)} %copy-done.2, bf16[2048,512]{1,0:T(8,128)(2,1)S(1)} %copy-done.6), custom_call_target="tpu_custom_call" | custom-call | tf_op jit(solution)/shard_map/inner/pallas_call | solution.py:288
  61.5 1.9 %copy-done.9 = f32[2048,512]{1,0:T(8,128)} copy-done((f32[2048,512]{1,0:T(8,128)}, f32[2048,512]{1,0:T(8,128)S(1)}, u32[]{:S(2)}) %copy-start.9) | copy-done | bytes 4194328
  63.5 14.4 %all-to-all-done.1 = bf16[8,512,128]{2,1,0:T(8,128)(2,1)S(1)} async-done(((bf16[8,512,128]{2,1,0:T(8,128)(2,1)}), bf16[8,512,128]{2,1,0:T(8,128)(2,1)S(1)}, u32[]{:S(2)}, u32[]{:S(2)}) %all-to-all-start.1) | async-done | bytes 1048608 | tf_op jit(solution)/shard_map/all_to_all | solution.py:226
  77.9 2.2 %copy-done.10 = f32[2048,512]{1,0:T(8,128)S(1)} copy-done((f32[2048,512]{1,0:T(8,128)S(1)}, f32[2048,512]{1,0:T(8,128)}, u32[]{:S(2)}) %copy-start.10) | copy-done | bytes 4194328
  80.1 1.6 copy-done.11
  81.7 3.8 %output.1 = (f32[2048,512]{1,0:T(8,128)S(1)}, f32[8,2,256]{2,1,0:T(2,128)S(1)}) custom-call(s32[8]{0:T(128)S(1)} %get-tuple-element.24.first_ref, f32[4]{0:T(128)S(1)} %copy-done.23, f32[1,512]{1,0:T(1,128)S(1)} %bitcast.9, bf16[2048,512]{1,0:T(8,128)(2,1)S(1)} %copy-done, bf16[2048,512]{1,0:T(8,128)(2,1)S(1)} %copy-done.11, f32[2048,512]{1,0:T(8,128)S(1)} %copy-done.10, ...), custom_call_target="tpu_custom_call" | custom-call | tf_op jit(solution)/shard_map/output/pallas_call | solution.py:316
  85.5 5.2 %all-gather = f32[32,2,256]{2,1,0:T(2,128)S(1)} all-gather(f32[8,2,256]{2,1,0:T(2,128)S(1)} %get-tuple-element.12), channel_id=2, replica_groups=mesh['seq'=8,'head'=4] {'head'}, dimensions={0}, use_global_device_ids=true | all-gather | bytes 81920 | tf_op jit(solution)/shard_map/all_gather | solution.py:327
  90.8 4.5 %cotangent.1 = (bf16[2048,512]{1,0:T(8,128)(2,1)S(1)}, bf16[8,512,128]{2,1,0:T(8,128)(2,1)S(1)}) custom-call(s32[8]{0:T(128)S(1)} %get-tuple-element.24.first_ref, f32[4]{0:T(128)S(1)} %copy-done.23, f32[1,512]{1,0:T(1,128)S(1)} %bitcast.10, f32[4,8,2,256]{3,2,1,0:T(2,128)S(1)} %bitcast.8, bf16[2048,512]{1,0:T(8,128)(2,1)S(1)} %copy-done, ...), custom_call_target="tpu_custom_call" | custom-call | tf_op jit(solution)/shard_map/cotangent/pallas_call | solution.py:329
  95.2 1.3 copy-done.19
  96.5 1.0 copy-done.21
  97.5 4.3 %all-to-all-start.2 = ((bf16[8,512,128]{2,1,0:T(8,128)(2,1)}), bf16[8,512,128]{2,1,0:T(8,128)(2,1)}, u32[]{:S(2)}, u32[]{:S(2)}) async-start(bf16[8,512,128]{2,1,0:T(8,128)(2,1)} %copy-done.21), calls=%async_computation.2 | async-start | bytes 2097152 | tf_op jit(solution)/shard_map/all_to_all | solution.py:226
  101.8 0.1 rev.7.cont_ref
  102.0 26.4 %all-to-all-done.2.in_ref = bf16[8,512,128]{2,1,0:T(8,128)(2,1)} async-done(((bf16[8,512,128]{2,1,0:T(8,128)(2,1)}), bf16[8,512,128]{2,1,0:T(8,128)(2,1)}, u32[]{:S(2)}, u32[]{:S(2)}) %all-to-all-start.2) | async-done | bytes 1048608 | tf_op jit(solution)/shard_map/all_to_all | solution.py:226
  128.3 2.2 %scan.3 = bf16[8,512,128]{2,1,0:T(8,128)(2,1)S(1)} custom-call(s32[64]{0:T(128)S(1)} %rev.6.order_ref, s32[64]{0:T(128)S(1)} %rev.7.cont_ref, f32[1]{0:T(128)} %bitcast.2.rate_ref, bf16[8,512,128]{2,1,0:T(8,128)(2,1)} %all-to-all-done.2.in_ref), custom_call_target="tpu_custom_call" | custom-call | tf_op jit(solution)/shard_map/scan/pallas_call | solution.py:304
  130.6 1.0 copy-done.17
  131.6 4.2 %all-to-all-start.3 = ((bf16[8,512,128]{2,1,0:T(8,128)(2,1)}), bf16[8,512,128]{2,1,0:T(8,128)(2,1)}, u32[]{:S(2)}, u32[]{:S(2)}) async-start(bf16[8,512,128]{2,1,0:T(8,128)(2,1)} %copy-done.17), calls=%async_computation.3 | async-start | bytes 2097152 | tf_op jit(solution)/shard_map/all_to_all | solution.py:226
  135.8 1.6 copy-done.3
  137.4 1.6 copy-done.7
  139.0 1.6 copy-done.20
  140.6 13.8 %inner_grads.1 = (bf16[2048,512]{1,0:T(8,128)(2,1)}, f32[2048,512]{1,0:T(8,128)S(1)}, f32[2048,512]{1,0:T(8,128)S(1)}) custom-call(s32[8]{0:T(128)S(1)} %get-tuple-element.24.first_ref, f32[4]{0:T(128)S(1)} %copy-done.23, f32[8,1,256]{2,1,0:T(1,128)S(1)} %reduce_sum.30.seg_ref, bf16[2048,512]{1,0:T(8,128)(2,1)S(1)} %copy-done, ...), custom_call_target="tpu_custom_call" | custom-call | tf_op jit(solution)/shard_map/inner_grads/pallas_call | solution.py:346
  154.4 2.0 %copy-done.13 = f32[2048,512]{1,0:T(8,128)} copy-done((f32[2048,512]{1,0:T(8,128)}, f32[2048,512]{1,0:T(8,128)S(1)}, u32[]{:S(2)}) %copy-start.13) | copy-done | bytes 4194328
  156.4 2.0 %copy-done.15 = f32[2048,512]{1,0:T(8,128)} copy-done((f32[2048,512]{1,0:T(8,128)}, f32[2048,512]{1,0:T(8,128)S(1)}, u32[]{:S(2)}) %copy-start.15) | copy-done | bytes 4194328
  158.3 3.2 %all-to-all-done.3 = bf16[8,512,128]{2,1,0:T(8,128)(2,1)} async-done(((bf16[8,512,128]{2,1,0:T(8,128)(2,1)}), bf16[8,512,128]{2,1,0:T(8,128)(2,1)}, u32[]{:S(2)}, u32[]{:S(2)}) %all-to-all-start.3) | async-done | bytes 1048608 | tf_op jit(solution)/shard_map/all_to_all | solution.py:226
  161.5 1.6 copy-done.4
  163.1 1.6 copy-done.8
  164.7 2.2 %copy-done.14 = f32[2048,512]{1,0:T(8,128)S(1)} copy-done((f32[2048,512]{1,0:T(8,128)S(1)}, f32[2048,512]{1,0:T(8,128)}, u32[]{:S(2)}) %copy-start.14) | copy-done | bytes 4194328
  166.9 2.2 %copy-done.16 = f32[2048,512]{1,0:T(8,128)S(1)} copy-done((f32[2048,512]{1,0:T(8,128)S(1)}, f32[2048,512]{1,0:T(8,128)}, u32[]{:S(2)}) %copy-start.16) | copy-done | bytes 4194328
  169.1 6.9 %outer_grads.1 = (bf16[2048,512]{1,0:T(8,128)(2,1)}, bf16[2048,512]{1,0:T(8,128)(2,1)}) custom-call(s32[8]{0:T(128)S(1)} %get-tuple-element.23.last_ref, f32[4]{0:T(128)S(1)} %copy-done.23, bf16[2048,512]{1,0:T(8,128)(2,1)S(1)} %copy-done.4, bf16[2048,512]{1,0:T(8,128)(2,1)S(1)} %copy-done.8, bf16[8,8,64,128]{3,2,1,0:T(8,128)(2,1)} %bitcast.5.after_ref, ...), custom_call_target="tpu_custom_call" | custom-call | tf_op jit(solution)/shard_map/outer_grads/pallas_call | solution.py:359
  (39 shorter events, 0.5 us)
Async XLA Ops:
  3.1 1.6 copy-start.1
  4.7 1.6 copy-start.5
  6.3 0.7 copy-start.22
  6.9 0.7 copy-start.25
  11.5 7.4 %copy-start.23 = (f32[4]{0:T(128)S(1)}, f32[4]{0:T(128)}, u32[]{:S(2)}) copy-start(f32[4]{0:T(128)} %rate_ref.11) | copy-start | bytes 52
  11.5 33.9 %all-to-all-start = ((bf16[8,528,128]{2,1,0:T(8,128)(2,1)}), bf16[8,528,128]{2,1,0:T(8,128)(2,1)S(1)}, u32[]{:S(2)}, u32[]{:S(2)}) async-start(bf16[8,528,128]{2,1,0:T(8,128)(2,1)} %summaries.1), calls=%async_computation | async-start | bytes 2162688 | tf_op jit(solution)/shard_map/all_to_all | solution.py:226
  45.7 6.5 %copy-start = (bf16[2048,512]{1,0:T(8,128)(2,1)S(1)}, bf16[2048,512]{1,0:T(8,128)(2,1)}, u32[]{:S(2)}) copy-start(bf16[2048,512]{1,0:T(8,128)(2,1)} %q_ref.7) | copy-start | bytes 6291460
  47.3 1.0 copy-start.18
  48.3 29.6 %all-to-all-start.1 = ((bf16[8,512,128]{2,1,0:T(8,128)(2,1)}), bf16[8,512,128]{2,1,0:T(8,128)(2,1)S(1)}, u32[]{:S(2)}, u32[]{:S(2)}) async-start(bf16[8,512,128]{2,1,0:T(8,128)(2,1)} %copy-done.18), calls=%async_computation.1 | async-start | bytes 2097152 | tf_op jit(solution)/shard_map/all_to_all | solution.py:226
  52.2 1.6 copy-start.2
  53.8 1.6 copy-start.6
  55.3 22.6 %copy-start.24 = (f32[512]{0:T(512)S(1)}, f32[512]{0:T(512)}, u32[]{:S(2)}) copy-start(f32[512]{0:T(512)} %param.12) | copy-start | bytes 6148
  61.5 2.0 %copy-start.9 = (f32[2048,512]{1,0:T(8,128)}, f32[2048,512]{1,0:T(8,128)S(1)}, u32[]{:S(2)}) copy-start(f32[2048,512]{1,0:T(8,128)S(1)} %inner.1.inner_ref) | copy-start | bytes 12582916
  77.9 2.2 %copy-start.10 = (f32[2048,512]{1,0:T(8,128)S(1)}, f32[2048,512]{1,0:T(8,128)}, u32[]{:S(2)}) copy-start(f32[2048,512]{1,0:T(8,128)} %copy-done.9) | copy-start | bytes 12582916
  80.1 1.6 copy-start.11
  81.7 9.1 %copy-start.12 = (bf16[2048,512]{1,0:T(8,128)(2,1)S(1)}, bf16[2048,512]{1,0:T(8,128)(2,1)}, u32[]{:S(2)}) copy-start(bf16[2048,512]{1,0:T(8,128)(2,1)} %u_ref.3) | copy-start | bytes 6291460
  95.2 1.3 copy-start.19
  96.5 1.0 copy-start.21
  97.5 30.8 %all-to-all-start.2 = ((bf16[8,512,128]{2,1,0:T(8,128)(2,1)}), bf16[8,512,128]{2,1,0:T(8,128)(2,1)}, u32[]{:S(2)}, u32[]{:S(2)}) async-start(bf16[8,512,128]{2,1,0:T(8,128)(2,1)} %copy-done.21), calls=%async_computation.2 | async-start | bytes 2097152 | tf_op jit(solution)/shard_map/all_to_all | solution.py:226
  130.6 1.0 copy-start.17
  131.6 30.0 %all-to-all-start.3 = ((bf16[8,512,128]{2,1,0:T(8,128)(2,1)}), bf16[8,512,128]{2,1,0:T(8,128)(2,1)}, u32[]{:S(2)}, u32[]{:S(2)}) async-start(bf16[8,512,128]{2,1,0:T(8,128)(2,1)} %copy-done.17), calls=%async_computation.3 | async-start | bytes 2097152 | tf_op jit(solution)/shard_map/all_to_all | solution.py:226
  135.8 1.6 copy-start.3
  137.4 1.6 copy-start.7
  139.0 1.6 copy-start.20
  154.4 2.0 %copy-start.13 = (f32[2048,512]{1,0:T(8,128)}, f32[2048,512]{1,0:T(8,128)S(1)}, u32[]{:S(2)}) copy-start(f32[2048,512]{1,0:T(8,128)S(1)} %get-tuple-element.17.dk_in) | copy-start | bytes 12582916
  156.4 2.0 %copy-start.15 = (f32[2048,512]{1,0:T(8,128)}, f32[2048,512]{1,0:T(8,128)S(1)}, u32[]{:S(2)}) copy-start(f32[2048,512]{1,0:T(8,128)S(1)} %get-tuple-element.18.dv_in) | copy-start | bytes 12582916
  161.5 1.6 copy-start.4
  163.1 1.6 copy-start.8
  164.7 2.2 %copy-start.14 = (f32[2048,512]{1,0:T(8,128)S(1)}, f32[2048,512]{1,0:T(8,128)}, u32[]{:S(2)}) copy-start(f32[2048,512]{1,0:T(8,128)} %copy-done.13) | copy-start | bytes 12582916
  166.9 2.2 %copy-start.16 = (f32[2048,512]{1,0:T(8,128)S(1)}, f32[2048,512]{1,0:T(8,128)}, u32[]{:S(2)}) copy-start(f32[2048,512]{1,0:T(8,128)} %copy-done.15) | copy-start | bytes 12582916

commit v2 on v1

v2 whole, which is shorter than its diff:
```python
import functools

import jax
import jax.numpy as jnp
from jax import lax
from jax.experimental import pallas as pl
from jax.experimental.pallas import tpu as pltpu
from jax.sharding import PartitionSpec as P

HEAD_SIZE = 128
LANES = 128
EPSILON = 1e-06
TAIL = 16
F32 = jnp.float32
BF16 = jnp.bfloat16


def dot(a, b, ca, cb):
    return lax.dot_general(a, b, (((ca,), (cb,)), ((), ())), preferred_element_type=F32)


def head_cols(h):
    return slice(h * HEAD_SIZE, (h + 1) * HEAD_SIZE)


def token_index(span):
    return lax.broadcasted_iota(jnp.int32, (span, LANES), 0)


def key_table(rate, span):
    return jnp.exp(-rate * (span - 1.0 - token_index(span).astype(F32)))


def query_table(rate, span):
    return jnp.exp(-rate * (token_index(span).astype(F32) + 1.0))


def row_to_cols(row, width):
    cols = jnp.transpose(jnp.broadcast_to(row, (LANES, row.shape[1])))
    return jnp.concatenate([cols] * (width // LANES), axis=1) if width > LANES else cols


def cols_to_row(cols):
    return jnp.sum(jnp.transpose(cols), axis=0, keepdims=True)


def doc_bounds(len_ref, start, span):
    end = jnp.int32(0)
    first = jnp.int32(0)
    last = jnp.int32(0)
    for d in range(len_ref.shape[0]):
        before = end
        end = end + len_ref[d]
        first = jnp.where((before < start) & (end >= start), end, first)
        last = jnp.where(end < start + span, end, last)
    return first - start, last - start


def segment_row(len_ref, start, span):
    position = start + lax.broadcasted_iota(jnp.int32, (1, span), 1)
    end = jnp.int32(0)
    segment = jnp.zeros((1, span), F32)
    for d in range(len_ref.shape[0]):
        end = end + len_ref[d]
        segment += jnp.where(end <= position, 1.0, 0.0)
    return segment


def put_state(out_ref, step, h, rows, value):
    chunks = HEAD_SIZE // rows
    for part in range(chunks):
        out_ref[h * chunks + part, pl.ds(pl.multiple_of(step * rows, rows), rows), :] = value[
            part * rows : (part + 1) * rows
        ]


def get_state(ref, h, rows):
    chunks = HEAD_SIZE // rows
    return ref[h * chunks : (h + 1) * chunks, 0].reshape(HEAD_SIZE, HEAD_SIZE)


def summary_kernel(heads, rows, len_ref, home_ref, rate_ref, k_ref, v_ref, out_ref, table):
    step = pl.program_id(0)
    span = k_ref.shape[0]

    @pl.when(step == 0)
    def _():
        for h in range(heads):
            table[h] = key_table(rate_ref[h], span)
        tail = jnp.zeros((TAIL, LANES), F32)
        lane = lax.broadcasted_iota(jnp.int32, (TAIL, LANES), 1)
        for i in range(home_ref.shape[0]):
            tail = jnp.where(lane == i, home_ref[i].astype(F32), tail)
        for d in range(out_ref.shape[0]):
            out_ref[d, out_ref.shape[1] - TAIL :, :] = tail.astype(BF16)

    _, last = doc_bounds(len_ref, home_ref[step] * span, span)
    live = token_index(span) >= last
    for h in range(heads):
        side = jnp.where(live, table[h], 0.0)
        weighted = (side * v_ref[:, head_cols(h)].astype(F32)).astype(BF16)
        put_state(out_ref, step, h, rows, dot(k_ref[:, head_cols(h)], weighted, 0, 0).astype(BF16))


def scan_kernel(rows, spans, span, reverse, len_ref, order_ref, rate_ref, in_ref, out_ref, cont):
    slots = out_ref.shape[1] // rows
    head = (lax.axis_index("seq") * rows) // HEAD_SIZE
    factor = jnp.exp(jnp.full((8, LANES), -rate_ref[head] * span, F32))[0:1]

    def reset(c, carry):
        cont[c] = 1
        return carry

    def cut(d, end):
        end = end + len_ref[d]
        cont[end // span] = 0
        return end

    lax.fori_loop(0, spans + 1, reset, 0)
    lax.fori_loop(0, len_ref.shape[0], cut, jnp.int32(0))

    def body(i, state):
        c = spans - 1 - i if reverse else i
        place = order_ref[c]
        device, slot = place // slots, place % slots
        at = pl.ds(pl.multiple_of(slot * rows, rows), rows)
        out_ref[device, at, :] = state.astype(BF16)
        carried = jnp.where(cont[c] > 0, factor * state, 0.0)
        return carried + in_ref[device, at, :].astype(F32)

    lax.fori_loop(0, spans, body, jnp.zeros((rows, LANES), F32))


def fill_decay(decay, rate_ref, heads, span):
    j = lax.broadcasted_iota(jnp.int32, (span, span), 0)
    l = lax.broadcasted_iota(jnp.int32, (span, span), 1)
    spread = (j - l).astype(F32)
    for h in range(heads):
        decay[h] = jnp.where(
            spread >= 0.0, jnp.exp(-rate_ref[h] * jnp.maximum(spread, 0.0)), 0.0
        )


def local_kernel(heads, len_ref, home_ref, rate_ref, q_ref, k_ref, v_ref, out_ref, decay):
    step = pl.program_id(0)
    span = q_ref.shape[0]

    @pl.when(step == 0)
    def _():
        fill_decay(decay, rate_ref, heads, span)

    seg = segment_row(len_ref, home_ref[step] * span, span)
    same = row_to_cols(seg, span) == seg
    for h in range(heads):
        cols = head_cols(h)
        scores = dot(q_ref[:, cols], k_ref[:, cols], 1, 1)
        mixing = (scores * jnp.where(same, decay[h], 0.0)).astype(BF16)
        out_ref[:, cols] = dot(mixing, v_ref[:, cols], 1, 0).astype(BF16)


def output_kernel(
    heads, rows, len_ref, home_ref, rate_ref, gain_ref, q_ref, u_ref, inner_ref, prev_ref, out_ref, sums_ref, table
):
    step = pl.program_id(0)
    span = q_ref.shape[0]

    @pl.when(step == 0)
    def _():
        for h in range(heads):
            table[h] = query_table(rate_ref[h], span)

    first, _ = doc_bounds(len_ref, home_ref[step] * span, span)
    live = token_index(span) < first
    squares = jnp.zeros((span, LANES), F32)
    crossed = jnp.zeros((span, LANES), F32)
    for h in range(heads):
        cols = head_cols(h)
        outer = dot(q_ref[:, cols], get_state(prev_ref, h, rows), 1, 0)
        attn = inner_ref[:, cols].astype(F32) + jnp.where(live, table[h], 0.0) * outer
        out_ref[:, cols] = attn.astype(BF16)
        squares += attn * attn
        crossed += gain_ref[:, cols] * u_ref[:, cols].astype(F32) * attn
    sums_ref[0, 0:1, :] = cols_to_row(squares)
    sums_ref[0, 1:2, :] = cols_to_row(crossed)


def cotangent_kernel(
    heads, rows, channels, len_ref, home_ref, rate_ref, gain_ref, sums_ref, q_ref, u_ref, attn_ref, g_ref, out_ref, table
):
    step = pl.program_id(0)
    span = q_ref.shape[0]

    @pl.when(step == 0)
    def _():
        for h in range(heads):
            table[h] = query_table(rate_ref[h], span)

    total = jnp.sum(sums_ref[:, 0], axis=0)
    scaling = 1.0 / jnp.sqrt(total[0:1] / channels + EPSILON)
    pulled = total[1:2] / channels
    direct = row_to_cols(scaling, LANES)
    along = row_to_cols(scaling * scaling * scaling * pulled, LANES)
    first, _ = doc_bounds(len_ref, home_ref[step] * span, span)
    live = token_index(span) < first
    for h in range(heads):
        cols = head_cols(h)
        grad = direct * gain_ref[:, cols] * u_ref[:, cols].astype(F32)
        grad = grad - along * attn_ref[:, cols].astype(F32)
        grad = grad.astype(BF16)
        g_ref[:, cols] = grad
        weighted = (jnp.where(live, table[h], 0.0) * grad.astype(F32)).astype(BF16)
        put_state(out_ref, step, h, rows, dot(q_ref[:, cols], weighted, 0, 0).astype(BF16))


def inner_grads_kernel(
    heads, rows, len_ref, home_ref, rate_ref, q_ref, k_ref, v_ref, g_ref, prev_ref,
    dq_ref, dk_ref, dv_ref, decay, table,
):
    step = pl.program_id(0)
    span = q_ref.shape[0]

    @pl.when(step == 0)
    def _():
        fill_decay(decay, rate_ref, heads, span)
        for h in range(heads):
            table[h] = query_table(rate_ref[h], span)

    seg = segment_row(len_ref, home_ref[step] * span, span)
    same = row_to_cols(seg, span) == seg
    first, _ = doc_bounds(len_ref, home_ref[step] * span, span)
    live = token_index(span) < first
    for h in range(heads):
        cols = head_cols(h)
        q, k, v, g = q_ref[:, cols], k_ref[:, cols], v_ref[:, cols], g_ref[:, cols]
        mask = jnp.where(same, decay[h], 0.0)
        mixing = (dot(q, k, 1, 1) * mask).astype(BF16)
        score_grad = (dot(g, v, 1, 1) * mask).astype(BF16)
        outer = dot(g, get_state(prev_ref, h, rows), 1, 1)
        dq = dot(score_grad, k, 1, 0) + jnp.where(live, table[h], 0.0) * outer
        dq_ref[:, cols] = dq.astype(BF16)
        dk_ref[:, cols] = dot(score_grad, q, 0, 0).astype(BF16)
        dv_ref[:, cols] = dot(mixing, g, 0, 0).astype(BF16)


def outer_grads_kernel(
    heads, rows, len_ref, home_ref, rate_ref, k_ref, v_ref, after_ref, dk_in, dv_in, dk_ref, dv_ref, table
):
    step = pl.program_id(0)
    span = k_ref.shape[0]

    @pl.when(step == 0)
    def _():
        for h in range(heads):
            table[h] = key_table(rate_ref[h], span)

    _, last = doc_bounds(len_ref, home_ref[step] * span, span)
    live = token_index(span) >= last
    for h in range(heads):
        cols = head_cols(h)
        side = jnp.where(live, table[h], 0.0)
        after = get_state(after_ref, h, rows)
        dk = dk_in[:, cols].astype(F32) + side * dot(v_ref[:, cols], after, 1, 1)
        dv = dv_in[:, cols].astype(F32) + side * dot(k_ref[:, cols], after, 1, 0)
        dk_ref[:, cols] = dk.astype(BF16)
        dv_ref[:, cols] = dv.astype(BF16)


def exchange(blocks):
    return lax.all_to_all(blocks, "seq", split_axis=0, concat_axis=0, tiled=True)


def shards(query, key, value, upstream, norm_gain, decay_rate, document_lengths, group_home):
    devices = lax.axis_size("seq")
    tokens, width = query.shape
    heads = width // HEAD_SIZE
    slots = group_home.shape[0]
    span = tokens // slots
    spans = slots * devices
    rows = width // devices
    channels = width * lax.axis_size("head")
    params = pltpu.CompilerParams(vmem_limit_bytes=60 << 20)
    roomy = pltpu.CompilerParams(vmem_limit_bytes=16 << 20)

    smem = pl.BlockSpec(memory_space=pltpu.SMEM)
    tok = pl.BlockSpec((span, width), lambda i: (i, 0))
    gain_spec = pl.BlockSpec((1, width), lambda i: (0, 0))
    state_spec = pl.BlockSpec((devices, 1, rows, LANES), lambda i: (0, i, 0, 0))
    gain = norm_gain.reshape(1, width)

    def whole(shape):
        return pl.BlockSpec(shape, lambda i: (0,) * len(shape))

    def shaped(shape, dtype):
        return jax.ShapeDtypeStruct(shape, dtype)

    side_table = pltpu.VMEM((heads, span, LANES), F32)
    decay_table = pltpu.VMEM((heads, span, span), F32)
    packed = (devices, slots * rows + TAIL, LANES)
    plain = (devices, slots * rows, LANES)

    sent = pl.pallas_call(
        functools.partial(summary_kernel, heads, rows),
        grid=(slots,),
        in_specs=[smem, smem, smem, tok, tok],
        out_specs=whole(packed),
        out_shape=shaped(packed, BF16),
        scratch_shapes=[side_table],
        compiler_params=params,
        name="summaries",
    )(document_lengths, group_home, decay_rate, key, value)

    arrived = exchange(sent)

    inner = pl.pallas_call(
        functools.partial(local_kernel, heads),
        grid=(slots,),
        in_specs=[smem, smem, smem, tok, tok, tok],
        out_specs=tok,
        out_shape=shaped((tokens, width), BF16),
        scratch_shapes=[decay_table],
        compiler_params=params,
        name="inner",
    )(document_lengths, group_home, decay_rate, query, key, value)

    homes = arrived[:, slots * rows, :slots].astype(jnp.int32).reshape(-1)
    hits = homes[None, :] == jnp.arange(spans, dtype=jnp.int32)[:, None]
    order = jnp.sum(jnp.where(hits, jnp.arange(spans, dtype=jnp.int32)[None, :], 0), axis=1)

    def scan(blocks, reverse):
        return pl.pallas_call(
            functools.partial(scan_kernel, rows, spans, span, reverse),
            grid=(1,),
            in_specs=[smem, smem, smem, whole(blocks.shape)],
            out_specs=whole(plain),
            out_shape=shaped(plain, BF16),
            scratch_shapes=[pltpu.SMEM((spans + 1,), jnp.int32)],
            compiler_params=roomy,
            name="scan",
        )(document_lengths, order, decay_rate, blocks)

    prev = exchange(scan(arrived, False)).reshape(devices, slots, rows, LANES)

    attn, sums = pl.pallas_call(
        functools.partial(output_kernel, heads, rows),
        grid=(slots,),
        in_specs=[smem, smem, smem, gain_spec, tok, tok, tok, state_spec],
        out_specs=[tok, pl.BlockSpec((1, 2, span), lambda i: (i, 0, 0))],
        out_shape=[shaped((tokens, width), BF16), shaped((slots, 2, span), F32)],
        scratch_shapes=[side_table],
        compiler_params=params,
        name="output",
    )(document_lengths, group_home, decay_rate, gain, query, upstream, inner, prev)

    sums = lax.all_gather(sums, "head")

    grad_in, rev_sent = pl.pallas_call(
        functools.partial(cotangent_kernel, heads, rows, channels),
        grid=(slots,),
        in_specs=[
            smem, smem, smem, gain_spec,
            pl.BlockSpec((sums.shape[0], 1, 2, span), lambda i: (0, i, 0, 0)),
            tok, tok, tok,
        ],
        out_specs=[tok, whole(plain)],
        out_shape=[shaped((tokens, width), BF16), shaped(plain, BF16)],
        scratch_shapes=[side_table],
        compiler_params=params,
        name="cotangent",
    )(document_lengths, group_home, decay_rate, gain, sums, query, upstream, attn)

    rev_arrived = exchange(rev_sent)

    query_grad, key_inner, value_inner = pl.pallas_call(
        functools.partial(inner_grads_kernel, heads, rows),
        grid=(slots,),
        in_specs=[smem, smem, smem, tok, tok, tok, tok, state_spec],
        out_specs=[tok, tok, tok],
        out_shape=[shaped((tokens, width), BF16), shaped((tokens, width), BF16), shaped((tokens, width), BF16)],
        scratch_shapes=[decay_table, side_table],
        compiler_params=params,
        name="inner_grads",
    )(document_lengths, group_home, decay_rate, query, key, value, grad_in, prev)

    after = exchange(scan(rev_arrived, True)).reshape(devices, slots, rows, LANES)

    key_grad, value_grad = pl.pallas_call(
        functools.partial(outer_grads_kernel, heads, rows),
        grid=(slots,),
        in_specs=[smem, smem, smem, tok, tok, state_spec, tok, tok],
        out_specs=[tok, tok],
        out_shape=[shaped((tokens, width), BF16)] * 2,
        scratch_shapes=[side_table],
        compiler_params=params,
        name="outer_grads",
    )(document_lengths, group_home, decay_rate, key, value, after, key_inner, value_inner)
    return query_grad, key_grad, value_grad


def solution(mesh):
    in_specs = (
        P("seq", "head"),
        P("seq", "head"),
        P("seq", "head"),
        P("seq", "head"),
        P("head"),
        P("head"),
        P(),
        P("seq"),
    )
    out_specs = (P("seq", "head"), P("seq", "head"), P("seq", "head"))
    return jax.shard_map(shards, mesh=mesh, in_specs=in_specs, out_specs=out_specs, check_vma=False)
```

time: 177 us -> 172 us (0.972)
  blocking collectives: 5.24 us -> 71.4 us
  waiting for transfers between devices: 69.1 us -> 27.5 us
  local copies, waits for them, and re-layouts: 34.9 us -> 2.02 us
  Pallas kernels: 43 us -> 62.3 us
  starting transfers between devices: 19.6 us -> 7.19 us
  other arithmetic: 2.73 us -> 0.13 us
    all_to_all x0 -> x2, blocking collectives: none -> 64.8 us  [exchange(): lax.all_to_all(blocks, 'seq', split_axis=0, concat_axis=0, tiled=True)]
    all_to_all x4 -> x2, waiting for transfers between devices: 69.1 us -> 27.5 us  [exchange(): lax.all_to_all(blocks, 'seq', split_axis=0, concat_axis=0, tiled=True)]
    unnamed x52 -> x12, local copies, waits for them, and re-layouts: 33.9 us -> 1.94 us
    all_to_all x4 -> x2, starting transfers between devices: 19.6 us -> 7.19 us  [exchange(): lax.all_to_all(blocks, 'seq', split_axis=0, concat_axis=0, tiled=True)]
    pallas_call x1, Pallas kernels: 3.82 us -> 7.76 us  [shards(): pl.pallas_call(functools.partial(output_kernel, heads, rows), grid=(slots...]
    pallas_call x1, Pallas kernels: 4.46 us -> 8.27 us  [shards(): pl.pallas_call(functools.partial(cotangent_kernel, heads, rows, channels)...]
    pallas_call x1, Pallas kernels: 3.95 us -> 7.07 us  [shards(): pl.pallas_call(functools.partial(summary_kernel, heads, rows), grid=(slot...]
    pallas_call x1, Pallas kernels: 6.18 us -> 9.29 us  [shards(): pl.pallas_call(functools.partial(local_kernel, heads), grid=(slots,), in_...]
  transfers between devices with their start and end apart: 4 -> 2, of which waited for: 4 -> 2; matrix products, arithmetic and copies ran while one was open for 1% -> 0% of each run, Pallas kernels for 11% -> 14%
where the time goes in v2:
time: 172 us; the launch traced here: 171 us
  blocking collectives  71.4 us (42%)
  Pallas kernels  62.3 us (36%)
  waiting for transfers between devices  27.5 us (16%)
  starting transfers between devices  7.19 us (4%)
  local copies, waits for them, and re-layouts  2.02 us (1%)
    all_to_all x2, blocking collectives, exchange(): lax.all_to_all(blocks, 'seq', split_axis=0, concat_axis=0, tiled=True)  64.8 us
    all_to_all x2, waiting for transfers between devices, exchange(): lax.all_to_all(blocks, 'seq', split_axis=0, concat_axis=0, tiled=True)  27.5 us
    pallas_call x1, Pallas kernels, shards(): pl.pallas_call(functools.partial(inner_grads_kernel, heads, rows), grid=(...  14.4 us
    pallas_call x1, Pallas kernels, shards(): pl.pallas_call(functools.partial(local_kernel, heads), grid=(slots,), in_...  9.29 us
    pallas_call x1, Pallas kernels, shards(): pl.pallas_call(functools.partial(outer_grads_kernel, heads, rows), grid=(...  8.75 us
    pallas_call x1, Pallas kernels, shards(): pl.pallas_call(functools.partial(cotangent_kernel, heads, rows, channels)...  8.27 us
    pallas_call x1, Pallas kernels, shards(): pl.pallas_call(functools.partial(output_kernel, heads, rows), grid=(slots...  7.76 us
    all_to_all x2, starting transfers between devices, exchange(): lax.all_to_all(blocks, 'seq', split_axis=0, concat_axis=0, tiled=True)  7.19 us
  transfers between devices with their start and end apart: 2, of which 2 were waited for; matrix products, arithmetic and copies ran while one was open for 0% of the time, Pallas kernels for 14%

profile of v2, /device:TPU:0, one launch (start us, length us, event | category | flops | bytes accessed | tf_op | source)
XLA Modules:
  0.0 171.2 jit_solution(7666973264753068619)
XLA Ops:
  0.6 7.1 %summaries.1 = bf16[8,528,128]{2,1,0:T(8,128)(2,1)} custom-call(s32[32]{0:T(128)} %len_ref.15, s32[8]{0:T(128)} %home_ref.11, f32[4]{0:T(128)} %rate_ref.15, bf16[2048,512]{1,0:T(8,128)(2,1)} %k_ref.7, bf16[2048,512]{1,0:T(8,128)(2,1)} %v_ref.7), custom_call_target="tpu_custom_call" | custom-call | tf_op jit(solution)/shard_map/summaries/pallas_call | solution.py:301
  7.7 0.0 copy-start
  7.7 0.0 copy-start.2
  7.7 34.6 %all_to_all.20.in_ref = bf16[8,528,128]{2,1,0:T(8,128)(2,1)S(1)} all-to-all(bf16[8,528,128]{2,1,0:T(8,128)(2,1)} %summaries.1), channel_id=1, replica_groups=mesh['seq'=8,'head'=4] {'seq'}, dimensions={0} | all-to-all | bytes 2162688 | tf_op jit(solution)/shard_map/all_to_all | solution.py:269
  42.4 0.1 reshape.25
  42.4 0.1 select_reduce_fusion.order_ref
  42.6 0.0 copy-done
  42.6 0.0 copy-done.2
  42.6 3.4 %scan.2 = bf16[8,512,128]{2,1,0:T(8,128)(2,1)} custom-call(s32[32]{0:T(128)S(1)} %copy-done, s32[64]{0:T(128)S(1)} %select_reduce_fusion.order_ref, f32[4]{0:T(128)S(1)} %copy-done.2, bf16[8,528,128]{2,1,0:T(8,128)(2,1)S(1)} %all_to_all.20.in_ref), custom_call_target="tpu_custom_call" | custom-call | tf_op jit(solution)/shard_map/scan/pallas_call | solution.py:330
  46.0 3.6 %all-to-all-start.1 = ((bf16[8,512,128]{2,1,0:T(8,128)(2,1)}), bf16[8,512,128]{2,1,0:T(8,128)(2,1)S(1)}, u32[]{:S(2)}, u32[]{:S(2)}) async-start(bf16[8,512,128]{2,1,0:T(8,128)(2,1)} %scan.2), calls=%async_computation.1 | async-start | bytes 2097152 | tf_op jit(solution)/shard_map/all_to_all | solution.py:269
  49.6 9.3 %inner.1.inner_ref = bf16[2048,512]{1,0:T(8,128)(2,1)} custom-call(s32[32]{0:T(128)} %len_ref.15, s32[8]{0:T(128)} %home_ref.11, f32[4]{0:T(128)} %rate_ref.15, bf16[2048,512]{1,0:T(8,128)(2,1)} %q_ref.7, bf16[2048,512]{1,0:T(8,128)(2,1)} %k_ref.7, bf16[2048,512]{1,0:T(8,128)(2,1)} %v_ref.7), custom_call_target="tpu_custom_call" | custom-call | tf_op jit(solution)/shard_map/inner/pallas_call | solution.py:314
  58.9 15.9 %all-to-all-done.1 = bf16[8,512,128]{2,1,0:T(8,128)(2,1)S(1)} async-done(((bf16[8,512,128]{2,1,0:T(8,128)(2,1)}), bf16[8,512,128]{2,1,0:T(8,128)(2,1)S(1)}, u32[]{:S(2)}, u32[]{:S(2)}) %all-to-all-start.1) | async-done | bytes 1048608 | tf_op jit(solution)/shard_map/all_to_all | solution.py:269
  74.7 0.0 copy-start.4
  74.7 1.0 copy-done.4
  75.7 7.8 %output.1 = (bf16[2048,512]{1,0:T(8,128)(2,1)}, f32[8,2,256]{2,1,0:T(2,128)}) custom-call(s32[32]{0:T(128)} %len_ref.15, s32[8]{0:T(128)} %home_ref.11, f32[4]{0:T(128)} %rate_ref.15, f32[1,512]{1,0:T(1,128)} %bitcast.8, bf16[2048,512]{1,0:T(8,128)(2,1)} %q_ref.7, bf16[2048,512]{1,0:T(8,128)(2,1)} %u_ref.3, bf16[2048,512]{1,0:T(8,128)(2,1)} %inner.1.inner_ref, ...), custom_call_target="tpu_custom_call" | custom-call | tf_op jit(solution)/shard_map/output/pallas_call | solution.py:343
  83.4 6.7 %all-gather = f32[32,2,256]{2,1,0:T(2,128)} all-gather(f32[8,2,256]{2,1,0:T(2,128)} %get-tuple-element.12), channel_id=2, replica_groups=mesh['seq'=8,'head'=4] {'head'}, dimensions={0}, use_global_device_ids=true | all-gather | bytes 81920 | tf_op jit(solution)/shard_map/all_gather | solution.py:354
  90.1 8.3 %cotangent.1 = (bf16[2048,512]{1,0:T(8,128)(2,1)}, bf16[8,512,128]{2,1,0:T(8,128)(2,1)}) custom-call(s32[32]{0:T(128)} %len_ref.15, s32[8]{0:T(128)} %home_ref.11, f32[4]{0:T(128)} %rate_ref.15, f32[1,512]{1,0:T(1,128)} %bitcast.9, f32[4,8,2,256]{3,2,1,0:T(2,128)} %bitcast.7, bf16[2048,512]{1,0:T(8,128)(2,1)} %q_ref.7, bf16[2048,512]{1,0:T(8,128)(2,1)} %u_ref.3, ...), custom_call_target="tpu_custom_call" | custom-call | tf_op jit(solution)/shard_map/cotangent/pallas_call | solution.py:356
  98.4 0.0 copy-start.1
  98.4 0.0 copy-start.3
  98.4 30.1 %all_to_all.21.in_ref = bf16[8,512,128]{2,1,0:T(8,128)(2,1)S(1)} all-to-all(bf16[8,512,128]{2,1,0:T(8,128)(2,1)} %get-tuple-element.16), channel_id=1, replica_groups=mesh['seq'=8,'head'=4] {'seq'}, dimensions={0} | all-to-all | bytes 2097152 | tf_op jit(solution)/shard_map/all_to_all | solution.py:269
  128.5 0.0 copy-done.1
  128.5 0.0 copy-done.3
  128.5 3.3 %scan.3 = bf16[8,512,128]{2,1,0:T(8,128)(2,1)} custom-call(s32[32]{0:T(128)S(1)} %copy-done.1, s32[64]{0:T(128)S(1)} %select_reduce_fusion.order_ref, f32[4]{0:T(128)S(1)} %copy-done.3, bf16[8,512,128]{2,1,0:T(8,128)(2,1)S(1)} %all_to_all.21.in_ref), custom_call_target="tpu_custom_call" | custom-call | tf_op jit(solution)/shard_map/scan/pallas_call | solution.py:330
  131.9 3.6 %all-to-all-start.3 = ((bf16[8,512,128]{2,1,0:T(8,128)(2,1)}), bf16[8,512,128]{2,1,0:T(8,128)(2,1)S(1)}, u32[]{:S(2)}, u32[]{:S(2)}) async-start(bf16[8,512,128]{2,1,0:T(8,128)(2,1)} %scan.3), calls=%async_computation.3 | async-start | bytes 2097152 | tf_op jit(solution)/shard_map/all_to_all | solution.py:269
  135.5 14.4 %inner_grads.1 = (bf16[2048,512]{1,0:T(8,128)(2,1)}, bf16[2048,512]{1,0:T(8,128)(2,1)}, bf16[2048,512]{1,0:T(8,128)(2,1)}) custom-call(s32[32]{0:T(128)} %len_ref.15, s32[8]{0:T(128)} %home_ref.11, f32[4]{0:T(128)} %rate_ref.15, bf16[2048,512]{1,0:T(8,128)(2,1)} %q_ref.7, bf16[2048,512]{1,0:T(8,128)(2,1)} %k_ref.7, bf16[2048,512]{1,0:T(8,128)(2,1)} %v_ref.7, ...), custom_call_target="tpu_custom_call" | custom-call | tf_op jit(solution)/shard_map/inner_grads/pallas_call | solution.py:373
  149.9 11.6 %all-to-all-done.3 = bf16[8,512,128]{2,1,0:T(8,128)(2,1)S(1)} async-done(((bf16[8,512,128]{2,1,0:T(8,128)(2,1)}), bf16[8,512,128]{2,1,0:T(8,128)(2,1)S(1)}, u32[]{:S(2)}, u32[]{:S(2)}) %all-to-all-start.3) | async-done | bytes 1048608 | tf_op jit(solution)/shard_map/all_to_all | solution.py:269
  161.5 0.0 copy-start.5
  161.5 1.0 copy-done.5
  162.4 8.8 %outer_grads.1 = (bf16[2048,512]{1,0:T(8,128)(2,1)}, bf16[2048,512]{1,0:T(8,128)(2,1)}) custom-call(s32[32]{0:T(128)} %len_ref.15, s32[8]{0:T(128)} %home_ref.11, f32[4]{0:T(128)} %rate_ref.15, bf16[2048,512]{1,0:T(8,128)(2,1)} %k_ref.7, bf16[2048,512]{1,0:T(8,128)(2,1)} %v_ref.7, bf16[8,8,64,128]{3,2,1,0:T(8,128)(2,1)} %bitcast.6, ...), custom_call_target="tpu_custom_call" | custom-call | tf_op jit(solution)/shard_map/outer_grads/pallas_call | solution.py:386
  (1 shorter events, 0.0 us)
Async XLA Ops:
  7.7 34.9 %copy-start = (s32[32]{0:T(128)S(1)}, s32[32]{0:T(128)}, u32[]{:S(2)}) copy-start(s32[32]{0:T(128)} %len_ref.15) | copy-start | bytes 388
  7.7 34.9 %copy-start.2 = (f32[4]{0:T(128)S(1)}, f32[4]{0:T(128)}, u32[]{:S(2)}) copy-start(f32[4]{0:T(128)} %rate_ref.15) | copy-start | bytes 52
  46.0 28.7 %all-to-all-start.1 = ((bf16[8,512,128]{2,1,0:T(8,128)(2,1)}), bf16[8,512,128]{2,1,0:T(8,128)(2,1)S(1)}, u32[]{:S(2)}, u32[]{:S(2)}) async-start(bf16[8,512,128]{2,1,0:T(8,128)(2,1)} %scan.2), calls=%async_computation.1 | async-start | bytes 2097152 | tf_op jit(solution)/shard_map/all_to_all | solution.py:269
  74.7 1.0 copy-start.4
  98.4 30.1 %copy-start.1 = (s32[32]{0:T(128)S(1)}, s32[32]{0:T(128)}, u32[]{:S(2)}) copy-start(s32[32]{0:T(128)} %len_ref.15) | copy-start | bytes 388
  98.4 30.1 %copy-start.3 = (f32[4]{0:T(128)S(1)}, f32[4]{0:T(128)}, u32[]{:S(2)}) copy-start(f32[4]{0:T(128)} %rate_ref.15) | copy-start | bytes 52
  131.9 29.6 %all-to-all-start.3 = ((bf16[8,512,128]{2,1,0:T(8,128)(2,1)}), bf16[8,512,128]{2,1,0:T(8,128)(2,1)S(1)}, u32[]{:S(2)}, u32[]{:S(2)}) async-start(bf16[8,512,128]{2,1,0:T(8,128)(2,1)} %scan.3), calls=%async_computation.3 | async-start | bytes 2097152 | tf_op jit(solution)/shard_map/all_to_all | solution.py:269
  161.5 1.0 copy-start.5

commit v3 on v2

--- a/solution.py
+++ b/solution.py
@@ -44,26 +44,26 @@
     return jnp.sum(jnp.transpose(cols), axis=0, keepdims=True)
 
 
-def doc_bounds(len_ref, start, span):
-    end = jnp.int32(0)
-    first = jnp.int32(0)
-    last = jnp.int32(0)
-    for d in range(len_ref.shape[0]):
-        before = end
+def fill_tables(len_ref, first_ref, last_ref, span):
+    spans = first_ref.shape[0] - 1
+    far = jnp.int32(spans * span)
+
+    def reset(c, carry):
+        first_ref[c] = far
+        last_ref[c] = 0
+        return carry
+
+    def note(d, end):
         end = end + len_ref[d]
-        first = jnp.where((before < start) & (end >= start), end, first)
-        last = jnp.where(end < start + span, end, last)
-    return first - start, last - start
-
-
-def segment_row(len_ref, start, span):
-    position = start + lax.broadcasted_iota(jnp.int32, (1, span), 1)
-    end = jnp.int32(0)
-    segment = jnp.zeros((1, span), F32)
-    for d in range(len_ref.shape[0]):
-        end = end + len_ref[d]
-        segment += jnp.where(end <= position, 1.0, 0.0)
-    return segment
+        c = lax.shift_right_logical(end, span.bit_length() - 1) if span & (span - 1) == 0 else end // span
+        inside = end - c * span
+        last_ref[c] = inside
+        first_ref[c] = jnp.minimum(first_ref[c], inside)
+        return end
+
+    lax.fori_loop(0, spans + 1, reset, 0, unroll=8)
+    lax.fori_loop(0, len_ref.shape[0], note, jnp.int32(0), unroll=4)
+    first_ref[0] = 0
 
 
 def put_state(out_ref, step, h, rows, value):
@@ -79,12 +79,15 @@
     return ref[h * chunks : (h + 1) * chunks, 0].reshape(HEAD_SIZE, HEAD_SIZE)
 
 
-def summary_kernel(heads, rows, len_ref, home_ref, rate_ref, k_ref, v_ref, out_ref, table):
+def summary_kernel(
+    heads, rows, len_ref, home_ref, rate_ref, k_ref, v_ref, out_ref, first_ref, last_ref, table
+):
     step = pl.program_id(0)
     span = k_ref.shape[0]
 
     @pl.when(step == 0)
     def _():
+        fill_tables(len_ref, first_ref, last_ref, span)
         for h in range(heads):
             table[h] = key_table(rate_ref[h], span)
         tail = jnp.zeros((TAIL, LANES), F32)
@@ -94,30 +97,17 @@
         for d in range(out_ref.shape[0]):
             out_ref[d, out_ref.shape[1] - TAIL :, :] = tail.astype(BF16)
 
-    _, last = doc_bounds(len_ref, home_ref[step] * span, span)
-    live = token_index(span) >= last
+    live = token_index(span) >= last_ref[home_ref[step]]
     for h in range(heads):
         side = jnp.where(live, table[h], 0.0)
         weighted = (side * v_ref[:, head_cols(h)].astype(F32)).astype(BF16)
         put_state(out_ref, step, h, rows, dot(k_ref[:, head_cols(h)], weighted, 0, 0).astype(BF16))
 
 
-def scan_kernel(rows, spans, span, reverse, len_ref, order_ref, rate_ref, in_ref, out_ref, cont):
+def scan_kernel(rows, spans, span, reverse, first_ref, order_ref, rate_ref, in_ref, out_ref):
     slots = out_ref.shape[1] // rows
     head = (lax.axis_index("seq") * rows) // HEAD_SIZE
     factor = jnp.exp(jnp.full((8, LANES), -rate_ref[head] * span, F32))[0:1]
-
-    def reset(c, carry):
-        cont[c] = 1
-        return carry
-
-    def cut(d, end):
-        end = end + len_ref[d]
-        cont[end // span] = 0
-        return end
-
-    lax.fori_loop(0, spans + 1, reset, 0)
-    lax.fori_loop(0, len_ref.shape[0], cut, jnp.int32(0))
 
     def body(i, state):
         c = spans - 1 - i if reverse else i
@@ -125,7 +115,7 @@
         device, slot = place // slots, place % slots
         at = pl.ds(pl.multiple_of(slot * rows, rows), rows)
         out_ref[device, at, :] = state.astype(BF16)
-        carried = jnp.where(cont[c] > 0, factor * state, 0.0)
+        carried = jnp.where(first_ref[c] >= span, factor * state, 0.0)
         return carried + in_ref[device, at, :].astype(F32)
 
     lax.fori_loop(0, spans, body, jnp.zeros((rows, LANES), F32))
@@ -141,7 +131,7 @@
         )
 
 
-def local_kernel(heads, len_ref, home_ref, rate_ref, q_ref, k_ref, v_ref, out_ref, decay):
+def local_kernel(heads, rate_ref, seg_ref, q_ref, k_ref, v_ref, out_ref, decay):
     step = pl.program_id(0)
     span = q_ref.shape[0]
 
@@ -149,7 +139,7 @@
     def _():
         fill_decay(decay, rate_ref, heads, span)
 
-    seg = segment_row(len_ref, home_ref[step] * span, span)
+    seg = seg_ref[0]
     same = row_to_cols(seg, span) == seg
     for h in range(heads):
         cols = head_cols(h)
@@ -159,7 +149,7 @@
 
 
 def output_kernel(
-    heads, rows, len_ref, home_ref, rate_ref, gain_ref, q_ref, u_ref, inner_ref, prev_ref, out_ref, sums_ref, table
+    heads, rows, first_ref, home_ref, rate_ref, gain_ref, q_ref, u_ref, inner_ref, prev_ref, out_ref, sums_ref, table
 ):
     step = pl.program_id(0)
     span = q_ref.shape[0]
@@ -169,8 +159,7 @@
         for h in range(heads):
             table[h] = query_table(rate_ref[h], span)
 
-    first, _ = doc_bounds(len_ref, home_ref[step] * span, span)
-    live = token_index(span) < first
+    live = token_index(span) < first_ref[home_ref[step]]
     squares = jnp.zeros((span, LANES), F32)
     crossed = jnp.zeros((span, LANES), F32)
     for h in range(heads):
@@ -185,7 +174,7 @@
 
 
 def cotangent_kernel(
-    heads, rows, channels, len_ref, home_ref, rate_ref, gain_ref, sums_ref, q_ref, u_ref, attn_ref, g_ref, out_ref, table
+    heads, rows, channels, first_ref, home_ref, rate_ref, gain_ref, sums_ref, q_ref, u_ref, attn_ref, g_ref, out_ref, table
 ):
     step = pl.program_id(0)
     span = q_ref.shape[0]
@@ -200,8 +189,7 @@
     pulled = total[1:2] / channels
     direct = row_to_cols(scaling, LANES)
     along = row_to_cols(scaling * scaling * scaling * pulled, LANES)
-    first, _ = doc_bounds(len_ref, home_ref[step] * span, span)
-    live = token_index(span) < first
+    live = token_index(span) < first_ref[home_ref[step]]
     for h in range(heads):
         cols = head_cols(h)
         grad = direct * gain_ref[:, cols] * u_ref[:, cols].astype(F32)
@@ -213,7 +201,7 @@
 
 
 def inner_grads_kernel(
-    heads, rows, len_ref, home_ref, rate_ref, q_ref, k_ref, v_ref, g_ref, prev_ref,
+    heads, rows, first_ref, home_ref, rate_ref, seg_ref, q_ref, k_ref, v_ref, g_ref, prev_ref,
     dq_ref, dk_ref, dv_ref, decay, table,
 ):
     step = pl.program_id(0)
@@ -225,10 +213,9 @@
         for h in range(heads):
             table[h] = query_table(rate_ref[h], span)
 
-    seg = segment_row(len_ref, home_ref[step] * span, span)
+    seg = seg_ref[0]
     same = row_to_cols(seg, span) == seg
-    first, _ = doc_bounds(len_ref, home_ref[step] * span, span)
-    live = token_index(span) < first
+    live = token_index(span) < first_ref[home_ref[step]]
     for h in range(heads):
         cols = head_cols(h)
         q, k, v, g = q_ref[:, cols], k_ref[:, cols], v_ref[:, cols], g_ref[:, cols]
@@ -243,7 +230,7 @@
 
 
 def outer_grads_kernel(
-    heads, rows, len_ref, home_ref, rate_ref, k_ref, v_ref, after_ref, dk_in, dv_in, dk_ref, dv_ref, table
+    heads, rows, last_ref, home_ref, rate_ref, k_ref, v_ref, after_ref, dk_in, dv_in, dk_ref, dv_ref, table
 ):
     step = pl.program_id(0)
     span = k_ref.shape[0]
@@ -253,8 +240,7 @@
         for h in range(heads):
             table[h] = key_table(rate_ref[h], span)
 
-    _, last = doc_bounds(len_ref, home_ref[step] * span, span)
-    live = token_index(span) >= last
+    live = token_index(span) >= last_ref[home_ref[step]]
     for h in range(heads):
         cols = head_cols(h)
         side = jnp.where(live, table[h], 0.0)
@@ -278,10 +264,17 @@
     spans = slots * devices
     rows = width // devices
     channels = width * lax.axis_size("head")
-    params = pltpu.CompilerParams(vmem_limit_bytes=60 << 20)
+    alone = pltpu.CompilerParams(vmem_limit_bytes=60 << 20)
+    params = pltpu.CompilerParams(vmem_limit_bytes=52 << 20)
     roomy = pltpu.CompilerParams(vmem_limit_bytes=16 << 20)
 
+    doc_ends = jnp.cumsum(document_lengths)
+    positions = (group_home * span)[:, None] + jnp.arange(span, dtype=jnp.int32)[None, :]
+    seg = jnp.sum((doc_ends <= positions[..., None]).astype(F32), axis=-1).reshape(slots, 1, span)
+
     smem = pl.BlockSpec(memory_space=pltpu.SMEM)
+    seg_spec = pl.BlockSpec((1, 1, span), lambda i: (i, 0, 0))
+    spans_table = jax.ShapeDtypeStruct((spans + 1,), jnp.int32)
     tok = pl.BlockSpec((span, width), lambda i: (i, 0))
     gain_spec = pl.BlockSpec((1, width), lambda i: (0, 0))
     state_spec = pl.BlockSpec((devices, 1, rows, LANES), lambda i: (0, i, 0, 0))
@@ -298,14 +291,14 @@
     packed = (devices, slots * rows + TAIL, LANES)
     plain = (devices, slots * rows, LANES)
 
-    sent = pl.pallas_call(
+    sent, first, last = pl.pallas_call(
         functools.partial(summary_kernel, heads, rows),
         grid=(slots,),
         in_specs=[smem, smem, smem, tok, tok],
-        out_specs=whole(packed),
-        out_shape=shaped(packed, BF16),
+        out_specs=[whole(packed), smem, smem],
+        out_shape=[shaped(packed, BF16), spans_table, spans_table],
         scratch_shapes=[side_table],
-        compiler_params=params,
+        compiler_params=alone,
         name="summaries",
     )(document_lengths, group_home, decay_rate, key, value)
 
@@ -314,13 +307,13 @@
     inner = pl.pallas_call(
         functools.partial(local_kernel, heads),
         grid=(slots,),
-        in_specs=[smem, smem, smem, tok, tok, tok],
+        in_specs=[smem, seg_spec, tok, tok, tok],
         out_specs=tok,
         out_shape=shaped((tokens, width), BF16),
         scratch_shapes=[decay_table],
         compiler_params=params,
         name="inner",
-    )(document_lengths, group_home, decay_rate, query, key, value)
+    )(decay_rate, seg, query, key, value)
 
     homes = arrived[:, slots * rows, :slots].astype(jnp.int32).reshape(-1)
     hits = homes[None, :] == jnp.arange(spans, dtype=jnp.int32)[:, None]
@@ -333,10 +326,9 @@
             in_specs=[smem, smem, smem, whole(blocks.shape)],
             out_specs=whole(plain),
             out_shape=shaped(plain, BF16),
-            scratch_shapes=[pltpu.SMEM((spans + 1,), jnp.int32)],
             compiler_params=roomy,
             name="scan",
-        )(document_lengths, order, decay_rate, blocks)
+        )(first, order, decay_rate, blocks)
 
     prev = exchange(scan(arrived, False)).reshape(devices, slots, rows, LANES)
 
@@ -349,7 +341,7 @@
         scratch_shapes=[side_table],
         compiler_params=params,
         name="output",
-    )(document_lengths, group_home, decay_rate, gain, query, upstream, inner, prev)
+    )(first, group_home, decay_rate, gain, query, upstream, inner, prev)
 
     sums = lax.all_gather(sums, "head")
 
@@ -366,20 +358,20 @@
         scratch_shapes=[side_table],
         compiler_params=params,
         name="cotangent",
-    )(document_lengths, group_home, decay_rate, gain, sums, query, upstream, attn)
+    )(first, group_home, decay_rate, gain, sums, query, upstream, attn)
 
     rev_arrived = exchange(rev_sent)
 
     query_grad, key_inner, value_inner = pl.pallas_call(
         functools.partial(inner_grads_kernel, heads, rows),
         grid=(slots,),
-        in_specs=[smem, smem, smem, tok, tok, tok, tok, state_spec],
+        in_specs=[smem, smem, smem, seg_spec, tok, tok, tok, tok, state_spec],
         out_specs=[tok, tok, tok],
         out_shape=[shaped((tokens, width), BF16), shaped((tokens, width), BF16), shaped((tokens, width), BF16)],
         scratch_shapes=[decay_table, side_table],
         compiler_params=params,
         name="inner_grads",
-    )(document_lengths, group_home, decay_rate, query, key, value, grad_in, prev)
+    )(first, group_home, decay_rate, seg, query, key, value, grad_in, prev)
 
     after = exchange(scan(rev_arrived, True)).reshape(devices, slots, rows, LANES)
 
@@ -392,7 +384,7 @@
         scratch_shapes=[side_table],
         compiler_params=params,
         name="outer_grads",
-    )(document_lengths, group_home, decay_rate, key, value, after, key_inner, value_inner)
+    )(last, group_home, decay_rate, key, value, after, key_inner, value_inner)
     return query_grad, key_grad, value_grad
 
 

time: 172 us -> 166 us (0.965)
  Pallas kernels: 62.3 us -> 59.8 us
  blocking collectives: 71.4 us -> 69.1 us
  local copies, waits for them, and re-layouts: 2.02 us -> 0.21 us
    unnamed x12, local copies, waits for them, and re-layouts: 1.94 us -> 0.04 us
where the time goes in v3:
time: 166 us; the launch traced here: 164 us
  blocking collectives  69.1 us (42%)
  Pallas kernels  59.8 us (36%)
  waiting for transfers between devices  26.9 us (16%)
  starting transfers between devices  7.2 us (4%)
    all_to_all x2, blocking collectives, exchange(): lax.all_to_all(blocks, 'seq', split_axis=0, concat_axis=0, tiled=True)  63.9 us
    all_to_all x2, waiting for transfers between devices, exchange(): lax.all_to_all(blocks, 'seq', split_axis=0, concat_axis=0, tiled=True)  26.9 us
    pallas_call x1, Pallas kernels, shards(): pl.pallas_call(functools.partial(inner_grads_kernel, heads, rows), grid=(...  14.4 us
    pallas_call x1, Pallas kernels, shards(): pl.pallas_call(functools.partial(local_kernel, heads), grid=(slots,), in_...  9.25 us
    pallas_call x1, Pallas kernels, shards(): pl.pallas_call(functools.partial(outer_grads_kernel, heads, rows), grid=(...  8.49 us
    pallas_call x1, Pallas kernels, shards(): pl.pallas_call(functools.partial(cotangent_kernel, heads, rows, channels)...  7.7 us
    pallas_call x1, Pallas kernels, shards(): pl.pallas_call(functools.partial(output_kernel, heads, rows), grid=(slots...  7.54 us
    all_to_all x2, starting transfers between devices, exchange(): lax.all_to_all(blocks, 'seq', split_axis=0, concat_axis=0, tiled=True)  7.2 us
  transfers between devices with their start and end apart: 2, of which 2 were waited for; matrix products, arithmetic and copies ran while one was open for 0% of the time, Pallas kernels for 14%

profile of v3, /device:TPU:0, one launch (start us, length us, event | category | flops | bytes accessed | tf_op | source)
XLA Modules:
  0.0 164.4 jit_solution(18137339529906562368)
XLA Ops:
  0.6 7.2 %summaries.1 = (bf16[8,528,128]{2,1,0:T(8,128)(2,1)}, s32[65]{0:T(128)}, s32[65]{0:T(128)}) custom-call(s32[32]{0:T(128)} %len_ref.1, s32[8]{0:T(128)} %home_ref.9, f32[4]{0:T(128)} %rate_ref.15, bf16[2048,512]{1,0:T(8,128)(2,1)} %k_ref.7, bf16[2048,512]{1,0:T(8,128)(2,1)} %v_ref.7), custom_call_target="tpu_custom_call" | custom-call | tf_op jit(solution)/shard_map/summaries/pallas_call | solution.py:294
  7.8 0.0 copy-start
  7.8 0.0 copy-start.2
  7.8 34.5 %all_to_all.20.in_ref = bf16[8,528,128]{2,1,0:T(8,128)(2,1)S(1)} all-to-all(bf16[8,528,128]{2,1,0:T(8,128)(2,1)} %get-tuple-element.16), channel_id=1, replica_groups=mesh['seq'=8,'head'=4] {'seq'}, dimensions={0} | all-to-all | bytes 2162688 | tf_op jit(solution)/shard_map/all_to_all | solution.py:255
  42.4 0.1 reshape.76
  42.5 0.1 select_reduce_fusion.order_ref
  42.6 0.0 copy-done
  42.6 0.0 copy-done.2
  42.6 0.0 copy-start.5
  42.6 0.0 copy-start.1
  42.6 2.7 %scan.2 = bf16[8,512,128]{2,1,0:T(8,128)(2,1)} custom-call(s32[65]{0:T(128)S(1)} %copy-done.2, s32[64]{0:T(128)S(1)} %select_reduce_fusion.order_ref, f32[4]{0:T(128)S(1)} %copy-done, bf16[8,528,128]{2,1,0:T(8,128)(2,1)S(1)} %all_to_all.20.in_ref), custom_call_target="tpu_custom_call" | custom-call | tf_op jit(solution)/shard_map/scan/pallas_call | solution.py:323
  45.3 3.6 %all-to-all-start.1 = ((bf16[8,512,128]{2,1,0:T(8,128)(2,1)}), bf16[8,512,128]{2,1,0:T(8,128)(2,1)S(1)}, u32[]{:S(2)}, u32[]{:S(2)}) async-start(bf16[8,512,128]{2,1,0:T(8,128)(2,1)} %scan.2), calls=%async_computation.1 | async-start | bytes 2097152 | tf_op jit(solution)/shard_map/all_to_all | solution.py:255
  48.8 0.0 copy-done.5
  48.8 0.1 copy.14
  48.9 0.1 reduce-window.8
  49.0 0.1 reduce
  49.1 0.0 copy-done.1
  49.1 0.1 iota_add_fusion
  49.2 0.1 convert_reduce_fusion
  49.3 0.0 copy-start.3
  49.3 9.2 %inner.1.inner_ref = bf16[2048,512]{1,0:T(8,128)(2,1)} custom-call(f32[4]{0:T(128)S(1)} %copy-done, f32[8,1,256]{2,1,0:T(1,128)S(1)} %reshape.72.seg_ref, bf16[2048,512]{1,0:T(8,128)(2,1)} %q_ref.7, bf16[2048,512]{1,0:T(8,128)(2,1)} %k_ref.7, bf16[2048,512]{1,0:T(8,128)(2,1)} %v_ref.7), custom_call_target="tpu_custom_call" | custom-call | tf_op jit(solution)/shard_map/inner/pallas_call | solution.py:307
  58.6 15.4 %all-to-all-done.1 = bf16[8,512,128]{2,1,0:T(8,128)(2,1)S(1)} async-done(((bf16[8,512,128]{2,1,0:T(8,128)(2,1)}), bf16[8,512,128]{2,1,0:T(8,128)(2,1)S(1)}, u32[]{:S(2)}, u32[]{:S(2)}) %all-to-all-start.1) | async-done | bytes 1048608 | tf_op jit(solution)/shard_map/all_to_all | solution.py:255
  74.0 0.0 copy-done.3
  74.0 7.5 %output.1 = (bf16[2048,512]{1,0:T(8,128)(2,1)}, f32[8,2,256]{2,1,0:T(2,128)S(1)}) custom-call(s32[65]{0:T(128)S(1)} %copy-done.2, s32[8]{0:T(128)S(1)} %copy-done.1, f32[4]{0:T(128)S(1)} %copy-done, f32[1,512]{1,0:T(1,128)S(1)} %bitcast.9, bf16[2048,512]{1,0:T(8,128)(2,1)} %q_ref.7, bf16[2048,512]{1,0:T(8,128)(2,1)} %u_ref.3, ...), custom_call_target="tpu_custom_call" | custom-call | tf_op jit(solution)/shard_map/output/pallas_call | solution.py:335
  81.5 5.2 %all-gather = f32[32,2,256]{2,1,0:T(2,128)S(1)} all-gather(f32[8,2,256]{2,1,0:T(2,128)S(1)} %get-tuple-element.17), channel_id=2, replica_groups=mesh['seq'=8,'head'=4] {'head'}, dimensions={0}, use_global_device_ids=true | all-gather | bytes 81920 | tf_op jit(solution)/shard_map/all_gather | solution.py:346
  86.8 7.7 %cotangent.1 = (bf16[2048,512]{1,0:T(8,128)(2,1)}, bf16[8,512,128]{2,1,0:T(8,128)(2,1)S(1)}) custom-call(s32[65]{0:T(128)S(1)} %copy-done.2, s32[8]{0:T(128)S(1)} %copy-done.1, f32[4]{0:T(128)S(1)} %copy-done, f32[1,512]{1,0:T(1,128)S(1)} %bitcast.10, f32[4,8,2,256]{3,2,1,0:T(2,128)S(1)} %bitcast.8, bf16[2048,512]{1,0:T(8,128)(2,1)} %q_ref.7, ...), custom_call_target="tpu_custom_call" | custom-call | tf_op jit(solution)/shard_map/cotangent/pallas_call | solution.py:348
  94.5 29.4 %all_to_all.21.in_ref = bf16[8,512,128]{2,1,0:T(8,128)(2,1)S(1)} all-to-all(bf16[8,512,128]{2,1,0:T(8,128)(2,1)S(1)} %get-tuple-element.22), channel_id=1, replica_groups=mesh['seq'=8,'head'=4] {'seq'}, dimensions={0} | all-to-all | bytes 2097152 | tf_op jit(solution)/shard_map/all_to_all | solution.py:255
  123.9 2.6 %scan.3 = bf16[8,512,128]{2,1,0:T(8,128)(2,1)} custom-call(s32[65]{0:T(128)S(1)} %copy-done.2, s32[64]{0:T(128)S(1)} %select_reduce_fusion.order_ref, f32[4]{0:T(128)S(1)} %copy-done, bf16[8,512,128]{2,1,0:T(8,128)(2,1)S(1)} %all_to_all.21.in_ref), custom_call_target="tpu_custom_call" | custom-call | tf_op jit(solution)/shard_map/scan/pallas_call | solution.py:323
  126.5 3.6 %all-to-all-start.3 = ((bf16[8,512,128]{2,1,0:T(8,128)(2,1)}), bf16[8,512,128]{2,1,0:T(8,128)(2,1)S(1)}, u32[]{:S(2)}, u32[]{:S(2)}) async-start(bf16[8,512,128]{2,1,0:T(8,128)(2,1)} %scan.3), calls=%async_computation.3 | async-start | bytes 2097152 | tf_op jit(solution)/shard_map/all_to_all | solution.py:255
  130.1 0.0 copy-start.4
  130.1 14.4 %inner_grads.1 = (bf16[2048,512]{1,0:T(8,128)(2,1)}, bf16[2048,512]{1,0:T(8,128)(2,1)}, bf16[2048,512]{1,0:T(8,128)(2,1)}) custom-call(s32[65]{0:T(128)S(1)} %copy-done.2, s32[8]{0:T(128)S(1)} %copy-done.1, f32[4]{0:T(128)S(1)} %copy-done, f32[8,1,256]{2,1,0:T(1,128)S(1)} %reshape.72.seg_ref, bf16[2048,512]{1,0:T(8,128)(2,1)} %q_ref.7, ...), custom_call_target="tpu_custom_call" | custom-call | tf_op jit(solution)/shard_map/inner_grads/pallas_call | solution.py:365
  144.5 11.5 %all-to-all-done.3 = bf16[8,512,128]{2,1,0:T(8,128)(2,1)S(1)} async-done(((bf16[8,512,128]{2,1,0:T(8,128)(2,1)}), bf16[8,512,128]{2,1,0:T(8,128)(2,1)S(1)}, u32[]{:S(2)}, u32[]{:S(2)}) %all-to-all-start.3) | async-done | bytes 1048608 | tf_op jit(solution)/shard_map/all_to_all | solution.py:255
  155.9 0.0 copy-done.4
  155.9 8.5 %outer_grads.1 = (bf16[2048,512]{1,0:T(8,128)(2,1)}, bf16[2048,512]{1,0:T(8,128)(2,1)}) custom-call(s32[65]{0:T(128)S(1)} %copy-done.4, s32[8]{0:T(128)S(1)} %copy-done.1, f32[4]{0:T(128)S(1)} %copy-done, bf16[2048,512]{1,0:T(8,128)(2,1)} %k_ref.7, bf16[2048,512]{1,0:T(8,128)(2,1)} %v_ref.7, bf16[8,8,64,128]{3,2,1,0:T(8,128)(2,1)S(1)} %bitcast.7, ...), custom_call_target="tpu_custom_call" | custom-call | tf_op jit(solution)/shard_map/outer_grads/pallas_call | solution.py:378
  (3 shorter events, 0.0 us)
Async XLA Ops:
  7.8 34.8 %copy-start = (f32[4]{0:T(128)S(1)}, f32[4]{0:T(128)}, u32[]{:S(2)}) copy-start(f32[4]{0:T(128)} %rate_ref.15) | copy-start | bytes 52
  7.8 34.7 %copy-start.2 = (s32[65]{0:T(128)S(1)}, s32[65]{0:T(128)}, u32[]{:S(2)}) copy-start(s32[65]{0:T(128)} %get-tuple-element.15.first_ref) | copy-start | bytes 784
  42.6 6.2 %copy-start.5 = (s32[32]{0:T(128)S(1)}, s32[32]{0:T(128)}, u32[]{:S(2)}) copy-start(s32[32]{0:T(128)} %len_ref.1) | copy-start | bytes 388
  42.6 6.5 %copy-start.1 = (s32[8]{0:T(128)S(1)}, s32[8]{0:T(128)}, u32[]{:S(2)}) copy-start(s32[8]{0:T(128)} %home_ref.9) | copy-start | bytes 100
  45.3 28.7 %all-to-all-start.1 = ((bf16[8,512,128]{2,1,0:T(8,128)(2,1)}), bf16[8,512,128]{2,1,0:T(8,128)(2,1)S(1)}, u32[]{:S(2)}, u32[]{:S(2)}) async-start(bf16[8,512,128]{2,1,0:T(8,128)(2,1)} %scan.2), calls=%async_computation.1 | async-start | bytes 2097152 | tf_op jit(solution)/shard_map/all_to_all | solution.py:255
  49.3 24.7 %copy-start.3 = (f32[512]{0:T(512)S(1)}, f32[512]{0:T(512)}, u32[]{:S(2)}) copy-start(f32[512]{0:T(512)} %param.12) | copy-start | bytes 6148
  126.5 29.5 %all-to-all-start.3 = ((bf16[8,512,128]{2,1,0:T(8,128)(2,1)}), bf16[8,512,128]{2,1,0:T(8,128)(2,1)S(1)}, u32[]{:S(2)}, u32[]{:S(2)}) async-start(bf16[8,512,128]{2,1,0:T(8,128)(2,1)} %scan.3), calls=%async_computation.3 | async-start | bytes 2097152 | tf_op jit(solution)/shard_map/all_to_all | solution.py:255
  130.1 25.8 %copy-start.4 = (s32[65]{0:T(128)S(1)}, s32[65]{0:T(128)}, u32[]{:S(2)}) copy-start(s32[65]{0:T(128)} %get-tuple-element.21.last_ref) | copy-start | bytes 784

commit v4 on v3

v4 whole, which is shorter than its diff:
```python
import functools

import jax
import jax.numpy as jnp
from jax import lax
from jax.experimental import pallas as pl
from jax.experimental.pallas import tpu as pltpu
from jax.sharding import PartitionSpec as P

HEAD_SIZE = 128
LANES = 128
EPSILON = 1e-06
LIMIT = 60
HANDOFF = 54
RECEIVE = 40
LASTING = 52
TAIL = 16
F32 = jnp.float32
BF16 = jnp.bfloat16


def dot(a, b, ca, cb):
    return lax.dot_general(a, b, (((ca,), (cb,)), ((), ())), preferred_element_type=F32)


def head_cols(h):
    return slice(h * HEAD_SIZE, (h + 1) * HEAD_SIZE)


def token_index(span):
    return lax.broadcasted_iota(jnp.int32, (span, LANES), 0)


def key_table(rate, span):
    return jnp.exp(-rate * (span - 1.0 - token_index(span).astype(F32)))


def query_table(rate, span):
    return jnp.exp(-rate * (token_index(span).astype(F32) + 1.0))


def row_to_cols(row, width):
    cols = jnp.transpose(jnp.broadcast_to(row, (LANES, row.shape[1])))
    return jnp.concatenate([cols] * (width // LANES), axis=1) if width > LANES else cols


def cols_to_row(cols):
    return jnp.sum(jnp.transpose(cols), axis=0, keepdims=True)


def fill_tables(len_ref, first_ref, last_ref, span):
    spans = first_ref.shape[0] - 1
    far = jnp.int32(spans * span)

    def reset(c, carry):
        first_ref[c] = far
        last_ref[c] = 0
        return carry

    def note(d, end):
        end = end + len_ref[d]
        c = lax.shift_right_logical(end, span.bit_length() - 1) if span & (span - 1) == 0 else end // span
        inside = end - c * span
        last_ref[c] = inside
        first_ref[c] = jnp.minimum(first_ref[c], inside)
        return end

    lax.fori_loop(0, spans + 1, reset, 0, unroll=8)
    lax.fori_loop(0, len_ref.shape[0], note, jnp.int32(0), unroll=4)
    first_ref[0] = 0


def tokens_at(i, span):
    return pl.ds(pl.multiple_of(i * span, span), span)


def rows_at(i, rows):
    return pl.ds(pl.multiple_of(i * rows, rows), rows)


def put_state(ref, i, h, rows, value):
    chunks = HEAD_SIZE // rows
    for part in range(chunks):
        ref[h * chunks + part, rows_at(i, rows), :] = value[part * rows : (part + 1) * rows]


def get_state(ref, i, h, rows):
    chunks = HEAD_SIZE // rows
    return ref[h * chunks : (h + 1) * chunks, rows_at(i, rows), :].reshape(HEAD_SIZE, HEAD_SIZE)


def span_copies(i, span, sources, targets, sem):
    at = tokens_at(i, span)
    return [
        pltpu.make_async_copy(source.at[at], target.at[at], sem.at[a, i])
        for a, (source, target) in enumerate(zip(sources, targets))
    ]


def start_all(copies):
    for copy in copies:
        copy.start()


def wait_all(copies):
    for copy in copies:
        copy.wait()


def each_span(slots, body):
    def turn(i, carry):
        body(i)
        return carry

    lax.fori_loop(0, slots, turn, 0)


def summary_kernel(
    heads, rows, span, len_ref, home_ref, rate_ref, k_hbm, v_hbm,
    sent_hbm, first_ref, last_ref, k_ref, v_ref, table, packed, sem, out_sem,
):
    slots = home_ref.shape[0]
    load = lambda i: span_copies(i, span, (k_hbm, v_hbm), (k_ref, v_ref), sem)

    def store(i):
        at = rows_at(i, rows)
        return pltpu.make_async_copy(packed.at[:, at], sent_hbm.at[:, at], out_sem.at[i])

    for i in range(slots):
        start_all(load(i))
    fill_tables(len_ref, first_ref, last_ref, span)
    for h in range(heads):
        table[h] = key_table(rate_ref[h], span)
    tail = jnp.zeros((TAIL, LANES), F32)
    lane = lax.broadcasted_iota(jnp.int32, (TAIL, LANES), 1)
    for i in range(slots):
        tail = jnp.where(lane == i, home_ref[i].astype(F32), tail)
    for d in range(packed.shape[0]):
        packed[d, slots * rows :, :] = tail.astype(BF16)
    at = pl.ds(slots * rows, TAIL)
    ending = pltpu.make_async_copy(packed.at[:, at], sent_hbm.at[:, at], out_sem.at[slots])
    ending.start()

    def body(i):
        wait_all(load(i))
        at = tokens_at(i, span)
        live = token_index(span) >= last_ref[home_ref[i]]
        for h in range(heads):
            cols = head_cols(h)
            side = jnp.where(live, table[h], 0.0)
            weighted = (side * v_ref[at, cols].astype(F32)).astype(BF16)
            put_state(packed, i, h, rows, dot(k_ref[at, cols], weighted, 0, 0).astype(BF16))
        store(i).start()

    each_span(slots, body)
    for i in range(slots):
        store(i).wait()
    ending.wait()


def scan_kernel(rows, span, reverse, first_ref, order_ref, rate_ref, in_ref, out_hbm, states, sem):
    slots = states.shape[1] // rows
    spans = order_ref.shape[0]
    head = (lax.axis_index("seq") * rows) // HEAD_SIZE
    factor = jnp.exp(jnp.full((8, LANES), -rate_ref[head] * span, F32))[0:1]

    def body(i, state):
        c = spans - 1 - i if reverse else i
        place = order_ref[c]
        device, slot = place // slots, place % slots
        at = rows_at(slot, rows)
        states[device, at, :] = state.astype(BF16)
        carried = jnp.where(first_ref[c] >= span, factor * state, 0.0)
        return carried + in_ref[device, at, :].astype(F32)

    lax.fori_loop(0, spans, body, jnp.zeros((rows, LANES), F32), unroll=4)
    done = pltpu.make_async_copy(states, out_hbm, sem)
    done.start()
    done.wait()


def fill_decay(decay, rate_ref, heads, span):
    j = lax.broadcasted_iota(jnp.int32, (span, span), 0)
    l = lax.broadcasted_iota(jnp.int32, (span, span), 1)
    spread = (j - l).astype(F32)
    for h in range(heads):
        decay[h] = jnp.where(
            spread >= 0.0, jnp.exp(-rate_ref[h] * jnp.maximum(spread, 0.0)), 0.0
        )


def local_kernel(
    heads, span, rate_ref, seg_ref, q_hbm, k_hbm, v_hbm, out_hbm,
    q_ref, k_ref, v_ref, out_ref, decay, sem, out_sem,
):
    slots = seg_ref.shape[0]
    load = lambda i: span_copies(i, span, (q_hbm, k_hbm, v_hbm), (q_ref, k_ref, v_ref), sem)
    store = lambda i: span_copies(i, span, (out_ref,), (out_hbm,), out_sem)
    for i in range(slots):
        start_all(load(i))
    fill_decay(decay, rate_ref, heads, span)

    def body(i):
        wait_all(load(i))
        at = tokens_at(i, span)
        seg = seg_ref[i]
        same = row_to_cols(seg, span) == seg
        for h in range(heads):
            cols = head_cols(h)
            scores = dot(q_ref[at, cols], k_ref[at, cols], 1, 1)
            mixing = (scores * jnp.where(same, decay[h], 0.0)).astype(BF16)
            out_ref[at, cols] = dot(mixing, v_ref[at, cols], 1, 0).astype(BF16)
        start_all(store(i))

    each_span(slots, body)
    for i in range(slots):
        wait_all(store(i))


def output_kernel(
    heads, rows, span, first_ref, home_ref, rate_ref, gain_ref, q_hbm, u_hbm, inner_hbm, prev_ref,
    out_ref, q_ref, u_ref, sums_ref, inner_ref, table, sem,
):
    slots = home_ref.shape[0]
    load = lambda i: span_copies(i, span, (q_hbm, u_hbm, inner_hbm), (q_ref, u_ref, inner_ref), sem)
    for i in range(slots):
        start_all(load(i))
    for h in range(heads):
        table[h] = query_table(rate_ref[h], span)

    def body(i):
        wait_all(load(i))
        at = tokens_at(i, span)
        live = token_index(span) < first_ref[home_ref[i]]
        squares = jnp.zeros((span, LANES), F32)
        crossed = jnp.zeros((span, LANES), F32)
        for h in range(heads):
            cols = head_cols(h)
            outer = dot(q_ref[at, cols], get_state(prev_ref, i, h, rows), 1, 0)
            attn = inner_ref[at, cols].astype(F32) + jnp.where(live, table[h], 0.0) * outer
            out_ref[at, cols] = attn
            squares += attn * attn
            crossed += gain_ref[:, cols] * u_ref[at, cols].astype(F32) * attn
        sums_ref[i, 0:1, :] = cols_to_row(squares)
        sums_ref[i, 1:2, :] = cols_to_row(crossed)

    each_span(slots, body)


def cotangent_kernel(
    heads, rows, span, channels, first_ref, home_ref, rate_ref, gain_ref, sums_ref, q_ref, u_ref, attn_ref,
    g_hbm, sent_hbm, g_ref, table, packed, g_sem, out_sem,
):
    slots = home_ref.shape[0]
    save = lambda i: span_copies(i, span, (g_ref,), (g_hbm,), g_sem)
    for h in range(heads):
        table[h] = query_table(rate_ref[h], span)

    def store(i):
        at = rows_at(i, rows)
        return pltpu.make_async_copy(packed.at[:, at], sent_hbm.at[:, at], out_sem.at[i])

    def body(i):
        at = tokens_at(i, span)
        total = jnp.sum(sums_ref[:, i], axis=0)
        scaling = 1.0 / jnp.sqrt(total[0:1] / channels + EPSILON)
        pulled = total[1:2] / channels
        direct = row_to_cols(scaling, LANES)
        along = row_to_cols(scaling * scaling * scaling * pulled, LANES)
        live = token_index(span) < first_ref[home_ref[i]]
        for h in range(heads):
            cols = head_cols(h)
            grad = direct * gain_ref[:, cols] * u_ref[at, cols].astype(F32) - along * attn_ref[at, cols]
            grad = grad.astype(BF16)
            g_ref[at, cols] = grad
            weighted = (jnp.where(live, table[h], 0.0) * grad.astype(F32)).astype(BF16)
            put_state(packed, i, h, rows, dot(q_ref[at, cols], weighted, 0, 0).astype(BF16))
        store(i).start()
        start_all(save(i))

    each_span(slots, body)
    for i in range(slots):
        store(i).wait()
        wait_all(save(i))


def inner_grads_kernel(
    heads, rows, span, first_ref, home_ref, rate_ref, seg_ref, q_hbm, k_hbm, v_hbm, g_hbm, prev_ref,
    dq_hbm, dk_hbm, dv_hbm, q_ref, k_ref, v_ref, g_ref, dq_ref, dk_ref, dv_ref, decay, table, sem, out_sem,
):
    slots = home_ref.shape[0]
    load = lambda i: span_copies(
        i, span, (q_hbm, k_hbm, v_hbm, g_hbm), (q_ref, k_ref, v_ref, g_ref), sem
    )
    store = lambda i: span_copies(i, span, (dq_ref, dk_ref, dv_ref), (dq_hbm, dk_hbm, dv_hbm), out_sem)
    for i in range(slots):
        start_all(load(i))
    fill_decay(decay, rate_ref, heads, span)
    for h in range(heads):
        table[h] = query_table(rate_ref[h], span)

    def body(i):
        wait_all(load(i))
        at = tokens_at(i, span)
        seg = seg_ref[i]
        same = row_to_cols(seg, span) == seg
        live = token_index(span) < first_ref[home_ref[i]]
        for h in range(heads):
            cols = head_cols(h)
            q, k, v, g = q_ref[at, cols], k_ref[at, cols], v_ref[at, cols], g_ref[at, cols]
            mask = jnp.where(same, decay[h], 0.0)
            mixing = (dot(q, k, 1, 1) * mask).astype(BF16)
            score_grad = (dot(g, v, 1, 1) * mask).astype(BF16)
            outer = dot(g, get_state(prev_ref, i, h, rows), 1, 1)
            dq = dot(score_grad, k, 1, 0) + jnp.where(live, table[h], 0.0) * outer
            dq_ref[at, cols] = dq.astype(BF16)
            dk_ref[at, cols] = dot(score_grad, q, 0, 0).astype(BF16)
            dv_ref[at, cols] = dot(mixing, g, 0, 0).astype(BF16)
        start_all(store(i))

    each_span(slots, body)
    for i in range(slots):
        wait_all(store(i))


def outer_grads_kernel(
    heads, rows, span, last_ref, home_ref, rate_ref, k_hbm, v_hbm, after_ref, dk_part, dv_part,
    dk_hbm, dv_hbm, k_ref, v_ref, dk_in, dv_in, dk_ref, dv_ref, table, sem, out_sem,
):
    slots = home_ref.shape[0]
    load = lambda i: span_copies(
        i, span, (k_hbm, v_hbm, dk_part, dv_part), (k_ref, v_ref, dk_in, dv_in), sem
    )
    store = lambda i: span_copies(i, span, (dk_ref, dv_ref), (dk_hbm, dv_hbm), out_sem)
    for i in range(slots):
        start_all(load(i))
    for h in range(heads):
        table[h] = key_table(rate_ref[h], span)

    def body(i):
        wait_all(load(i))
        at = tokens_at(i, span)
        live = token_index(span) >= last_ref[home_ref[i]]
        for h in range(heads):
            cols = head_cols(h)
            side = jnp.where(live, table[h], 0.0)
            after = get_state(after_ref, i, h, rows)
            dk = dk_in[at, cols].astype(F32) + side * dot(v_ref[at, cols], after, 1, 1)
            dv = dv_in[at, cols].astype(F32) + side * dot(k_ref[at, cols], after, 1, 0)
            dk_ref[at, cols] = dk.astype(BF16)
            dv_ref[at, cols] = dv.astype(BF16)
        start_all(store(i))

    each_span(slots, body)
    for i in range(slots):
        wait_all(store(i))


def exchange(blocks):
    return lax.all_to_all(blocks, "seq", split_axis=0, concat_axis=0, tiled=True)


def shards(query, key, value, upstream, norm_gain, decay_rate, document_lengths, group_home):
    devices = lax.axis_size("seq")
    tokens, width = query.shape
    heads = width // HEAD_SIZE
    slots = group_home.shape[0]
    span = tokens // slots
    spans = slots * devices
    rows = width // devices
    channels = width * lax.axis_size("head")

    doc_ends = jnp.cumsum(document_lengths)
    positions = (group_home * span)[:, None] + jnp.arange(span, dtype=jnp.int32)[None, :]
    seg = jnp.sum((doc_ends <= positions[..., None]).astype(F32), axis=-1).reshape(slots, 1, span)
    gain = norm_gain.reshape(1, width)

    smem = pl.BlockSpec(memory_space=pltpu.SMEM)
    vmem = pl.BlockSpec(memory_space=pltpu.VMEM)
    hbm = pl.BlockSpec(memory_space=pl.ANY)
    table = pltpu.VMEM((heads, span, LANES), F32)
    decay = pltpu.VMEM((heads, span, span), F32)
    packed = (devices, slots * rows + TAIL, LANES)
    plain = (devices, slots * rows, LANES)
    token_bf16 = pltpu.VMEM((tokens, width), BF16)
    token_f32 = pltpu.VMEM((tokens, width), F32)
    per_slot = pltpu.SemaphoreType.DMA((slots,))

    def sems(count):
        return pltpu.SemaphoreType.DMA((count, slots))

    def shaped(shape, dtype):
        return jax.ShapeDtypeStruct(shape, dtype)

    def call(kernel, name, limit, flops, in_specs, out_specs, out_shape, scratch, *static):
        return pl.pallas_call(
            functools.partial(kernel, *static),
            in_specs=in_specs,
            out_specs=out_specs,
            out_shape=out_shape,
            scratch_shapes=scratch,
            compiler_params=pltpu.CompilerParams(vmem_limit_bytes=limit << 20),
            cost_estimate=pl.CostEstimate(flops=flops, bytes_accessed=0, transcendentals=0),
            name=name,
        )

    work = 2 * tokens * width * span
    spans_table = shaped((spans + 1,), jnp.int32)
    sent, first, last = call(
        summary_kernel, "summaries", 60, work // 2,
        [smem, smem, smem, hbm, hbm],
        [hbm, smem, smem],
        [shaped(packed, BF16), spans_table, spans_table],
        [token_bf16] * 2 + [table, pltpu.VMEM(packed, BF16), sems(2), pltpu.SemaphoreType.DMA((slots + 1,))],
        heads, rows, span,
    )(document_lengths, group_home, decay_rate, key, value)

    arrived = exchange(sent)

    inner = call(
        local_kernel, "inner", LIMIT, 2 * work,
        [smem, vmem, hbm, hbm, hbm],
        hbm,
        shaped((tokens, width), BF16),
        [token_bf16] * 4 + [decay, sems(3), sems(1)],
        heads, span,
    )(decay_rate, seg, query, key, value)

    homes = arrived[:, slots * rows, :slots].astype(jnp.int32).reshape(-1)
    hits = homes[None, :] == jnp.arange(spans, dtype=jnp.int32)[:, None]
    order = jnp.sum(jnp.where(hits, jnp.arange(spans, dtype=jnp.int32)[None, :], 0), axis=1)

    def scan(blocks, reverse):
        return call(
            scan_kernel, "scan", 8, work // 8,
            [smem, smem, smem, vmem],
            hbm,
            shaped(plain, BF16),
            [pltpu.VMEM(plain, BF16), pltpu.SemaphoreType.DMA],
            rows, span, reverse,
        )(first, order, decay_rate, blocks)

    prev = exchange(scan(arrived, False))

    attn, query_v, upstream_v, sums = call(
        output_kernel, "output", HANDOFF, work // 2,
        [smem, smem, smem, vmem, hbm, hbm, hbm, vmem],
        [vmem] * 4,
        [token_f32, token_bf16, token_bf16, shaped((slots, 2, span), F32)],
        [token_bf16, table, sems(3)],
        heads, rows, span,
    )(first, group_home, decay_rate, gain, query, upstream, inner, prev)

    sums = lax.all_gather(sums, "head")

    grad_in, rev_sent = call(
        cotangent_kernel, "cotangent", RECEIVE, work // 2,
        [smem, smem, smem, vmem, vmem, vmem, vmem, vmem],
        [hbm, hbm],
        [shaped((tokens, width), BF16), shaped(plain, BF16)],
        [token_bf16, table, pltpu.VMEM(plain, BF16), sems(1), per_slot],
        heads, rows, span, channels,
    )(first, group_home, decay_rate, gain, sums, query_v, upstream_v, attn)

    rev_arrived = exchange(rev_sent)

    query_grad, key_inner, value_inner = call(
        inner_grads_kernel, "inner_grads", LASTING, 6 * work,
        [smem, smem, smem, vmem, hbm, hbm, hbm, hbm, vmem],
        [hbm] * 3,
        [shaped((tokens, width), BF16)] * 3,
        [token_bf16] * 7 + [decay, table, sems(4), sems(3)],
        heads, rows, span,
    )(first, group_home, decay_rate, seg, query, key, value, grad_in, prev)

    after = exchange(scan(rev_arrived, True))

    key_grad, value_grad = call(
        outer_grads_kernel, "outer_grads", LASTING, work,
        [smem, smem, smem, hbm, hbm, vmem, hbm, hbm],
        [hbm, hbm],
        [shaped((tokens, width), BF16)] * 2,
        [token_bf16] * 6 + [table, sems(4), sems(2)],
        heads, rows, span,
    )(last, group_home, decay_rate, key, value, after, key_inner, value_inner)
    return query_grad, key_grad, value_grad


def solution(mesh):
    in_specs = (
        P("seq", "head"),
        P("seq", "head"),
        P("seq", "head"),
        P("seq", "head"),
        P("head"),
        P("head"),
        P(),
        P("seq"),
    )
    out_specs = (P("seq", "head"), P("seq", "head"), P("seq", "head"))
    return jax.shard_map(shards, mesh=mesh, in_specs=in_specs, out_specs=out_specs, check_vma=False)
```

time: 166 us -> 157 us (0.946)
  Pallas kernels: 59.8 us -> 50.1 us
    pallas_call x8, Pallas kernels: 59.8 us -> 50.1 us  [the longest x1 14.6 us: shards(): call(inner_grads_kernel, 'inner_grads', LASTING, 6 * work, [smem, smem, s...]
  transfers between devices with their start and end apart: 2 -> 2, of which waited for: 2 -> 2; matrix products, arithmetic and copies ran while one was open for 0% -> 1% of each run, Pallas kernels for 14% -> 15%
where the time goes in v4:
time: 157 us
  blocking collectives  69.4 us (44%)
  Pallas kernels  50.1 us (32%)
  waiting for transfers between devices  27.1 us (17%)
  starting transfers between devices  7.22 us (5%)
  local copies, waits for them, and re-layouts  1.79 us (1%)
    all_to_all x2, blocking collectives, exchange(): lax.all_to_all(blocks, 'seq', split_axis=0, concat_axis=0, tiled=True)  63.9 us
    all_to_all x2, waiting for transfers between devices, exchange(): lax.all_to_all(blocks, 'seq', split_axis=0, concat_axis=0, tiled=True)  27.1 us
    pallas_call x1, Pallas kernels, shards(): call(inner_grads_kernel, 'inner_grads', LASTING, 6 * work, [smem, smem, s...  14.6 us
    pallas_call x1, Pallas kernels, shards(): call(local_kernel, 'inner', LIMIT, 2 * work, [smem, vmem, hbm, hbm, hbm],...  8.14 us
    all_to_all x2, starting transfers between devices, exchange(): lax.all_to_all(blocks, 'seq', split_axis=0, concat_axis=0, tiled=True)  7.22 us
    pallas_call x1, Pallas kernels, shards(): call(output_kernel, 'output', HANDOFF, work // 2, [smem, smem, smem, vmem...  6.42 us
    pallas_call x1, Pallas kernels, shards(): call(outer_grads_kernel, 'outer_grads', LASTING, work, [smem, smem, smem,...  6.37 us
    all_gather x1, blocking collectives, shards(): sums = lax.all_gather(sums, 'head')  5.45 us
  transfers between devices with their start and end apart: 2, of which 2 were waited for; matrix products, arithmetic and copies ran while one was open for 1% of the time, Pallas kernels for 15%

profile of v4, /device:TPU:0, one launch (start us, length us, event | category | flops | bytes accessed | tf_op | source)
XLA Modules:
  0.0 156.9 jit_solution(11067293555696049469)
XLA Ops:
  0.6 5.4 %summaries.1 = (bf16[8,528,128]{2,1,0:T(8,128)(2,1)}, s32[65]{0:T(128)}, s32[65]{0:T(128)}) custom-call(s32[32]{0:T(128)} %len_ref.1, s32[8]{0:T(128)} %home_ref.9, f32[4]{0:T(128)} %rate_ref.15, bf16[2048,512]{1,0:T(8,128)(2,1)} %k_hbm.7, bf16[2048,512]{1,0:T(8,128)(2,1)} %v_hbm.7), custom_call_target="tpu_custom_call" | custom-call | flops 268435456 | tf_op jit(solution)/shard_map/summaries/pallas_call | solution.py:409
  6.0 0.0 copy-start.3
  6.0 0.0 copy-start.8
  6.0 34.5 %all_to_all.20.in_ref = bf16[8,528,128]{2,1,0:T(8,128)(2,1)S(1)} all-to-all(bf16[8,528,128]{2,1,0:T(8,128)(2,1)} %get-tuple-element.18), channel_id=1, replica_groups=mesh['seq'=8,'head'=4] {'seq'}, dimensions={0} | all-to-all | bytes 2162688 | tf_op jit(solution)/shard_map/all_to_all | solution.py:360
  40.5 0.1 reshape.68
  40.6 0.1 select_reduce_fusion.order_ref
  40.7 0.0 copy-done.3
  40.7 0.0 copy-done.8
  40.8 0.0 copy-start.12
  40.8 0.0 copy-start.6
  40.8 2.2 %scan.2 = bf16[8,512,128]{2,1,0:T(8,128)(2,1)} custom-call(s32[65]{0:T(128)S(1)} %copy-done.8, s32[64]{0:T(128)S(1)} %select_reduce_fusion.order_ref, f32[4]{0:T(128)S(1)} %copy-done.3, bf16[8,528,128]{2,1,0:T(8,128)(2,1)S(1)} %all_to_all.20.in_ref), custom_call_target="tpu_custom_call" | custom-call | flops 67108864 | tf_op jit(solution)/shard_map/scan/pallas_call | solution.py:434
  43.0 3.6 %all-to-all-start.1 = ((bf16[8,512,128]{2,1,0:T(8,128)(2,1)}), bf16[8,512,128]{2,1,0:T(8,128)(2,1)S(1)}, u32[]{:S(2)}, u32[]{:S(2)}) async-start(bf16[8,512,128]{2,1,0:T(8,128)(2,1)} %scan.2), calls=%async_computation.1 | async-start | bytes 2097152 | tf_op jit(solution)/shard_map/all_to_all | solution.py:360
  46.6 0.0 copy-done.12
  46.6 0.1 copy.14
  46.7 0.1 reduce-window.8
  46.7 0.1 reduce
  46.8 0.0 copy-done.6
  46.9 0.1 iota_add_fusion
  46.9 0.1 convert_reduce_fusion
  47.0 0.6 reshape.66.seg_ref
  47.7 8.1 %inner.1.inner_hbm = bf16[2048,512]{1,0:T(8,128)(2,1)} custom-call(f32[4]{0:T(128)} %rate_ref.15, f32[8,1,256]{2,1,0:T(1,128)} %reshape.66.seg_ref, bf16[2048,512]{1,0:T(8,128)(2,1)} %q_hbm.5, bf16[2048,512]{1,0:T(8,128)(2,1)} %k_hbm.7, bf16[2048,512]{1,0:T(8,128)(2,1)} %v_hbm.7), custom_call_target="tpu_custom_call" | custom-call | flops 1073741824 | tf_op jit(solution)/shard_map/inner/pallas_call | solution.py:420
  55.8 15.9 %all-to-all-done.1.prev_ref = bf16[8,512,128]{2,1,0:T(8,128)(2,1)S(1)} async-done(((bf16[8,512,128]{2,1,0:T(8,128)(2,1)}), bf16[8,512,128]{2,1,0:T(8,128)(2,1)S(1)}, u32[]{:S(2)}, u32[]{:S(2)}) %all-to-all-start.1) | async-done | bytes 1048608 | tf_op jit(solution)/shard_map/all_to_all | solution.py:360
  71.7 0.0 copy-start
  71.7 1.0 copy-done
  72.7 0.0 copy-start.4
  72.7 0.0 copy-start.5
  72.7 0.0 copy-start.7
  72.7 0.0 copy-start.9
  72.7 6.4 %output.1 = (f32[2048,512]{1,0:T(8,128)S(1)}, bf16[2048,512]{1,0:T(8,128)(2,1)S(1)}, bf16[2048,512]{1,0:T(8,128)(2,1)S(1)}, f32[8,2,256]{2,1,0:T(2,128)}) custom-call(s32[65]{0:T(128)} %get-tuple-element.17.first_ref, s32[8]{0:T(128)} %home_ref.9, f32[4]{0:T(128)} %rate_ref.15, f32[1,512]{1,0:T(1,128)} %bitcast.4, bf16[2048,512]{1,0:T(8,128)(2,1)} %q_hbm.5, ...), custom_call_target="tpu_custom_call" | custom-call | flops 268435456 | tf_op jit(solution)/shard_map/output/pallas_call | solution.py:445
  79.2 5.4 %all-gather = f32[32,2,256]{2,1,0:T(2,128)S(1)} all-gather(f32[8,2,256]{2,1,0:T(2,128)} %get-tuple-element.19), channel_id=2, replica_groups=mesh['seq'=8,'head'=4] {'head'}, dimensions={0}, use_global_device_ids=true | all-gather | bytes 81920 | tf_op jit(solution)/shard_map/all_gather | solution.py:454
  84.6 0.0 copy-done.4
  84.6 0.0 copy-done.5
  84.6 0.0 copy-done.7
  84.6 0.0 copy-done.9
  84.6 4.8 %cotangent.1 = (bf16[2048,512]{1,0:T(8,128)(2,1)S(1)}, bf16[8,512,128]{2,1,0:T(8,128)(2,1)S(1)}) custom-call(s32[65]{0:T(128)S(1)} %copy-done.9, s32[8]{0:T(128)S(1)} %copy-done.7, f32[4]{0:T(128)S(1)} %copy-done.4, f32[1,512]{1,0:T(1,128)S(1)} %bitcast.5, f32[4,8,2,256]{3,2,1,0:T(2,128)S(1)} %bitcast.3, bf16[2048,512]{1,0:T(8,128)(2,1)S(1)} %get-tuple-element.20.q_ref, ...), custom_call_target="tpu_custom_call" | custom-call | flops 268435456 | tf_op jit(solution)/shard_map/cotangent/pallas_call | solution.py:456
  89.5 0.0 copy-start.11
  89.5 29.4 %all_to_all.21.in_ref = bf16[8,512,128]{2,1,0:T(8,128)(2,1)S(1)} all-to-all(bf16[8,512,128]{2,1,0:T(8,128)(2,1)S(1)} %get-tuple-element.26), channel_id=1, replica_groups=mesh['seq'=8,'head'=4] {'seq'}, dimensions={0} | all-to-all | bytes 2097152 | tf_op jit(solution)/shard_map/all_to_all | solution.py:360
  118.9 0.0 copy-done.11
  118.9 0.0 copy-start.1
  118.9 2.2 %scan.3 = bf16[8,512,128]{2,1,0:T(8,128)(2,1)} custom-call(s32[65]{0:T(128)S(1)} %copy-done.9, s32[64]{0:T(128)S(1)} %select_reduce_fusion.order_ref, f32[4]{0:T(128)S(1)} %copy-done.4, bf16[8,512,128]{2,1,0:T(8,128)(2,1)S(1)} %all_to_all.21.in_ref), custom_call_target="tpu_custom_call" | custom-call | flops 67108864 | tf_op jit(solution)/shard_map/scan/pallas_call | solution.py:434
  121.1 3.6 %all-to-all-start.3 = ((bf16[8,512,128]{2,1,0:T(8,128)(2,1)}), bf16[8,512,128]{2,1,0:T(8,128)(2,1)S(1)}, u32[]{:S(2)}, u32[]{:S(2)}) async-start(bf16[8,512,128]{2,1,0:T(8,128)(2,1)} %scan.3), calls=%async_computation.3 | async-start | bytes 2097152 | tf_op jit(solution)/shard_map/all_to_all | solution.py:360
  124.7 0.0 copy-done.1
  124.7 0.0 copy-done.2
  124.7 0.0 copy-start.10
  124.8 14.6 %inner_grads.1 = (bf16[2048,512]{1,0:T(8,128)(2,1)}, bf16[2048,512]{1,0:T(8,128)(2,1)}, bf16[2048,512]{1,0:T(8,128)(2,1)}) custom-call(s32[65]{0:T(128)S(1)} %copy-done.9, s32[8]{0:T(128)S(1)} %copy-done.7, f32[4]{0:T(128)S(1)} %copy-done.4, f32[8,1,256]{2,1,0:T(1,128)S(1)} %copy-done.2, bf16[2048,512]{1,0:T(8,128)(2,1)} %q_hbm.5, bf16[2048,512]{1,0:T(8,128)(2,1)} %k_hbm.7, ...), custom_call_target="tpu_custom_call" | custom-call | flops 3221225472 | tf_op jit(solution)/shard_map/inner_grads/pallas_call | solution.py:467
  139.4 11.2 %all-to-all-done.3.after_ref = bf16[8,512,128]{2,1,0:T(8,128)(2,1)S(1)} async-done(((bf16[8,512,128]{2,1,0:T(8,128)(2,1)}), bf16[8,512,128]{2,1,0:T(8,128)(2,1)S(1)}, u32[]{:S(2)}, u32[]{:S(2)}) %all-to-all-start.3) | async-done | bytes 1048608 | tf_op jit(solution)/shard_map/all_to_all | solution.py:360
  150.6 0.0 copy-done.10
  150.6 6.4 %outer_grads.1 = (bf16[2048,512]{1,0:T(8,128)(2,1)}, bf16[2048,512]{1,0:T(8,128)(2,1)}) custom-call(s32[65]{0:T(128)S(1)} %copy-done.10, s32[8]{0:T(128)S(1)} %copy-done.7, f32[4]{0:T(128)S(1)} %copy-done.4, bf16[2048,512]{1,0:T(8,128)(2,1)} %k_hbm.7, bf16[2048,512]{1,0:T(8,128)(2,1)} %v_hbm.7, bf16[8,512,128]{2,1,0:T(8,128)(2,1)S(1)} %all-to-all-done.3.after_ref, ...), custom_call_target="tpu_custom_call" | custom-call | flops 536870912 | tf_op jit(solution)/shard_map/outer_grads/pallas_call | solution.py:478
  (3 shorter events, 0.0 us)
Async XLA Ops:
  6.0 34.8 %copy-start.3 = (f32[4]{0:T(128)S(1)}, f32[4]{0:T(128)}, u32[]{:S(2)}) copy-start(f32[4]{0:T(128)} %rate_ref.15) | copy-start | bytes 52
  6.0 34.7 %copy-start.8 = (s32[65]{0:T(128)S(1)}, s32[65]{0:T(128)}, u32[]{:S(2)}) copy-start(s32[65]{0:T(128)} %get-tuple-element.17.first_ref) | copy-start | bytes 784
  40.8 5.8 %copy-start.12 = (s32[32]{0:T(128)S(1)}, s32[32]{0:T(128)}, u32[]{:S(2)}) copy-start(s32[32]{0:T(128)} %len_ref.1) | copy-start | bytes 388
  40.8 6.1 %copy-start.6 = (s32[8]{0:T(128)S(1)}, s32[8]{0:T(128)}, u32[]{:S(2)}) copy-start(s32[8]{0:T(128)} %home_ref.9) | copy-start | bytes 100
  43.0 28.7 %all-to-all-start.1 = ((bf16[8,512,128]{2,1,0:T(8,128)(2,1)}), bf16[8,512,128]{2,1,0:T(8,128)(2,1)S(1)}, u32[]{:S(2)}, u32[]{:S(2)}) async-start(bf16[8,512,128]{2,1,0:T(8,128)(2,1)} %scan.2), calls=%async_computation.1 | async-start | bytes 2097152 | tf_op jit(solution)/shard_map/all_to_all | solution.py:360
  71.7 1.0 copy-start
  72.7 11.9 %copy-start.4 = (f32[4]{0:T(128)S(1)}, f32[4]{0:T(128)}, u32[]{:S(2)}) copy-start(f32[4]{0:T(128)} %rate_ref.15) | copy-start | bytes 52
  72.7 11.9 %copy-start.5 = (f32[512]{0:T(512)S(1)}, f32[512]{0:T(512)}, u32[]{:S(2)}) copy-start(f32[512]{0:T(512)} %param.12) | copy-start | bytes 6148
  72.7 11.9 %copy-start.7 = (s32[8]{0:T(128)S(1)}, s32[8]{0:T(128)}, u32[]{:S(2)}) copy-start(s32[8]{0:T(128)} %home_ref.9) | copy-start | bytes 100
  72.7 11.9 %copy-start.9 = (s32[65]{0:T(128)S(1)}, s32[65]{0:T(128)}, u32[]{:S(2)}) copy-start(s32[65]{0:T(128)} %get-tuple-element.17.first_ref) | copy-start | bytes 784
  89.5 29.4 %copy-start.11 = (bf16[2048,512]{1,0:T(8,128)(2,1)}, bf16[2048,512]{1,0:T(8,128)(2,1)S(1)}, u32[]{:S(2)}) copy-start(bf16[2048,512]{1,0:T(8,128)(2,1)S(1)} %get-tuple-element.23.g_hbm) | copy-start | bytes 6291460
  118.9 5.8 %copy-start.1 = (bf16[8,512,128]{2,1,0:T(8,128)(2,1)S(1)}, bf16[8,512,128]{2,1,0:T(8,128)(2,1)}, u32[]{:S(2)}) copy-start(bf16[8,512,128]{2,1,0:T(8,128)(2,1)} %copy-done) | copy-start | bytes 3145732
  118.9 5.8 %copy-start.2 = (f32[8,1,256]{2,1,0:T(1,128)S(1)}, f32[8,1,256]{2,1,0:T(1,128)}, u32[]{:S(2)}) copy-start(f32[8,1,256]{2,1,0:T(1,128)} %reshape.66.seg_ref) | copy-start | bytes 24580
  121.1 29.5 %all-to-all-start.3 = ((bf16[8,512,128]{2,1,0:T(8,128)(2,1)}), bf16[8,512,128]{2,1,0:T(8,128)(2,1)S(1)}, u32[]{:S(2)}, u32[]{:S(2)}) async-start(bf16[8,512,128]{2,1,0:T(8,128)(2,1)} %scan.3), calls=%async_computation.3 | async-start | bytes 2097152 | tf_op jit(solution)/shard_map/all_to_all | solution.py:360
  124.7 25.8 %copy-start.10 = (s32[65]{0:T(128)S(1)}, s32[65]{0:T(128)}, u32[]{:S(2)}) copy-start(s32[65]{0:T(128)} %get-tuple-element.25.last_ref) | copy-start | bytes 784

commit v5 on v4

v5 whole, which is shorter than its diff:
```python
import functools

import jax
import jax.numpy as jnp
from jax import lax
from jax.experimental import pallas as pl
from jax.experimental.pallas import tpu as pltpu
from jax.sharding import PartitionSpec as P


HEAD_SIZE = 128
LANES = 128
EPSILON = 1e-06
TAIL = 16
LIMIT = 60
ROOMY = 16
HANDOFF = 54
RECEIVE = 40
LASTING = 52
F32 = jnp.float32
BF16 = jnp.bfloat16


def dot(a, b, ca, cb):
    return lax.dot_general(a, b, (((ca,), (cb,)), ((), ())), preferred_element_type=F32)


def head_cols(h):
    return slice(h * HEAD_SIZE, (h + 1) * HEAD_SIZE)


def token_index(span):
    return lax.broadcasted_iota(jnp.int32, (span, LANES), 0)


def fill_key_table(table, rate_ref, base, span):
    for h in range(table.shape[0]):
        table[h] = jnp.exp(-rate_ref[base + h] * (span - 1.0 - token_index(span).astype(F32)))


def fill_query_table(table, rate_ref, base, span):
    for h in range(table.shape[0]):
        table[h] = jnp.exp(-rate_ref[base + h] * (token_index(span).astype(F32) + 1.0))


def fill_decay(decay, rate_ref, base, span):
    j = lax.broadcasted_iota(jnp.int32, (span, span), 0)
    l = lax.broadcasted_iota(jnp.int32, (span, span), 1)
    spread = (j - l).astype(F32)
    for h in range(decay.shape[0]):
        falling = jnp.exp(-rate_ref[base + h] * jnp.maximum(spread, 0.0))
        decay[h] = jnp.where(spread >= 0.0, falling, 0.0)


def row_to_cols(row, width):
    cols = jnp.transpose(jnp.broadcast_to(row, (LANES, row.shape[1])))
    return jnp.concatenate([cols] * (width // LANES), axis=1) if width > LANES else cols


def cols_to_row(cols):
    return jnp.sum(jnp.transpose(cols), axis=0, keepdims=True)


def fill_tables(len_ref, first_ref, last_ref, span):
    spans = first_ref.shape[0] - 1
    far = jnp.int32(spans * span)

    def reset(c, carry):
        first_ref[c] = far
        last_ref[c] = 0
        return carry

    def note(d, end):
        end = end + len_ref[d]
        c = lax.shift_right_logical(end, span.bit_length() - 1) if span & (span - 1) == 0 else end // span
        inside = end - c * span
        last_ref[c] = inside
        first_ref[c] = jnp.minimum(first_ref[c], inside)
        return end

    lax.fori_loop(0, spans + 1, reset, 0, unroll=8)
    lax.fori_loop(0, len_ref.shape[0], note, jnp.int32(0), unroll=4)
    first_ref[0] = 0


def tokens_at(i, span):
    return pl.ds(pl.multiple_of(i * span, span), span)


def rows_at(i, rows):
    return pl.ds(pl.multiple_of(i * rows, rows), rows)


def put_state(ref, i, h, rows, value):
    chunks = HEAD_SIZE // rows
    for part in range(chunks):
        ref[h * chunks + part, rows_at(i, rows), :] = value[part * rows : (part + 1) * rows]


def get_state(ref, i, h, rows):
    chunks = HEAD_SIZE // rows
    return ref[h * chunks : (h + 1) * chunks, rows_at(i, rows), :].reshape(HEAD_SIZE, HEAD_SIZE)


def span_copies(i, span, sources, targets, sem):
    at = tokens_at(i, span)
    return [
        pltpu.make_async_copy(source.at[at], target.at[at], sem.at[a, i])
        for a, (source, target) in enumerate(zip(sources, targets))
    ]


def start_all(copies):
    for copy in copies:
        copy.start()


def wait_all(copies):
    for copy in copies:
        copy.wait()


def each_span(slots, body):
    def turn(i, carry):
        body(i)
        return carry

    lax.fori_loop(0, slots, turn, 0)


def columns(base, heads):
    return pl.ds(base * HEAD_SIZE, heads * HEAD_SIZE)


def to_blocks(packed, blocks, sem):
    me = lax.axis_index("seq")
    return [
        pltpu.make_async_copy(packed.at[jnp.bitwise_xor(me, k)], block, sem.at[k])
        for k, block in enumerate(blocks)
    ]


def from_blocks(blocks, packed, sem):
    me = lax.axis_index("seq")
    return [
        pltpu.make_async_copy(block, packed.at[jnp.bitwise_xor(me, k)], sem.at[k])
        for k, block in enumerate(blocks)
    ]


def summary_kernel(base, heads, rows, span, lead, count, *refs):
    if lead:
        len_ref, home_ref, rate_ref, k_hbm, v_hbm, sent_hbm, first_ref, last_ref = refs[:8]
        refs = refs[8:]
    else:
        last_ref, home_ref, rate_ref, k_hbm, v_hbm = refs[:5]
        blocks, refs = refs[5 : 5 + count], refs[5 + count :]
    k_ref, v_ref, table, packed, sem, out_sem = refs
    slots = home_ref.shape[0]
    part = columns(base, heads)
    sources = (k_hbm.at[:, part], v_hbm.at[:, part])
    load = lambda i: span_copies(i, span, sources, (k_ref, v_ref), sem)
    for i in range(slots):
        start_all(load(i))
    if lead:
        fill_tables(len_ref, first_ref, last_ref, span)
    fill_key_table(table, rate_ref, base, span)
    if lead:
        tail = jnp.zeros((TAIL, LANES), F32)
        lane = lax.broadcasted_iota(jnp.int32, (TAIL, LANES), 1)
        for i in range(slots):
            tail = jnp.where(lane == i, home_ref[i].astype(F32), tail)
        for d in range(packed.shape[0]):
            packed[d, slots * rows :, :] = tail.astype(BF16)

    def body(i):
        wait_all(load(i))
        at = tokens_at(i, span)
        live = token_index(span) >= last_ref[home_ref[i]]
        for h in range(heads):
            cols = head_cols(h)
            side = jnp.where(live, table[h], 0.0)
            weighted = (side * v_ref[at, cols].astype(F32)).astype(BF16)
            put_state(packed, i, h, rows, dot(k_ref[at, cols], weighted, 0, 0).astype(BF16))

    each_span(slots, body)
    out = [pltpu.make_async_copy(packed, sent_hbm, out_sem.at[0])] if lead else to_blocks(packed, blocks, out_sem)
    start_all(out)
    wait_all(out)


def scan_kernel(base, rows, span, reverse, lead, count, first_ref, order_ref, rate_ref, *refs):
    sources, refs = refs[:count], refs[count + lead :]
    targets = refs[:count]
    arrived, states, in_sem, out_sem = refs[count:]
    slots = states.shape[1] // rows
    spans = order_ref.shape[0]
    loads = [pltpu.make_async_copy(sources[0], arrived, in_sem.at[0])] if lead else from_blocks(sources, arrived, in_sem)
    start_all(loads)
    head = base + (lax.axis_index("seq") * rows) // HEAD_SIZE
    factor = jnp.exp(jnp.full((8, LANES), -rate_ref[head] * span, F32))[0:1]
    wait_all(loads)

    def body(i, state):
        c = spans - 1 - i if reverse else i
        place = order_ref[c]
        device, slot = place // slots, place % slots
        at = rows_at(slot, rows)
        states[device, at, :] = state.astype(BF16)
        carried = jnp.where(first_ref[c] >= span, factor * state, 0.0)
        return carried + arrived[device, at, :].astype(F32)

    lax.fori_loop(0, spans, body, jnp.zeros((rows, LANES), F32), unroll=4)
    out = [pltpu.make_async_copy(states, targets[0], out_sem.at[0])] if lead else to_blocks(states, targets, out_sem)
    start_all(out)
    wait_all(out)


def local_kernel(
    heads, span, rate_ref, seg_ref, q_hbm, k_hbm, v_hbm, out_hbm,
    q_ref, k_ref, v_ref, out_ref, decay, sem, out_sem,
):
    slots = seg_ref.shape[0]
    load = lambda i: span_copies(i, span, (q_hbm, k_hbm, v_hbm), (q_ref, k_ref, v_ref), sem)
    store = lambda i: span_copies(i, span, (out_ref,), (out_hbm,), out_sem)
    for i in range(slots):
        start_all(load(i))
    fill_decay(decay, rate_ref, 0, span)

    def body(i):
        wait_all(load(i))
        at = tokens_at(i, span)
        seg = seg_ref[i]
        same = row_to_cols(seg, span) == seg
        for h in range(heads):
            cols = head_cols(h)
            scores = dot(q_ref[at, cols], k_ref[at, cols], 1, 1)
            mixing = (scores * jnp.where(same, decay[h], 0.0)).astype(BF16)
            out_ref[at, cols] = dot(mixing, v_ref[at, cols], 1, 0).astype(BF16)
        start_all(store(i))

    each_span(slots, body)
    for i in range(slots):
        wait_all(store(i))


def output_kernel(base, heads, rows, span, lead, count, first_ref, home_ref, rate_ref, gain_ref, q_hbm, u_hbm, inner_hbm, *refs):
    if not lead:
        before_ref, refs = refs[0], refs[1:]
    blocks, refs = refs[:count], refs[count:]
    out_ref, q_ref, u_ref, sums_ref, inner_ref, prev, table, sem, in_sem = refs
    slots = home_ref.shape[0]
    states = [pltpu.make_async_copy(blocks[0], prev, in_sem.at[0])] if lead else from_blocks(blocks, prev, in_sem)
    start_all(states)
    part = columns(base, heads)
    sources = (q_hbm.at[:, part], u_hbm.at[:, part], inner_hbm.at[:, part])
    load = lambda i: span_copies(i, span, sources, (q_ref, u_ref, inner_ref), sem)
    for i in range(slots):
        start_all(load(i))
    fill_query_table(table, rate_ref, base, span)
    wait_all(states)

    def body(i):
        wait_all(load(i))
        at = tokens_at(i, span)
        live = token_index(span) < first_ref[home_ref[i]]
        squares = jnp.zeros((span, LANES), F32)
        crossed = jnp.zeros((span, LANES), F32)
        for h in range(heads):
            cols = head_cols(h)
            outer = dot(q_ref[at, cols], get_state(prev, i, h, rows), 1, 0)
            attn = inner_ref[at, cols].astype(F32) + jnp.where(live, table[h], 0.0) * outer
            out_ref[at, cols] = attn
            squares += attn * attn
            crossed += gain_ref[:, head_cols(base + h)] * u_ref[at, cols].astype(F32) * attn
        squares, crossed = cols_to_row(squares), cols_to_row(crossed)
        if not lead:
            squares += before_ref[i, 0:1, :]
            crossed += before_ref[i, 1:2, :]
        sums_ref[i, 0:1, :] = squares
        sums_ref[i, 1:2, :] = crossed

    each_span(slots, body)


def cotangent_kernel(base, heads, rows, span, lead, count, channels, first_ref, home_ref, rate_ref, gain_ref, sums_ref, q_ref, u_ref, attn_ref, *refs):
    g_hbm, targets = refs[0], refs[1 : 1 + count]
    g_ref, table, packed, g_sem, out_sem = refs[1 + count :]
    slots = home_ref.shape[0]
    save = lambda i: span_copies(i, span, (g_ref,), (g_hbm,), g_sem)
    fill_query_table(table, rate_ref, base, span)

    def body(i):
        at = tokens_at(i, span)
        total = jnp.sum(sums_ref[:, i], axis=0)
        scaling = 1.0 / jnp.sqrt(total[0:1] / channels + EPSILON)
        pulled = total[1:2] / channels
        direct = row_to_cols(scaling, LANES)
        along = row_to_cols(scaling * scaling * scaling * pulled, LANES)
        live = token_index(span) < first_ref[home_ref[i]]
        for h in range(heads):
            cols = head_cols(h)
            grad = direct * gain_ref[:, head_cols(base + h)] * u_ref[at, cols].astype(F32)
            grad = (grad - along * attn_ref[at, cols]).astype(BF16)
            g_ref[at, cols] = grad
            weighted = (jnp.where(live, table[h], 0.0) * grad.astype(F32)).astype(BF16)
            put_state(packed, i, h, rows, dot(q_ref[at, cols], weighted, 0, 0).astype(BF16))
        start_all(save(i))

    each_span(slots, body)
    out = [pltpu.make_async_copy(packed, targets[0], out_sem.at[0])] if lead else to_blocks(packed, targets, out_sem)
    start_all(out)
    wait_all(out)
    for i in range(slots):
        wait_all(save(i))


def inner_grads_kernel(base, heads, rows, span, lead, count, first_ref, home_ref, rate_ref, seg_ref, q_hbm, k_hbm, v_hbm, g_hbm, *refs):
    blocks, refs = refs[:count], refs[count:]
    if not lead:
        refs = refs[3:]
    dq_hbm, dk_hbm, dv_hbm = refs[:3]
    q_ref, k_ref, v_ref, g_ref, dq_ref, dk_ref, dv_ref, prev, decay, table, sem, out_sem, in_sem = refs[3:]
    slots = home_ref.shape[0]
    part = columns(base, heads)
    sources = (q_hbm.at[:, part], k_hbm.at[:, part], v_hbm.at[:, part], g_hbm)
    targets = (dq_hbm.at[:, part], dk_hbm.at[:, part], dv_hbm.at[:, part])
    load = lambda i: span_copies(i, span, sources, (q_ref, k_ref, v_ref, g_ref), sem)
    store = lambda i: span_copies(i, span, (dq_ref, dk_ref, dv_ref), targets, out_sem)
    states = [pltpu.make_async_copy(blocks[0], prev, in_sem.at[0])] if lead else from_blocks(blocks, prev, in_sem)
    start_all(states)
    for i in range(slots):
        start_all(load(i))
    fill_decay(decay, rate_ref, base, span)
    fill_query_table(table, rate_ref, base, span)
    wait_all(states)

    def body(i):
        wait_all(load(i))
        at = tokens_at(i, span)
        seg = seg_ref[i]
        same = row_to_cols(seg, span) == seg
        live = token_index(span) < first_ref[home_ref[i]]
        for h in range(heads):
            cols = head_cols(h)
            q, k, v, g = q_ref[at, cols], k_ref[at, cols], v_ref[at, cols], g_ref[at, cols]
            mask = jnp.where(same, decay[h], 0.0)
            mixing = (dot(q, k, 1, 1) * mask).astype(BF16)
            score_grad = (dot(g, v, 1, 1) * mask).astype(BF16)
            outer = dot(g, get_state(prev, i, h, rows), 1, 1)
            dq = dot(score_grad, k, 1, 0) + jnp.where(live, table[h], 0.0) * outer
            dq_ref[at, cols] = dq.astype(BF16)
            dk_ref[at, cols] = dot(score_grad, q, 0, 0).astype(BF16)
            dv_ref[at, cols] = dot(mixing, g, 0, 0).astype(BF16)
        start_all(store(i))

    each_span(slots, body)
    for i in range(slots):
        wait_all(store(i))


def outer_grads_kernel(base, heads, rows, span, lead, count, last_ref, home_ref, rate_ref, k_hbm, v_hbm, dk_part, dv_part, *refs):
    blocks, refs = refs[:count], refs[count:]
    if not lead:
        refs = refs[2:]
    dk_hbm, dv_hbm = refs[:2]
    k_ref, v_ref, dk_in, dv_in, dk_ref, dv_ref, after_ref, table, sem, out_sem, in_sem = refs[2:]
    slots = home_ref.shape[0]
    part = columns(base, heads)
    sources = [ref.at[:, part] for ref in (k_hbm, v_hbm, dk_part, dv_part)]
    targets = (dk_hbm.at[:, part], dv_hbm.at[:, part])
    load = lambda i: span_copies(i, span, sources, (k_ref, v_ref, dk_in, dv_in), sem)
    store = lambda i: span_copies(i, span, (dk_ref, dv_ref), targets, out_sem)
    states = [pltpu.make_async_copy(blocks[0], after_ref, in_sem.at[0])] if lead else from_blocks(blocks, after_ref, in_sem)
    start_all(states)
    for i in range(slots):
        start_all(load(i))
    fill_key_table(table, rate_ref, base, span)
    wait_all(states)

    def body(i):
        wait_all(load(i))
        at = tokens_at(i, span)
        live = token_index(span) >= last_ref[home_ref[i]]
        for h in range(heads):
            cols = head_cols(h)
            side = jnp.where(live, table[h], 0.0)
            after = get_state(after_ref, i, h, rows)
            dk = dk_in[at, cols].astype(F32) + side * dot(v_ref[at, cols], after, 1, 1)
            dv = dv_in[at, cols].astype(F32) + side * dot(k_ref[at, cols], after, 1, 0)
            dk_ref[at, cols] = dk.astype(BF16)
            dv_ref[at, cols] = dv.astype(BF16)
        start_all(store(i))

    each_span(slots, body)
    for i in range(slots):
        wait_all(store(i))


def exchange(blocks):
    if len(blocks) == 1:
        return (lax.all_to_all(blocks[0], "seq", split_axis=0, concat_axis=0, tiled=True),)
    devices = len(blocks)
    moved = [blocks[0]] + [None] * (devices - 1)
    for k in range(devices - 1, 0, -1):
        moved[k] = lax.ppermute(blocks[k], "seq", [(i, i ^ k) for i in range(devices)])
    return tuple(moved)


def shards(query, key, value, upstream, norm_gain, decay_rate, document_lengths, group_home):
    devices = lax.axis_size("seq")
    assert devices & (devices - 1) == 0
    tokens, width = query.shape
    all_heads = width // HEAD_SIZE
    slots = group_home.shape[0]
    span = tokens // slots
    spans = slots * devices
    channels = width * lax.axis_size("head")
    halves = (all_heads // 2, all_heads - all_heads // 2)
    chunks = ((0, halves[0], True, 1), (halves[0], halves[1], False, devices))

    doc_ends = jnp.cumsum(document_lengths)
    positions = (group_home * span)[:, None] + jnp.arange(span, dtype=jnp.int32)[None, :]
    seg = jnp.sum((doc_ends <= positions[..., None]).astype(F32), axis=-1).reshape(slots, 1, span)
    gain = norm_gain.reshape(1, width)

    smem = pl.BlockSpec(memory_space=pltpu.SMEM)
    vmem = pl.BlockSpec(memory_space=pltpu.VMEM)
    hbm = pl.BlockSpec(memory_space=pl.ANY)
    whole = jax.ShapeDtypeStruct((tokens, width), BF16)
    spans_table = jax.ShapeDtypeStruct((spans + 1,), jnp.int32)

    def sems(*shape):
        return pltpu.SemaphoreType.DMA(shape)

    def call(kernel, limit, flops, in_specs, out_specs, out_shape, scratch, static, aliases={}):
        return pl.pallas_call(
            functools.partial(kernel, *static),
            in_specs=in_specs,
            out_specs=out_specs,
            out_shape=out_shape,
            scratch_shapes=scratch,
            input_output_aliases=aliases,
            compiler_params=pltpu.CompilerParams(vmem_limit_bytes=limit << 20),
            cost_estimate=pl.CostEstimate(flops=flops, bytes_accessed=0, transcendentals=0),
        )

    def shape_of(chunk):
        _, heads, lead, _ = chunk
        rows = heads * HEAD_SIZE // devices
        table = pltpu.VMEM((heads, span, LANES), F32)
        decay = pltpu.VMEM((heads, span, span), F32)
        token = pltpu.VMEM((tokens, heads * HEAD_SIZE), BF16)
        states = (devices, slots * rows, LANES)
        if lead:
            out = [jax.ShapeDtypeStruct(states, BF16)]
        else:
            out = [jax.ShapeDtypeStruct(states[1:], BF16)] * devices
        return rows, table, decay, token, pltpu.VMEM(states, BF16), out

    def static_of(chunk):
        base, heads, lead, count = chunk
        return (base, heads, shape_of(chunk)[0], span, lead, count)

    work = 2 * tokens * width * span

    def summaries(chunk, table_in):
        _, _, lead, count = chunk
        rows, table, _, token, states, out = shape_of(chunk)
        packed = states
        tables = []
        if lead:
            packed = pltpu.VMEM((devices, slots * rows + TAIL, LANES), BF16)
            out = [jax.ShapeDtypeStruct((devices, slots * rows + TAIL, LANES), BF16)]
            tables = [spans_table] * 2
        return call(
            summary_kernel, LIMIT, work // 4,
            [smem, smem, smem, hbm, hbm],
            [hbm] * count + [smem] * len(tables),
            out + tables,
            [token] * 2 + [table, packed, sems(2, slots), sems(count)],
            static_of(chunk),
        )(table_in, group_home, decay_rate, key, value)

    def scan(chunk, blocks, reverse, beside=()):
        base, _, lead, count = chunk
        rows, _, _, _, states, out = shape_of(chunk)
        arrived = pltpu.VMEM(blocks[0].shape, BF16) if lead else states
        return call(
            scan_kernel, ROOMY, work // 16,
            [smem, smem, smem] + [hbm] * (count + len(beside)),
            [hbm] * count,
            out,
            [arrived, states, sems(count), sems(count)],
            (base, rows, span, reverse, lead, count),
        )(first, order, decay_rate, *blocks, *beside)

    def outputs(chunk, inner, before, blocks):
        _, heads, lead, count = chunk
        _, table, _, token, states, _ = shape_of(chunk)
        part = (tokens, heads * HEAD_SIZE)
        extra = [] if lead else [before]
        return call(
            output_kernel, HANDOFF, work // 4,
            [smem, smem, smem, vmem, hbm, hbm, hbm] + [vmem] * len(extra) + [hbm] * count,
            [vmem] * 4,
            [pltpu.VMEM(part, F32), token, token, jax.ShapeDtypeStruct((slots, 2, span), F32)],
            [token, states, table, sems(3, slots), sems(count)],
            static_of(chunk),
        )(first, group_home, decay_rate, gain, query, upstream, inner, *extra, *blocks)

    def cotangents(chunk, sums, query_v, upstream_v, attn):
        _, heads, _, count = chunk
        _, table, _, token, states, out = shape_of(chunk)
        return call(
            cotangent_kernel, RECEIVE, work // 4,
            [smem, smem, smem] + [vmem] * 5,
            [hbm] * (1 + count),
            [jax.ShapeDtypeStruct((tokens, heads * HEAD_SIZE), BF16)] + out,
            [token, table, states, sems(1, slots), sems(count)],
            static_of(chunk) + (channels,),
        )(first, group_home, decay_rate, gain, sums, query_v, upstream_v, attn)

    def inner_grads(chunk, grad_in, blocks, into):
        _, _, _, count = chunk
        _, table, decay, token, states, _ = shape_of(chunk)
        start = 8 + count
        return call(
            inner_grads_kernel, LASTING, 3 * work,
            [smem, smem, smem, vmem] + [hbm] * (4 + count + len(into)),
            [hbm] * 3,
            [whole] * 3,
            [token] * 7 + [states, decay, table, sems(4, slots), sems(3, slots), sems(count)],
            static_of(chunk),
            {start + i: i for i in range(len(into))},
        )(first, group_home, decay_rate, seg, query, key, value, grad_in, *blocks, *into)

    def outer_grads(chunk, parts, blocks, into):
        _, _, _, count = chunk
        _, table, _, token, states, _ = shape_of(chunk)
        start = 7 + count
        return call(
            outer_grads_kernel, LASTING, work // 2,
            [smem, smem, smem] + [hbm] * (4 + count + len(into)),
            [hbm] * 2,
            [whole] * 2,
            [token] * 6 + [states, table, sems(4, slots), sems(2, slots), sems(count)],
            static_of(chunk),
            {start + i: i for i in range(len(into))},
        )(last, group_home, decay_rate, key, value, *parts, *blocks, *into)

    a, b = chunks
    sent_a, first, last = summaries(a, document_lengths)
    arrived_a = exchange([sent_a])
    sent_b = summaries(b, last)
    arrived_b = exchange(sent_b)

    homes = arrived_a[0][:, -TAIL, :slots].astype(jnp.int32).reshape(-1)
    hits = homes[None, :] == jnp.arange(spans, dtype=jnp.int32)[:, None]
    order = jnp.sum(jnp.where(hits, jnp.arange(spans, dtype=jnp.int32)[None, :], 0), axis=1)

    prev_a = exchange(scan(a, arrived_a, False, sent_b[:1]))
    prev_b = exchange(scan(b, arrived_b, False))

    inner = call(
        local_kernel, LIMIT, 2 * work,
        [smem, vmem, hbm, hbm, hbm],
        hbm,
        whole,
        [pltpu.VMEM((tokens, width), BF16)] * 4
        + [pltpu.VMEM((all_heads, span, span), F32), sems(3, slots), sems(1, slots)],
        (all_heads, span),
    )(decay_rate, seg, query, key, value)

    attn_a, query_a, upstream_a, sums = outputs(a, inner, None, prev_a)
    attn_b, query_b, upstream_b, sums = outputs(b, inner, sums, prev_b)
    sums = lax.all_gather(sums, "head")

    grad_a, *rev_a = cotangents(a, sums, query_a, upstream_a, attn_a)
    rev_a = exchange(rev_a)
    grad_b, *rev_b = cotangents(b, sums, query_b, upstream_b, attn_b)
    beside = rev_b[:1]
    rev_b = exchange(rev_b)

    after_a = exchange(scan(a, rev_a, True, beside))
    after_b = exchange(scan(b, rev_b, True))

    parts = inner_grads(a, grad_a, prev_a, ())
    query_grad, key_inner, value_inner = inner_grads(b, grad_b, prev_b, parts)
    finals = outer_grads(a, (key_inner, value_inner), after_a, ())
    key_grad, value_grad = outer_grads(b, (key_inner, value_inner), after_b, finals)
    return query_grad, key_grad, value_grad


def solution(mesh):
    in_specs = (
        P("seq", "head"),
        P("seq", "head"),
        P("seq", "head"),
        P("seq", "head"),
        P("head"),
        P("head"),
        P(),
        P("seq"),
    )
    out_specs = (P("seq", "head"), P("seq", "head"), P("seq", "head"))

    return jax.shard_map(shards, mesh=mesh, in_specs=in_specs, out_specs=out_specs, check_vma=False)
```

time: 157 us -> 206 us (1.31)
  starting transfers between devices: 7.22 us -> 72.9 us
  blocking collectives: 69.4 us -> 5.45 us
  Pallas kernels: 50.1 us -> 81.8 us
  waiting for transfers between devices: 27.1 us -> 34.7 us
  local copies, waits for them, and re-layouts: 1.79 us -> 8.21 us
    all_to_all x2 -> x0, blocking collectives: 63.9 us -> none  [exchange(): lax.all_to_all(blocks, 'seq', split_axis=0, concat_axis=0, tiled=True)]
    ppermute x0 -> x28, starting transfers between devices: none -> 54.8 us  [exchange(): lax.ppermute(blocks[k], 'seq', [(i, i ^ k) for i in range(devices)])]
    pallas_call x8 -> x15, Pallas kernels: 50.1 us -> 81.8 us  [the longest x2 20.7 us: inner_grads(): call(inner_grads_kernel, LASTING, 3 * work, [smem, smem, smem, vmem] + [h...]
    ppermute x0 -> x28, waiting for transfers between devices: none -> 18 us  [exchange(): lax.ppermute(blocks[k], 'seq', [(i, i ^ k) for i in range(devices)])]
    all_to_all x2 -> x4, starting transfers between devices: 7.22 us -> 18.1 us  [exchange(): lax.all_to_all(blocks[0], 'seq', split_axis=0, concat_axis=0, tiled=True)]
    all_to_all x2 -> x4, waiting for transfers between devices: 27.1 us -> 16.8 us  [exchange(): lax.all_to_all(blocks[0], 'seq', split_axis=0, concat_axis=0, tiled=True)]
    unnamed x26 -> x90, local copies, waits for them, and re-layouts: 1.03 us -> 7.44 us
  transfers between devices with their start and end apart: 2 -> 32, of which waited for: 2 -> 6; matrix products, arithmetic and copies ran while one was open for 1% -> 1% of each run, Pallas kernels for 15% -> 27%
where the time goes in v5:
time: 206 us; the launch traced here: 205 us
  Pallas kernels  81.8 us (40%)
  starting transfers between devices  72.9 us (35%)
  waiting for transfers between devices  34.7 us (17%)
  local copies, waits for them, and re-layouts  8.21 us (4%)
  blocking collectives  5.45 us (3%)
    ppermute x28, starting transfers between devices, exchange(): lax.ppermute(blocks[k], 'seq', [(i, i ^ k) for i in range(devices)])  54.8 us
    pallas_call x2, Pallas kernels, inner_grads(): call(inner_grads_kernel, LASTING, 3 * work, [smem, smem, smem, vmem] + [h...  20.7 us
    all_to_all x4, starting transfers between devices, exchange(): lax.all_to_all(blocks[0], 'seq', split_axis=0, concat_axis=0, tiled=True)  18.1 us
    ppermute x28, waiting for transfers between devices, exchange(): lax.ppermute(blocks[k], 'seq', [(i, i ^ k) for i in range(devices)])  18 us
    all_to_all x4, waiting for transfers between devices, exchange(): lax.all_to_all(blocks[0], 'seq', split_axis=0, concat_axis=0, tiled=True)  16.8 us
    pallas_call x2, Pallas kernels, outputs(): call(output_kernel, HANDOFF, work // 4, [smem, smem, smem, vmem, hbm, hbm...  12.4 us
    pallas_call x2, Pallas kernels, cotangents(): call(cotangent_kernel, RECEIVE, work // 4, [smem, smem, smem] + [vmem] *...  11.3 us
    pallas_call x2, Pallas kernels, outer_grads(): call(outer_grads_kernel, LASTING, work // 2, [smem, smem, smem] + [hbm] *...  10.1 us
  transfers between devices with their start and end apart: 32, of which 6 were waited for; matrix products, arithmetic and copies ran while one was open for 1% of the time, Pallas kernels for 27%

profile of v5, /device:TPU:0, one launch (start us, length us, event | category | flops | bytes accessed | tf_op | source)
XLA Modules:
  0.0 204.8 jit_solution(9719244792925611492)
XLA Ops:
  0.6 5.0 %shard_map.103 = (bf16[8,272,128]{2,1,0:T(8,128)(2,1)}, s32[65]{0:T(128)}, s32[65]{0:T(128)}) custom-call(s32[32]{0:T(128)} %refs_0_.1, s32[8]{0:T(128)} %home_ref.15, f32[4]{0:T(128)} %rate_ref.25, bf16[2048,512]{1,0:T(8,128)(2,1)} %k_hbm.9, bf16[2048,512]{1,0:T(8,128)(2,1)} %v_hbm.9), custom_call_target="tpu_custom_call" | custom-call | flops 134217728 | tf_op jit(solution)/shard_map/pallas_call | solution.py:476
  5.6 7.3 %all-to-all-start = ((bf16[8,272,128]{2,1,0:T(8,128)(2,1)}), bf16[8,272,128]{2,1,0:T(8,128)(2,1)S(1)}, u32[]{:S(2)}, u32[]{:S(2)}) async-start(bf16[8,272,128]{2,1,0:T(8,128)(2,1)} %get-tuple-element.60), calls=%async_computation | async-start | bytes 1114112 | tf_op jit(solution)/shard_map/all_to_all | solution.py:402
  13.0 4.5 %shard_map.105 = (bf16[256,128]{1,0:T(8,128)(2,1)}, bf16[256,128]{1,0:T(8,128)(2,1)}, bf16[256,128]{1,0:T(8,128)(2,1)}, bf16[256,128]{1,0:T(8,128)(2,1)}, bf16[2...) custom-call(s32[65]{0:T(128)} %get-tuple-element.61.refs_0_.last_ref, ...), custom_call_target="tpu_custom_call" | custom-call | flops 134217728 | tf_op jit(solution)/shard_map/pallas_call | solution.py:476
  17.5 10.6 %all-to-all-done.refs_0_ = bf16[8,272,128]{2,1,0:T(8,128)(2,1)S(1)} async-done(((bf16[8,272,128]{2,1,0:T(8,128)(2,1)}), bf16[8,272,128]{2,1,0:T(8,128)(2,1)S(1)}, u32[]{:S(2)}, u32[]{:S(2)}) %all-to-all-start) | async-done | bytes 557088 | tf_op jit(solution)/shard_map/all_to_all | solution.py:402
  29.3 2.1 %shard_map.106 = bf16[8,256,128]{2,1,0:T(8,128)(2,1)} custom-call(s32[65]{0:T(128)S(1)} %copy-done.31, s32[64]{0:T(128)S(1)} %select_reduce_fusion.order_ref, f32[4]{0:T(128)S(1)} %copy-done.29, bf16[8,272,128]{2,1,0:T(8,128)(2,1)S(1)} %all-to-all-done.refs_0_, bf16[256,128]{1,0:T(8,128)(2,1)S(1)} %copy-done.26), custom_call_target="tpu_custom_call" | custom-call | flops 33554432 | tf_op jit(solution)/shard_map/pallas_call | solution.py:489
  31.4 3.6 %all-to-all-start.1 = ((bf16[8,256,128]{2,1,0:T(8,128)(2,1)}), bf16[8,256,128]{2,1,0:T(8,128)(2,1)S(1)}, u32[]{:S(2)}, u32[]{:S(2)}) async-start(bf16[8,256,128]{2,1,0:T(8,128)(2,1)} %shard_map.106), calls=%async_computation.1 | async-start | bytes 1048576 | tf_op jit(solution)/shard_map/all_to_all | solution.py:402
  35.0 2.0 collective-permute-start
  37.1 1.5 collective-permute-start.1
  38.6 2.8 %collective-permute-start.3 = (bf16[256,128]{1,0:T(8,128)(2,1)S(1)}, bf16[256,128]{1,0:T(8,128)(2,1)S(1)}, u32[]{:S(2)}, u32[]{:S(2)}) collective-permute-start(bf16[256,128]{1,0:T(8,128)(2,1)S(1)} %copy-done.41), channel_id=1, source_target_pairs={{0,16},{4,20},{8,24},{12,28},{16,0},{20,4},{24,8},{28,12},{1,17},{... | collective-permute-start | bytes 196616 | tf_op jit(solution)/shard_map/ppermute | solution.py:406
  41.5 1.5 collective-permute-start.4
  42.9 3.7 %collective-permute-start.5 = (bf16[256,128]{1,0:T(8,128)(2,1)S(1)}, bf16[256,128]{1,0:T(8,128)(2,1)S(1)}, u32[]{:S(2)}, u32[]{:S(2)}) collective-permute-start(bf16[256,128]{1,0:T(8,128)(2,1)S(1)} %copy-done.39), channel_id=1, source_target_pairs={{0,24},{4,28},{8,16},{12,20},{16,8},{20,12},{24,0},{28,4},{1,25},{... | collective-permute-start | bytes 196616 | tf_op jit(solution)/shard_map/ppermute | solution.py:406
  46.6 4.3 %collective-permute-start.6 = (bf16[256,128]{1,0:T(8,128)(2,1)S(1)}, bf16[256,128]{1,0:T(8,128)(2,1)S(1)}, u32[]{:S(2)}, u32[]{:S(2)}) collective-permute-start(bf16[256,128]{1,0:T(8,128)(2,1)S(1)} %copy-done.38), channel_id=1, source_target_pairs={{0,28},{4,24},{8,20},{12,16},{16,12},{20,8},{24,4},{28,0},{1,29},{... | collective-permute-start | bytes 196616 | tf_op jit(solution)/shard_map/ppermute | solution.py:406
  51.3 6.7 %collective-permute-done.3.refs_4_ = bf16[256,128]{1,0:T(8,128)(2,1)S(1)} collective-permute-done((bf16[256,128]{1,0:T(8,128)(2,1)S(1)}, bf16[256,128]{1,0:T(8,128)(2,1)S(1)}, u32[]{:S(2)}, u32[]{:S(2)}) %collective-permute-start.3) | collective-permute-done | bytes 65568 | tf_op jit(solution)/shard_map/ppermute | solution.py:406
  58.0 2.1 %collective-permute-done.4.refs_5_ = bf16[256,128]{1,0:T(8,128)(2,1)S(1)} collective-permute-done((bf16[256,128]{1,0:T(8,128)(2,1)S(1)}, bf16[256,128]{1,0:T(8,128)(2,1)S(1)}, u32[]{:S(2)}, u32[]{:S(2)}) %collective-permute-start.4) | collective-permute-done | bytes 65568 | tf_op jit(solution)/shard_map/ppermute | solution.py:406
  60.0 2.8 %shard_map.108 = (bf16[256,128]{1,0:T(8,128)(2,1)S(1)}, bf16[256,128]{1,0:T(8,128)(2,1)S(1)}, bf16[256,128]{1,0:T(8,128)(2,1)S(1)}, bf16[256,128]{1,0:T(8,128)(2...) custom-call(s32[65]{0:T(128)S(1)} %copy-done.31, ...), custom_call_target="tpu_custom_call" | custom-call | flops 33554432 | tf_op jit(solution)/shard_map/pallas_call | solution.py:489
  64.2 2.1 %collective-permute-start.8 = (bf16[256,128]{1,0:T(8,128)(2,1)S(1)}, bf16[256,128]{1,0:T(8,128)(2,1)S(1)}, u32[]{:S(2)}, u32[]{:S(2)}) collective-permute-start(bf16[256,128]{1,0:T(8,128)(2,1)S(1)} %get-tuple-element.73), channel_id=1, source_target_pairs={{0,8},{4,12},{8,0},{12,4},{16,24},{20,28},{24,16},{28,20},{1,9},{5... | collective-permute-start | bytes 196616 | tf_op jit(solution)/shard_map/ppermute | solution.py:406
  68.0 2.0 collective-permute-start.10
  70.9 1.5 collective-permute-start.12
  72.4 3.2 %collective-permute-start.13 = (bf16[256,128]{1,0:T(8,128)(2,1)S(1)}, bf16[256,128]{1,0:T(8,128)(2,1)S(1)}, u32[]{:S(2)}, u32[]{:S(2)}) collective-permute-start(bf16[256,128]{1,0:T(8,128)(2,1)S(1)} %get-tuple-element.78), channel_id=1, source_target_pairs={{0,28},{4,24},{8,20},{12,16},{16,12},{20,8},{24,4},{28,0},{1,29},{... | collective-permute-start | bytes 196616 | tf_op jit(solution)/shard_map/ppermute | solution.py:406
  75.6 8.1 %shard_map.104.inner_hbm = bf16[2048,512]{1,0:T(8,128)(2,1)} custom-call(f32[4]{0:T(128)} %rate_ref.25, f32[8,1,256]{2,1,0:T(1,128)} %reshape.66.seg_ref, bf16[2048,512]{1,0:T(8,128)(2,1)} %q_hbm.9, bf16[2048,512]{1,0:T(8,128)(2,1)} %k_hbm.9, bf16[2048,512]{1,0:T(8,128)(2,1)} %v_hbm.9), custom_call_target="tpu_custom_call" | custom-call | flops 1073741824 | tf_op jit(solution)/shard_map/pallas_call | solution.py:565
  84.6 6.1 %shard_map.107 = (f32[2048,256]{1,0:T(8,128)S(1)}, bf16[2048,256]{1,0:T(8,128)(2,1)S(1)}, bf16[2048,256]{1,0:T(8,128)(2,1)S(1)}, f32[8,2,256]{2,1,0:T(2,128)}) custom-call(s32[65]{0:T(128)} %get-tuple-element.59.first_ref, s32[8]{0:T(128)} %home_ref.15, f32[4]{0:T(128)} %rate_ref.25, f32[1,512]{1,0:T(1,128)} %bitcast.5, bf16[2048,512]{1,0:T(8,128)(2,1)} %q_hbm.9, ...), custom_call_target="tpu_custom_call" | custom-call | flops 134217728 | tf_op jit(solution)/shard_map/pallas_call | solution.py:503
  91.5 6.3 %shard_map.109 = (f32[2048,256]{1,0:T(8,128)S(1)}, bf16[2048,256]{1,0:T(8,128)(2,1)S(1)}, bf16[2048,256]{1,0:T(8,128)(2,1)S(1)}, f32[8,2,256]{2,1,0:T(2,128)}) custom-call(s32[65]{0:T(128)} %get-tuple-element.59.first_ref, s32[8]{0:T(128)} %home_ref.15, f32[4]{0:T(128)} %rate_ref.25, f32[1,512]{1,0:T(1,128)} %bitcast.6, bf16[2048,512]{1,0:T(8,128)(2,1)} %q_hbm.9, ...), custom_call_target="tpu_custom_call" | custom-call | flops 134217728 | tf_op jit(solution)/shard_map/pallas_call | solution.py:503
  97.9 5.4 %all-gather = f32[32,2,256]{2,1,0:T(2,128)S(1)} all-gather(f32[8,2,256]{2,1,0:T(2,128)} %get-tuple-element.79), channel_id=2, replica_groups=mesh['seq'=8,'head'=4] {'head'}, dimensions={0}, use_global_device_ids=true | all-gather | bytes 81920 | tf_op jit(solution)/shard_map/all_gather | solution.py:577
  103.4 5.7 %shard_map.111 = (bf16[2048,256]{1,0:T(8,128)(2,1)S(1)}, bf16[8,256,128]{2,1,0:T(8,128)(2,1)}) custom-call(s32[65]{0:T(128)S(1)} %copy-done.32, s32[8]{0:T(128)S(1)} %copy-done.34, f32[4]{0:T(128)S(1)} %copy-done.30, f32[1,512]{1,0:T(1,128)S(1)} %bitcast.7, f32[4,8,2,256]{3,2,1,0:T(2,128)S(1)} %bitcast.3, bf16[2048,256]{1,0:T(8,128)(2,1)S(1)} %get-tuple-element.84.q_ref, ...), custom_call_target="tpu_custom_call" | custom-call | flops 134217728 | tf_op jit(solution)/shard_map/pallas_call | solution.py:515
  110.0 3.5 %all-to-all-start.2 = ((bf16[8,256,128]{2,1,0:T(8,128)(2,1)}), bf16[8,256,128]{2,1,0:T(8,128)(2,1)S(1)}, u32[]{:S(2)}, u32[]{:S(2)}) async-start(bf16[8,256,128]{2,1,0:T(8,128)(2,1)} %get-tuple-element.110), calls=%async_computation.2 | async-start | bytes 1048576 | tf_op jit(solution)/shard_map/all_to_all | solution.py:402
  113.5 1.2 copy-done.5
  114.7 1.2 copy-done.7
  116.0 5.6 %shard_map.110 = (bf16[2048,256]{1,0:T(8,128)(2,1)S(1)}, bf16[256,128]{1,0:T(8,128)(2,1)S(1)}, bf16[256,128]{1,0:T(8,128)(2,1)S(1)}, bf16[256,128]{1,0:T(8,128)(...) custom-call(s32[65]{0:T(128)S(1)} %copy-done.32, ...), custom_call_target="tpu_custom_call" | custom-call | flops 134217728 | tf_op jit(solution)/shard_map/pallas_call | solution.py:515
  122.6 6.1 %all-to-all-done.2.refs_0_ = bf16[8,256,128]{2,1,0:T(8,128)(2,1)S(1)} async-done(((bf16[8,256,128]{2,1,0:T(8,128)(2,1)}), bf16[8,256,128]{2,1,0:T(8,128)(2,1)S(1)}, u32[]{:S(2)}, u32[]{:S(2)}) %all-to-all-start.2) | async-done | bytes 524320 | tf_op jit(solution)/shard_map/all_to_all | solution.py:402
  128.7 2.0 shard_map.115
  130.7 3.6 %all-to-all-start.3 = ((bf16[8,256,128]{2,1,0:T(8,128)(2,1)}), bf16[8,256,128]{2,1,0:T(8,128)(2,1)S(1)}, u32[]{:S(2)}, u32[]{:S(2)}) async-start(bf16[8,256,128]{2,1,0:T(8,128)(2,1)} %shard_map.115), calls=%async_computation.3 | async-start | bytes 1048576 | tf_op jit(solution)/shard_map/all_to_all | solution.py:402
  134.4 2.0 collective-permute-start.14
  136.4 1.5 collective-permute-start.15
  137.9 2.9 %collective-permute-start.17 = (bf16[256,128]{1,0:T(8,128)(2,1)S(1)}, bf16[256,128]{1,0:T(8,128)(2,1)S(1)}, u32[]{:S(2)}, u32[]{:S(2)}) collective-permute-start(bf16[256,128]{1,0:T(8,128)(2,1)S(1)} %get-tuple-element.98), channel_id=1, source_target_pairs={{0,16},{4,20},{8,24},{12,28},{16,0},{20,4},{24,8},{28,12},{1,17},{... | collective-permute-start | bytes 196616 | tf_op jit(solution)/shard_map/ppermute | solution.py:406
  140.8 1.5 collective-permute-start.18
  142.3 3.8 %collective-permute-start.19 = (bf16[256,128]{1,0:T(8,128)(2,1)S(1)}, bf16[256,128]{1,0:T(8,128)(2,1)S(1)}, u32[]{:S(2)}, u32[]{:S(2)}) collective-permute-start(bf16[256,128]{1,0:T(8,128)(2,1)S(1)} %get-tuple-element.100), channel_id=1, source_target_pairs={{0,24},{4,28},{8,16},{12,20},{16,8},{20,12},{24,0},{28,4},{1,25},{... | collective-permute-start | bytes 196616 | tf_op jit(solution)/shard_map/ppermute | solution.py:406
  146.0 4.2 %collective-permute-start.20 = (bf16[256,128]{1,0:T(8,128)(2,1)S(1)}, bf16[256,128]{1,0:T(8,128)(2,1)S(1)}, u32[]{:S(2)}, u32[]{:S(2)}) collective-permute-start(bf16[256,128]{1,0:T(8,128)(2,1)S(1)} %get-tuple-element.101), channel_id=1, source_target_pairs={{0,28},{4,24},{8,20},{12,16},{16,12},{20,8},{24,4},{28,0},{1,29},{... | collective-permute-start | bytes 196616 | tf_op jit(solution)/shard_map/ppermute | solution.py:406
  150.3 7.0 %collective-permute-done.17.refs_4_ = bf16[256,128]{1,0:T(8,128)(2,1)S(1)} collective-permute-done((bf16[256,128]{1,0:T(8,128)(2,1)S(1)}, bf16[256,128]{1,0:T(8,128)(2,1)S(1)}, u32[]{:S(2)}, u32[]{:S(2)}) %collective-permute-start.17) | collective-permute-done | bytes 65568 | tf_op jit(solution)/shard_map/ppermute | solution.py:406
  157.3 2.1 %collective-permute-done.18.refs_5_ = bf16[256,128]{1,0:T(8,128)(2,1)S(1)} collective-permute-done((bf16[256,128]{1,0:T(8,128)(2,1)S(1)}, bf16[256,128]{1,0:T(8,128)(2,1)S(1)}, u32[]{:S(2)}, u32[]{:S(2)}) %collective-permute-start.18) | collective-permute-done | bytes 65568 | tf_op jit(solution)/shard_map/ppermute | solution.py:406
  159.4 2.8 %shard_map.114 = (bf16[256,128]{1,0:T(8,128)(2,1)S(1)}, bf16[256,128]{1,0:T(8,128)(2,1)S(1)}, bf16[256,128]{1,0:T(8,128)(2,1)S(1)}, bf16[256,128]{1,0:T(8,128)(2...) custom-call(s32[65]{0:T(128)S(1)} %copy-done.32, ...), custom_call_target="tpu_custom_call" | custom-call | flops 33554432 | tf_op jit(solution)/shard_map/pallas_call | solution.py:489
  163.0 2.2 %collective-permute-start.22 = (bf16[256,128]{1,0:T(8,128)(2,1)S(1)}, bf16[256,128]{1,0:T(8,128)(2,1)S(1)}, u32[]{:S(2)}, u32[]{:S(2)}) collective-permute-start(bf16[256,128]{1,0:T(8,128)(2,1)S(1)} %get-tuple-element.104), channel_id=1, source_target_pairs={{0,8},{4,12},{8,0},{12,4},{16,24},{20,28},{24,16},{28,20},{1,9},{5... | collective-permute-start | bytes 196616 | tf_op jit(solution)/shard_map/ppermute | solution.py:406
  165.3 10.0 %shard_map.112 = (bf16[2048,512]{1,0:T(8,128)(2,1)}, bf16[2048,512]{1,0:T(8,128)(2,1)}, bf16[2048,512]{1,0:T(8,128)(2,1)}) custom-call(s32[65]{0:T(128)S(1)} %copy-done.32, s32[8]{0:T(128)S(1)} %copy-done.34, f32[4]{0:T(128)S(1)} %copy-done.30, f32[8,1,256]{2,1,0:T(1,128)S(1)} %copy-done.28, bf16[2048,512]{1,0:T(8,128)(2,1)} %q_hbm.9, ...), custom_call_target="tpu_custom_call" | custom-call | flops 1610612736 | tf_op jit(solution)/shard_map/pallas_call | solution.py:528
  176.2 2.0 collective-permute-start.24
  179.2 1.5 collective-permute-start.26
  180.7 3.2 %collective-permute-start.27 = (bf16[256,128]{1,0:T(8,128)(2,1)S(1)}, bf16[256,128]{1,0:T(8,128)(2,1)S(1)}, u32[]{:S(2)}, u32[]{:S(2)}) collective-permute-start(bf16[256,128]{1,0:T(8,128)(2,1)S(1)} %get-tuple-element.109), channel_id=1, source_target_pairs={{0,28},{4,24},{8,20},{12,16},{16,12},{20,8},{24,4},{28,0},{1,29},{... | collective-permute-start | bytes 196616 | tf_op jit(solution)/shard_map/ppermute | solution.py:406
  183.9 10.7 %shard_map.113 = (bf16[2048,512]{1,0:T(8,128)(2,1)}, bf16[2048,512]{1,0:T(8,128)(2,1)}, bf16[2048,512]{1,0:T(8,128)(2,1)}) custom-call(s32[65]{0:T(128)S(1)} %copy-done.32, s32[8]{0:T(128)S(1)} %copy-done.34, f32[4]{0:T(128)S(1)} %copy-done.30, f32[8,1,256]{2,1,0:T(1,128)S(1)} %copy-done.28, ...), custom_call_target="tpu_custom_call", output_to_operand_aliasing={{0}: (16, {}), {1}: (17, {}), {2}: (18, {})} | custom-call | flops 1610612736 | tf_op jit(solution)/shard_map/pallas_call | solution.py:528
  194.7 4.7 %shard_map.116 = (bf16[2048,512]{1,0:T(8,128)(2,1)}, bf16[2048,512]{1,0:T(8,128)(2,1)}) custom-call(s32[65]{0:T(128)S(1)} %copy-done.36, s32[8]{0:T(128)S(1)} %copy-done.34, f32[4]{0:T(128)S(1)} %copy-done.30, bf16[2048,512]{1,0:T(8,128)(2,1)} %k_hbm.9, bf16[2048,512]{1,0:T(8,128)(2,1)} %v_hbm.9, bf16[2048,512]{1,0:T(8,128)(2,1)} %get-tuple-element.92.dk_part, ...), custom_call_target="tpu_custom_call" | custom-call | flops 268435456 | tf_op jit(solution)/shard_map/pallas_call | solution.py:542
  199.4 5.4 %shard_map.117 = (bf16[2048,512]{1,0:T(8,128)(2,1)}, bf16[2048,512]{1,0:T(8,128)(2,1)}) custom-call(s32[65]{0:T(128)S(1)} %copy-done.36, s32[8]{0:T(128)S(1)} %copy-done.34, f32[4]{0:T(128)S(1)} %copy-done.30, bf16[2048,512]{1,0:T(8,128)(2,1)} %k_hbm.9, bf16[2048,512]{1,0:T(8,128)(2,1)} %v_hbm.9, ...), custom_call_target="tpu_custom_call", output_to_operand_aliasing={{0}: (15, {}), {1}: (16, {})} | custom-call | flops 268435456 | tf_op jit(solution)/shard_map/pallas_call | solution.py:542
  (132 shorter events, 11.8 us)
Async XLA Ops:
  5.6 22.5 %all-to-all-start = ((bf16[8,272,128]{2,1,0:T(8,128)(2,1)}), bf16[8,272,128]{2,1,0:T(8,128)(2,1)S(1)}, u32[]{:S(2)}, u32[]{:S(2)}) async-start(bf16[8,272,128]{2,1,0:T(8,128)(2,1)} %get-tuple-element.60), calls=%async_computation | async-start | bytes 1114112 | tf_op jit(solution)/shard_map/all_to_all | solution.py:402
  17.5 25.4 %copy-start.33 = (s32[8]{0:T(128)S(1)}, s32[8]{0:T(128)}, u32[]{:S(2)}) copy-start(s32[8]{0:T(128)} %home_ref.15) | copy-start | bytes 100
  17.5 33.5 %copy-start.37 = (s32[32]{0:T(128)S(1)}, s32[32]{0:T(128)}, u32[]{:S(2)}) copy-start(s32[32]{0:T(128)} %refs_0_.1) | copy-start | bytes 388
  29.2 17.4 %copy-start.38 = (bf16[256,128]{1,0:T(8,128)(2,1)S(1)}, bf16[256,128]{1,0:T(8,128)(2,1)}, u32[]{:S(2)}) copy-start(bf16[256,128]{1,0:T(8,128)(2,1)} %get-tuple-element.70) | copy-start | bytes 196612
  29.2 30.8 %copy-start.27 = (bf16[256,128]{1,0:T(8,128)(2,1)S(1)}, bf16[256,128]{1,0:T(8,128)(2,1)}, u32[]{:S(2)}) copy-start(bf16[256,128]{1,0:T(8,128)(2,1)} %get-tuple-element.62.refs_1_.refs_0_) | copy-start | bytes 196612
  31.4 52.4 %all-to-all-start.1 = ((bf16[8,256,128]{2,1,0:T(8,128)(2,1)}), bf16[8,256,128]{2,1,0:T(8,128)(2,1)S(1)}, u32[]{:S(2)}, u32[]{:S(2)}) async-start(bf16[8,256,128]{2,1,0:T(8,128)(2,1)} %shard_map.106), calls=%async_computation.1 | async-start | bytes 1048576 | tf_op jit(solution)/shard_map/all_to_all | solution.py:402
  35.0 7.9 %collective-permute-start = (bf16[256,128]{1,0:T(8,128)(2,1)S(1)}, bf16[256,128]{1,0:T(8,128)(2,1)S(1)}, u32[]{:S(2)}, u32[]{:S(2)}) collective-permute-start(bf16[256,128]{1,0:T(8,128)(2,1)S(1)} %copy-done.44), channel_id=1, source_target_pairs={{0,4},{4,0},{8,12},{12,8},{16,20},{20,16},{24,28},{28,24},{1,5},{5... | collective-permute-start | bytes 196616 | tf_op jit(solution)/shard_map/ppermute | solution.py:406
  37.1 9.5 %collective-permute-start.1 = (bf16[256,128]{1,0:T(8,128)(2,1)S(1)}, bf16[256,128]{1,0:T(8,128)(2,1)S(1)}, u32[]{:S(2)}, u32[]{:S(2)}) collective-permute-start(bf16[256,128]{1,0:T(8,128)(2,1)S(1)} %copy-done.43), channel_id=1, source_target_pairs={{0,8},{4,12},{8,0},{12,4},{16,24},{20,28},{24,16},{28,20},{1,9},{5... | collective-permute-start | bytes 196616 | tf_op jit(solution)/shard_map/ppermute | solution.py:406
  38.5 12.7 %collective-permute-start.2 = (bf16[256,128]{1,0:T(8,128)(2,1)S(1)}, bf16[256,128]{1,0:T(8,128)(2,1)S(1)}, u32[]{:S(2)}, u32[]{:S(2)}) collective-permute-start(bf16[256,128]{1,0:T(8,128)(2,1)S(1)} %copy-done.42), channel_id=1, source_target_pairs={{0,12},{4,8},{8,4},{12,0},{16,28},{20,24},{24,20},{28,16},{1,13},{... | collective-permute-start | bytes 196616 | tf_op jit(solution)/shard_map/ppermute | solution.py:406
  38.6 19.3 %collective-permute-start.3 = (bf16[256,128]{1,0:T(8,128)(2,1)S(1)}, bf16[256,128]{1,0:T(8,128)(2,1)S(1)}, u32[]{:S(2)}, u32[]{:S(2)}) collective-permute-start(bf16[256,128]{1,0:T(8,128)(2,1)S(1)} %copy-done.41), channel_id=1, source_target_pairs={{0,16},{4,20},{8,24},{12,28},{16,0},{20,4},{24,8},{28,12},{1,17},{... | collective-permute-start | bytes 196616 | tf_op jit(solution)/shard_map/ppermute | solution.py:406
  41.5 18.6 %collective-permute-start.4 = (bf16[256,128]{1,0:T(8,128)(2,1)S(1)}, bf16[256,128]{1,0:T(8,128)(2,1)S(1)}, u32[]{:S(2)}, u32[]{:S(2)}) collective-permute-start(bf16[256,128]{1,0:T(8,128)(2,1)S(1)} %copy-done.40), channel_id=1, source_target_pairs={{0,20},{4,16},{8,28},{12,24},{16,4},{20,0},{24,12},{28,8},{1,21},{... | collective-permute-start | bytes 196616 | tf_op jit(solution)/shard_map/ppermute | solution.py:406
  42.9 17.1 %collective-permute-start.5 = (bf16[256,128]{1,0:T(8,128)(2,1)S(1)}, bf16[256,128]{1,0:T(8,128)(2,1)S(1)}, u32[]{:S(2)}, u32[]{:S(2)}) collective-permute-start(bf16[256,128]{1,0:T(8,128)(2,1)S(1)} %copy-done.39), channel_id=1, source_target_pairs={{0,24},{4,28},{8,16},{12,20},{16,8},{20,12},{24,0},{28,4},{1,25},{... | collective-permute-start | bytes 196616 | tf_op jit(solution)/shard_map/ppermute | solution.py:406
  46.6 13.4 %collective-permute-start.6 = (bf16[256,128]{1,0:T(8,128)(2,1)S(1)}, bf16[256,128]{1,0:T(8,128)(2,1)S(1)}, u32[]{:S(2)}, u32[]{:S(2)}) collective-permute-start(bf16[256,128]{1,0:T(8,128)(2,1)S(1)} %copy-done.38), channel_id=1, source_target_pairs={{0,28},{4,24},{8,20},{12,16},{16,12},{20,8},{24,4},{28,0},{1,29},{... | collective-permute-start | bytes 196616 | tf_op jit(solution)/shard_map/ppermute | solution.py:406
  63.4 7.5 %collective-permute-start.7 = (bf16[256,128]{1,0:T(8,128)(2,1)S(1)}, bf16[256,128]{1,0:T(8,128)(2,1)S(1)}, u32[]{:S(2)}, u32[]{:S(2)}) collective-permute-start(bf16[256,128]{1,0:T(8,128)(2,1)S(1)} %get-tuple-element.72), channel_id=1, source_target_pairs={{0,4},{4,0},{8,12},{12,8},{16,20},{20,16},{24,28},{28,24},{1,5},{5... | collective-permute-start | bytes 196616 | tf_op jit(solution)/shard_map/ppermute | solution.py:406
  64.2 8.2 %collective-permute-start.8 = (bf16[256,128]{1,0:T(8,128)(2,1)S(1)}, bf16[256,128]{1,0:T(8,128)(2,1)S(1)}, u32[]{:S(2)}, u32[]{:S(2)}) collective-permute-start(bf16[256,128]{1,0:T(8,128)(2,1)S(1)} %get-tuple-element.73), channel_id=1, source_target_pairs={{0,8},{4,12},{8,0},{12,4},{16,24},{20,28},{24,16},{28,20},{1,9},{5... | collective-permute-start | bytes 196616 | tf_op jit(solution)/shard_map/ppermute | solution.py:406
  67.1 23.7 %collective-permute-start.9 = (bf16[256,128]{1,0:T(8,128)(2,1)S(1)}, bf16[256,128]{1,0:T(8,128)(2,1)S(1)}, u32[]{:S(2)}, u32[]{:S(2)}) collective-permute-start(bf16[256,128]{1,0:T(8,128)(2,1)S(1)} %get-tuple-element.74), channel_id=1, source_target_pairs={{0,12},{4,8},{8,4},{12,0},{16,28},{20,24},{24,20},{28,16},{1,13},{... | collective-permute-start | bytes 196616 | tf_op jit(solution)/shard_map/ppermute | solution.py:406
  68.0 22.8 %collective-permute-start.10 = (bf16[256,128]{1,0:T(8,128)(2,1)S(1)}, bf16[256,128]{1,0:T(8,128)(2,1)S(1)}, u32[]{:S(2)}, u32[]{:S(2)}) collective-permute-start(bf16[256,128]{1,0:T(8,128)(2,1)S(1)} %get-tuple-element.75), channel_id=1, source_target_pairs={{0,16},{4,20},{8,24},{12,28},{16,0},{20,4},{24,8},{28,12},{1,17},{... | collective-permute-start | bytes 196616 | tf_op jit(solution)/shard_map/ppermute | solution.py:406
  70.0 20.8 %collective-permute-start.11 = (bf16[256,128]{1,0:T(8,128)(2,1)S(1)}, bf16[256,128]{1,0:T(8,128)(2,1)S(1)}, u32[]{:S(2)}, u32[]{:S(2)}) collective-permute-start(bf16[256,128]{1,0:T(8,128)(2,1)S(1)} %get-tuple-element.76), channel_id=1, source_target_pairs={{0,20},{4,16},{8,28},{12,24},{16,4},{20,0},{24,12},{28,8},{1,21},{... | collective-permute-start | bytes 196616 | tf_op jit(solution)/shard_map/ppermute | solution.py:406
  70.9 19.9 %collective-permute-start.12 = (bf16[256,128]{1,0:T(8,128)(2,1)S(1)}, bf16[256,128]{1,0:T(8,128)(2,1)S(1)}, u32[]{:S(2)}, u32[]{:S(2)}) collective-permute-start(bf16[256,128]{1,0:T(8,128)(2,1)S(1)} %get-tuple-element.77), channel_id=1, source_target_pairs={{0,24},{4,28},{8,16},{12,20},{16,8},{20,12},{24,0},{28,4},{1,25},{... | collective-permute-start | bytes 196616 | tf_op jit(solution)/shard_map/ppermute | solution.py:406
  72.4 18.4 %collective-permute-start.13 = (bf16[256,128]{1,0:T(8,128)(2,1)S(1)}, bf16[256,128]{1,0:T(8,128)(2,1)S(1)}, u32[]{:S(2)}, u32[]{:S(2)}) collective-permute-start(bf16[256,128]{1,0:T(8,128)(2,1)S(1)} %get-tuple-element.78), channel_id=1, source_target_pairs={{0,28},{4,24},{8,20},{12,16},{16,12},{20,8},{24,4},{28,0},{1,29},{... | collective-permute-start | bytes 196616 | tf_op jit(solution)/shard_map/ppermute | solution.py:406
  110.0 18.7 %all-to-all-start.2 = ((bf16[8,256,128]{2,1,0:T(8,128)(2,1)}), bf16[8,256,128]{2,1,0:T(8,128)(2,1)S(1)}, u32[]{:S(2)}, u32[]{:S(2)}) async-start(bf16[8,256,128]{2,1,0:T(8,128)(2,1)} %get-tuple-element.110), calls=%async_computation.2 | async-start | bytes 1048576 | tf_op jit(solution)/shard_map/all_to_all | solution.py:402
  122.6 42.6 %copy-start.1 = (bf16[8,256,128]{2,1,0:T(8,128)(2,1)S(1)}, bf16[8,256,128]{2,1,0:T(8,128)(2,1)}, u32[]{:S(2)}) copy-start(bf16[8,256,128]{2,1,0:T(8,128)(2,1)} %copy-done) | copy-start | bytes 1572868
  122.6 42.6 %copy-start.3 = (bf16[2048,256]{1,0:T(8,128)(2,1)S(1)}, bf16[2048,256]{1,0:T(8,128)(2,1)}, u32[]{:S(2)}) copy-start(bf16[2048,256]{1,0:T(8,128)(2,1)} %copy-done.2) | copy-start | bytes 3145732
  122.6 42.6 %copy-start.28 = (f32[8,1,256]{2,1,0:T(1,128)S(1)}, f32[8,1,256]{2,1,0:T(1,128)}, u32[]{:S(2)}) copy-start(f32[8,1,256]{2,1,0:T(1,128)} %reshape.66.seg_ref) | copy-start | bytes 24580
  130.7 63.9 %all-to-all-start.3 = ((bf16[8,256,128]{2,1,0:T(8,128)(2,1)}), bf16[8,256,128]{2,1,0:T(8,128)(2,1)S(1)}, u32[]{:S(2)}, u32[]{:S(2)}) async-start(bf16[8,256,128]{2,1,0:T(8,128)(2,1)} %shard_map.115), calls=%async_computation.3 | async-start | bytes 1048576 | tf_op jit(solution)/shard_map/all_to_all | solution.py:402
  134.4 7.9 %collective-permute-start.14 = (bf16[256,128]{1,0:T(8,128)(2,1)S(1)}, bf16[256,128]{1,0:T(8,128)(2,1)S(1)}, u32[]{:S(2)}, u32[]{:S(2)}) collective-permute-start(bf16[256,128]{1,0:T(8,128)(2,1)S(1)} %get-tuple-element.95), channel_id=1, source_target_pairs={{0,4},{4,0},{8,12},{12,8},{16,20},{20,16},{24,28},{28,24},{1,5},{5... | collective-permute-start | bytes 196616 | tf_op jit(solution)/shard_map/ppermute | solution.py:406
  136.4 9.6 %collective-permute-start.15 = (bf16[256,128]{1,0:T(8,128)(2,1)S(1)}, bf16[256,128]{1,0:T(8,128)(2,1)S(1)}, u32[]{:S(2)}, u32[]{:S(2)}) collective-permute-start(bf16[256,128]{1,0:T(8,128)(2,1)S(1)} %get-tuple-element.96), channel_id=1, source_target_pairs={{0,8},{4,12},{8,0},{12,4},{16,24},{20,28},{24,16},{28,20},{1,9},{5... | collective-permute-start | bytes 196616 | tf_op jit(solution)/shard_map/ppermute | solution.py:406
  137.9 12.4 %collective-permute-start.16 = (bf16[256,128]{1,0:T(8,128)(2,1)S(1)}, bf16[256,128]{1,0:T(8,128)(2,1)S(1)}, u32[]{:S(2)}, u32[]{:S(2)}) collective-permute-start(bf16[256,128]{1,0:T(8,128)(2,1)S(1)} %get-tuple-element.97), channel_id=1, source_target_pairs={{0,12},{4,8},{8,4},{12,0},{16,28},{20,24},{24,20},{28,16},{1,13},{... | collective-permute-start | bytes 196616 | tf_op jit(solution)/shard_map/ppermute | solution.py:406
  137.9 19.4 %collective-permute-start.17 = (bf16[256,128]{1,0:T(8,128)(2,1)S(1)}, bf16[256,128]{1,0:T(8,128)(2,1)S(1)}, u32[]{:S(2)}, u32[]{:S(2)}) collective-permute-start(bf16[256,128]{1,0:T(8,128)(2,1)S(1)} %get-tuple-element.98), channel_id=1, source_target_pairs={{0,16},{4,20},{8,24},{12,28},{16,0},{20,4},{24,8},{28,12},{1,17},{... | collective-permute-start | bytes 196616 | tf_op jit(solution)/shard_map/ppermute | solution.py:406
  140.8 18.6 %collective-permute-start.18 = (bf16[256,128]{1,0:T(8,128)(2,1)S(1)}, bf16[256,128]{1,0:T(8,128)(2,1)S(1)}, u32[]{:S(2)}, u32[]{:S(2)}) collective-permute-start(bf16[256,128]{1,0:T(8,128)(2,1)S(1)} %get-tuple-element.99), channel_id=1, source_target_pairs={{0,20},{4,16},{8,28},{12,24},{16,4},{20,0},{24,12},{28,8},{1,21},{... | collective-permute-start | bytes 196616 | tf_op jit(solution)/shard_map/ppermute | solution.py:406
  142.3 17.2 %collective-permute-start.19 = (bf16[256,128]{1,0:T(8,128)(2,1)S(1)}, bf16[256,128]{1,0:T(8,128)(2,1)S(1)}, u32[]{:S(2)}, u32[]{:S(2)}) collective-permute-start(bf16[256,128]{1,0:T(8,128)(2,1)S(1)} %get-tuple-element.100), channel_id=1, source_target_pairs={{0,24},{4,28},{8,16},{12,20},{16,8},{20,12},{24,0},{28,4},{1,25},{... | collective-permute-start | bytes 196616 | tf_op jit(solution)/shard_map/ppermute | solution.py:406
  146.0 13.4 %collective-permute-start.20 = (bf16[256,128]{1,0:T(8,128)(2,1)S(1)}, bf16[256,128]{1,0:T(8,128)(2,1)S(1)}, u32[]{:S(2)}, u32[]{:S(2)}) collective-permute-start(bf16[256,128]{1,0:T(8,128)(2,1)S(1)} %get-tuple-element.101), channel_id=1, source_target_pairs={{0,28},{4,24},{8,20},{12,16},{16,12},{20,8},{24,4},{28,0},{1,29},{... | collective-permute-start | bytes 196616 | tf_op jit(solution)/shard_map/ppermute | solution.py:406
  162.2 17.0 %collective-permute-start.21 = (bf16[256,128]{1,0:T(8,128)(2,1)S(1)}, bf16[256,128]{1,0:T(8,128)(2,1)S(1)}, u32[]{:S(2)}, u32[]{:S(2)}) collective-permute-start(bf16[256,128]{1,0:T(8,128)(2,1)S(1)} %get-tuple-element.103), channel_id=1, source_target_pairs={{0,4},{4,0},{8,12},{12,8},{16,20},{20,16},{24,28},{28,24},{1,5},{5... | collective-permute-start | bytes 196616 | tf_op jit(solution)/shard_map/ppermute | solution.py:406
  163.0 17.7 %collective-permute-start.22 = (bf16[256,128]{1,0:T(8,128)(2,1)S(1)}, bf16[256,128]{1,0:T(8,128)(2,1)S(1)}, u32[]{:S(2)}, u32[]{:S(2)}) collective-permute-start(bf16[256,128]{1,0:T(8,128)(2,1)S(1)} %get-tuple-element.104), channel_id=1, source_target_pairs={{0,8},{4,12},{8,0},{12,4},{16,24},{20,28},{24,16},{28,20},{1,9},{5... | collective-permute-start | bytes 196616 | tf_op jit(solution)/shard_map/ppermute | solution.py:406
  165.2 18.7 %copy-start.9 = (bf16[2048,256]{1,0:T(8,128)(2,1)S(1)}, bf16[2048,256]{1,0:T(8,128)(2,1)}, u32[]{:S(2)}) copy-start(bf16[2048,256]{1,0:T(8,128)(2,1)} %copy-done.8) | copy-start | bytes 3145732
  165.2 18.7 %copy-start.11 = (bf16[256,128]{1,0:T(8,128)(2,1)S(1)}, bf16[256,128]{1,0:T(8,128)(2,1)}, u32[]{:S(2)}) copy-start(bf16[256,128]{1,0:T(8,128)(2,1)} %copy-done.10) | copy-start | bytes 196612
  165.2 18.7 %copy-start.13 = (bf16[256,128]{1,0:T(8,128)(2,1)S(1)}, bf16[256,128]{1,0:T(8,128)(2,1)}, u32[]{:S(2)}) copy-start(bf16[256,128]{1,0:T(8,128)(2,1)} %copy-done.12) | copy-start | bytes 196612
  165.2 18.7 %copy-start.15 = (bf16[256,128]{1,0:T(8,128)(2,1)S(1)}, bf16[256,128]{1,0:T(8,128)(2,1)}, u32[]{:S(2)}) copy-start(bf16[256,128]{1,0:T(8,128)(2,1)} %copy-done.14) | copy-start | bytes 196612
  165.2 18.7 %copy-start.17 = (bf16[256,128]{1,0:T(8,128)(2,1)S(1)}, bf16[256,128]{1,0:T(8,128)(2,1)}, u32[]{:S(2)}) copy-start(bf16[256,128]{1,0:T(8,128)(2,1)} %copy-done.16) | copy-start | bytes 196612
  165.2 18.7 %copy-start.19 = (bf16[256,128]{1,0:T(8,128)(2,1)S(1)}, bf16[256,128]{1,0:T(8,128)(2,1)}, u32[]{:S(2)}) copy-start(bf16[256,128]{1,0:T(8,128)(2,1)} %copy-done.18) | copy-start | bytes 196612
  165.2 18.7 %copy-start.21 = (bf16[256,128]{1,0:T(8,128)(2,1)S(1)}, bf16[256,128]{1,0:T(8,128)(2,1)}, u32[]{:S(2)}) copy-start(bf16[256,128]{1,0:T(8,128)(2,1)} %copy-done.20) | copy-start | bytes 196612
  165.2 18.7 %copy-start.23 = (bf16[256,128]{1,0:T(8,128)(2,1)S(1)}, bf16[256,128]{1,0:T(8,128)(2,1)}, u32[]{:S(2)}) copy-start(bf16[256,128]{1,0:T(8,128)(2,1)} %copy-done.22) | copy-start | bytes 196612
  165.3 18.7 %copy-start.25 = (bf16[256,128]{1,0:T(8,128)(2,1)S(1)}, bf16[256,128]{1,0:T(8,128)(2,1)}, u32[]{:S(2)}) copy-start(bf16[256,128]{1,0:T(8,128)(2,1)} %copy-done.24) | copy-start | bytes 196612
  175.2 24.1 %collective-permute-start.23 = (bf16[256,128]{1,0:T(8,128)(2,1)S(1)}, bf16[256,128]{1,0:T(8,128)(2,1)S(1)}, u32[]{:S(2)}, u32[]{:S(2)}) collective-permute-start(bf16[256,128]{1,0:T(8,128)(2,1)S(1)} %get-tuple-element.105), channel_id=1, source_target_pairs={{0,12},{4,8},{8,4},{12,0},{16,28},{20,24},{24,20},{28,16},{1,13},{... | collective-permute-start | bytes 196616 | tf_op jit(solution)/shard_map/ppermute | solution.py:406
  176.2 23.2 %collective-permute-start.24 = (bf16[256,128]{1,0:T(8,128)(2,1)S(1)}, bf16[256,128]{1,0:T(8,128)(2,1)S(1)}, u32[]{:S(2)}, u32[]{:S(2)}) collective-permute-start(bf16[256,128]{1,0:T(8,128)(2,1)S(1)} %get-tuple-element.106), channel_id=1, source_target_pairs={{0,16},{4,20},{8,24},{12,28},{16,0},{20,4},{24,8},{28,12},{1,17},{... | collective-permute-start | bytes 196616 | tf_op jit(solution)/shard_map/ppermute | solution.py:406
  178.2 21.2 %collective-permute-start.25 = (bf16[256,128]{1,0:T(8,128)(2,1)S(1)}, bf16[256,128]{1,0:T(8,128)(2,1)S(1)}, u32[]{:S(2)}, u32[]{:S(2)}) collective-permute-start(bf16[256,128]{1,0:T(8,128)(2,1)S(1)} %get-tuple-element.107), channel_id=1, source_target_pairs={{0,20},{4,16},{8,28},{12,24},{16,4},{20,0},{24,12},{28,8},{1,21},{... | collective-permute-start | bytes 196616 | tf_op jit(solution)/shard_map/ppermute | solution.py:406
  179.2 20.2 %collective-permute-start.26 = (bf16[256,128]{1,0:T(8,128)(2,1)S(1)}, bf16[256,128]{1,0:T(8,128)(2,1)S(1)}, u32[]{:S(2)}, u32[]{:S(2)}) collective-permute-start(bf16[256,128]{1,0:T(8,128)(2,1)S(1)} %get-tuple-element.108), channel_id=1, source_target_pairs={{0,24},{4,28},{8,16},{12,20},{16,8},{20,12},{24,0},{28,4},{1,25},{... | collective-permute-start | bytes 196616 | tf_op jit(solution)/shard_map/ppermute | solution.py:406
  180.7 18.8 %collective-permute-start.27 = (bf16[256,128]{1,0:T(8,128)(2,1)S(1)}, bf16[256,128]{1,0:T(8,128)(2,1)S(1)}, u32[]{:S(2)}, u32[]{:S(2)}) collective-permute-start(bf16[256,128]{1,0:T(8,128)(2,1)S(1)} %get-tuple-element.109), channel_id=1, source_target_pairs={{0,28},{4,24},{8,20},{12,16},{16,12},{20,8},{24,4},{28,0},{1,29},{... | collective-permute-start | bytes 196616 | tf_op jit(solution)/shard_map/ppermute | solution.py:406
  (29 other events, 203.6 us)
